TPU v7x, 32 devices: a whole 2x2x4 slice. The times are simulated.
32 devices in a mesh: groups: 2 (over y), servers: 4 (over z), heads: 4 (over x, core).
Axes of the slice: x: 2, y: 2, z: 4, core: 2. Of those that a mesh axis runs over, the one named last changes fastest.
Arguments:
- grad_out: bfloat16 [4096, 2048], P(('groups', 'servers')), parts along dimension 0, may hold values from -6 to 6
- out_weight: bfloat16 [2048, 4096], P(None, 'heads'), may hold values from -0.125 to 0.125
- queries: bfloat16 [4096, 4096], P(('groups', 'servers'), 'heads'), parts along dimension 0, may hold values from -2.5 to 2.5
- attn_out: bfloat16 [4096, 4096], P(('groups', 'servers'), 'heads'), parts along dimension 0, may hold values from -4 to 4
- lse: float32 [32, 4096], P('heads', ('groups', 'servers')), parts along dimension 1, may hold values from 5 to 6.5
- keys: bfloat16 [4096, 512], P(('groups', 'servers'), 'heads'), parts along dimension 0, may hold values from -2.5 to 2.5
- values: bfloat16 [4096, 512], P(('groups', 'servers'), 'heads'), parts along dimension 0, may hold values from -4 to 4
- prefix_keys: bfloat16 [256, 512], P(('groups', 'servers'), 'heads'), parts along dimension 0, may hold values from -2.5 to 2.5
- prefix_values: bfloat16 [256, 512], P(('groups', 'servers'), 'heads'), parts along dimension 0, may hold values from -4 to 4
- fork_owner: int32 [128, 1], P('groups'), parts along dimension 0, may hold values from 0 to 3; in each aligned block of 16 rows (0 to 15, 16 to 31, ...) at most 8 rows name the same one
- fork_root: int32 [128], P('groups'), parts along dimension 0, may hold values from 0 to 3
- fork_offset: int32 [128], P('groups'), parts along dimension 0, may hold values from 1 to 64
Outputs:
- grad_queries: bfloat16 [4096, 4096], P(('groups', 'servers'), 'heads'), parts along dimension 0
- grad_keys: bfloat16 [4096, 512], P(('groups', 'servers'), 'heads'), parts along dimension 0
- grad_values: bfloat16 [4096, 512], P(('groups', 'servers'), 'heads'), parts along dimension 0
- prefix_grad_keys: bfloat16 [256, 512], P(('groups', 'servers'), 'heads'), parts along dimension 0
- prefix_grad_values: bfloat16 [256, 512], P(('groups', 'servers'), 'heads'), parts along dimension 0
There are 2 independent parts, one for each index of `groups`. A program takes and returns all parts, laid end to end along the dimension named above; an argument that names none is the same for every part. Nothing has to cross between parts.
Inputs may be any that keep to these rules, and one draw needn't show every extreme that they name: `fork_owner`: row g names the owner of the rollout that continuation g forks from. Among the continuations of one owner (aligned blocks of 16 rows) no owner is named more than 8 times.
All inputs are finite; a program needn't handle non-finite values.
Results may differ from a plain program's by a relative error of at most 0.0061.
Values may be sent and summed in bfloat16 or wider, within the bound.
No kernel may reach another device: no remote copies, remote signals or barrier semaphores. Data moves between devices by JAX's collectives and lax.ppermute only.
A program may use at most 128 MiB of HBM per device.

v0:
```python
import math

import jax
import jax.numpy as jnp
from jax import lax
from jax.sharding import PartitionSpec as P

HD = 128
CH_DEV = 16
ROOTS_DEV = 4
RLEN = 64
CLEN = 16


def attend(query_heads, out_heads, lse_rows, delta_rows, key_heads, value_heads, mask_rows):
    tok_count, head_local, head_size = query_heads.shape
    key_count, shared_heads, _ = key_heads.shape
    group_size = head_local // shared_heads
    scaling = head_size ** (-0.5)
    block_rows = math.gcd(tok_count, 128)
    block_count = tok_count // block_rows
    contract = (((1,), (1,)), ((), ()))
    across = (((0,), (0,)), ((), ()))
    key_list = [key_heads[:, 0]]
    value_list = [value_heads[:, 0]]

    def block_step(totals, block_index):
        key_totals, value_totals = totals
        start = block_index * block_rows
        query_block = lax.dynamic_slice_in_dim(query_heads, start, block_rows, 0).reshape(
            block_rows, shared_heads, group_size, head_size
        )
        out_block = lax.dynamic_slice_in_dim(out_heads, start, block_rows, 0).reshape(
            block_rows, shared_heads, group_size, head_size
        )
        lse_block = lax.dynamic_slice_in_dim(lse_rows, start, block_rows, 1).reshape(
            shared_heads, group_size, block_rows
        )
        delta_block = lax.dynamic_slice_in_dim(delta_rows, start, block_rows, 1).reshape(
            shared_heads, group_size, block_rows
        )
        allowed = mask_rows(start, block_rows)
        allowed_wide = jnp.broadcast_to(
            allowed[:, None, :], (block_rows, group_size, key_count)
        ).reshape(block_rows * group_size, key_count)
        query_flat = query_block[:, 0].reshape(block_rows * group_size, head_size)
        out_flat = out_block[:, 0].reshape(block_rows * group_size, head_size)
        lse_flat = jnp.transpose(lse_block[0]).reshape(-1)
        delta_flat = jnp.transpose(delta_block[0]).reshape(-1)
        scores = (
            lax.dot_general(query_flat, key_list[0], contract, preferred_element_type=jnp.float32)
            * scaling
        )
        weights = jnp.where(allowed_wide, jnp.exp(scores - lse_flat[:, None]), jnp.float32(0.0))
        weights_low = weights.astype(jnp.bfloat16)
        weight_grads = lax.dot_general(
            out_flat, value_list[0], contract, preferred_element_type=jnp.float32
        )
        score_grads = (weights * (weight_grads - delta_flat[:, None])).astype(jnp.bfloat16)
        grad_query = jnp.dot(score_grads, key_list[0], preferred_element_type=jnp.float32) * scaling
        query_parts = [grad_query.reshape(block_rows, group_size, head_size)]
        new_keys = [
            lax.dot_general(score_grads, query_flat, across, preferred_element_type=jnp.float32)
            * scaling
        ]
        new_values = [
            lax.dot_general(weights_low, out_flat, across, preferred_element_type=jnp.float32)
        ]
        key_totals = key_totals + jnp.stack(new_keys, axis=1)
        value_totals = value_totals + jnp.stack(new_values, axis=1)
        grad_block = jnp.stack(query_parts, axis=1).reshape(block_rows, head_local, head_size)
        return ((key_totals, value_totals), grad_block)

    empty_grads = jnp.zeros(key_heads.shape, jnp.float32)
    totals, query_grads = lax.scan(
        block_step, (empty_grads, empty_grads), jnp.arange(block_count, dtype=jnp.int32)
    )
    return (query_grads.reshape(tok_count, head_local, head_size), totals[0], totals[1])


def local(
    grad_out,
    out_weight,
    queries,
    attn_out,
    lse,
    keys,
    values,
    prefix_keys,
    prefix_values,
    fork_owner,
    fork_root,
    fork_offset,
):
    tok_rows = queries.shape[0]
    head_local = lse.shape[0]
    shared_heads = keys.shape[1] // HD
    shared_width = keys.shape[1]
    servers_count = lax.axis_size("servers")
    my_index = lax.axis_index("servers")
    root_rows = ROOTS_DEV * RLEN
    out_grad = jnp.dot(grad_out, out_weight, preferred_element_type=jnp.float32).astype(
        jnp.bfloat16
    )
    out_heads = out_grad.reshape(tok_rows, head_local, HD)
    query_heads = queries.reshape(tok_rows, head_local, HD)
    output_heads = attn_out.reshape(tok_rows, head_local, HD)
    delta_rows = jnp.transpose(
        jnp.sum(out_heads.astype(jnp.float32) * output_heads.astype(jnp.float32), axis=2)
    )
    key_heads = keys.reshape(tok_rows, shared_heads, HD)
    value_heads = values.reshape(tok_rows, shared_heads, HD)
    gathered = (
        lax.all_gather(prefix_keys, "servers", axis=0, tiled=True),
        lax.all_gather(prefix_values, "servers", axis=0, tiled=True),
    )
    prompt_keys = gathered[0].reshape(-1, shared_heads, HD)
    prompt_values = gathered[1].reshape(-1, shared_heads, HD)
    prompt_count = prompt_keys.shape[0]

    def open_rows(start, rows):
        return jnp.ones((rows, prompt_count), dtype=jnp.bool_)

    pre_query_grad, pre_key_grad, pre_value_grad = attend(
        query_heads, out_heads, lse, delta_rows, prompt_keys, prompt_values, open_rows
    )
    prompt_sums = (
        lax.psum_scatter(
            pre_key_grad.reshape(-1, shared_width), "servers", scatter_dimension=0, tiled=True
        ),
        lax.psum_scatter(
            pre_value_grad.reshape(-1, shared_width), "servers", scatter_dimension=0, tiled=True
        ),
    )
    local_index = jnp.arange(tok_rows, dtype=jnp.int32)
    child_part = local_index - root_rows
    in_root = local_index < root_rows
    segment_ids = jnp.where(in_root, local_index // RLEN, ROOTS_DEV + child_part // CLEN)
    segment_pos = jnp.where(in_root, local_index % RLEN, child_part % CLEN)

    def own_rows(start, rows):
        query_seg = lax.dynamic_slice_in_dim(segment_ids, start, rows, 0)
        query_pos = lax.dynamic_slice_in_dim(segment_pos, start, rows, 0)
        return (query_seg[:, None] == segment_ids[None, :]) & (
            segment_pos[None, :] <= query_pos[:, None]
        )

    local_query_grad, local_key_grad, local_value_grad = attend(
        query_heads, out_heads, lse, delta_rows, key_heads, value_heads, own_rows
    )
    child_query = query_heads[root_rows:]
    child_out = out_heads[root_rows:]
    child_lse = lse[:, root_rows:]
    child_delta = delta_rows[:, root_rows:]
    owners_all = fork_owner[:, 0].reshape(servers_count, CH_DEV)
    roots_all = fork_root.reshape(servers_count, CH_DEV)
    my_owners = lax.dynamic_index_in_dim(owners_all, my_index, 0, keepdims=False)
    my_roots = lax.dynamic_index_in_dim(roots_all, my_index, 0, keepdims=False)
    my_offsets = lax.dynamic_slice_in_dim(fork_offset, my_index * CH_DEV, CH_DEV, 0)
    positions = jnp.arange(RLEN, dtype=jnp.int32)
    parent_key_index = jnp.arange(CH_DEV * RLEN, dtype=jnp.int32)
    parent_slot = parent_key_index // RLEN
    parent_pos = parent_key_index % RLEN

    def parent_rows(start, rows):
        child_ids = (start + jnp.arange(rows, dtype=jnp.int32)) // CLEN
        child_limit = jnp.take(my_offsets, child_ids, axis=0)
        return (child_ids[:, None] == parent_slot[None, :]) & (
            parent_pos[None, :] < child_limit[:, None]
        )

    root_keys = keys[:root_rows]
    root_values = values[:root_rows]
    all_roots = (
        lax.all_gather(root_keys, "servers", axis=0, tiled=True),
        lax.all_gather(root_values, "servers", axis=0, tiled=True),
    )
    parent_index = ((my_owners * ROOTS_DEV + my_roots) * RLEN)[:, None] + positions[None, :]
    flat_index = parent_index.reshape(-1)
    parent_keys = jnp.take(all_roots[0], flat_index, axis=0).reshape(
        CH_DEV * RLEN, shared_heads, HD
    )
    parent_values = jnp.take(all_roots[1], flat_index, axis=0).reshape(
        CH_DEV * RLEN, shared_heads, HD
    )
    parent_query_grad, parent_key_grad, parent_value_grad = attend(
        child_query, child_out, child_lse, child_delta, parent_keys, parent_values, parent_rows
    )
    dense_keys = (
        jnp.zeros((all_roots[0].shape[0], shared_width), jnp.float32)
        .at[flat_index]
        .add(parent_key_grad.reshape(-1, shared_width))
    )
    dense_values = (
        jnp.zeros((all_roots[1].shape[0], shared_width), jnp.float32)
        .at[flat_index]
        .add(parent_value_grad.reshape(-1, shared_width))
    )
    root_sums = (
        lax.psum_scatter(dense_keys, "servers", scatter_dimension=0, tiled=True),
        lax.psum_scatter(dense_values, "servers", scatter_dimension=0, tiled=True),
    )
    root_key_part = root_sums[0]
    root_value_part = root_sums[1]
    own_query_grad = pre_query_grad + local_query_grad
    grad_query = jnp.concatenate(
        [own_query_grad[:root_rows], own_query_grad[root_rows:] + parent_query_grad], axis=0
    )
    grad_queries = grad_query.astype(jnp.bfloat16).reshape(tok_rows, head_local * HD)
    local_keys = local_key_grad.reshape(tok_rows, shared_width)
    local_values = local_value_grad.reshape(tok_rows, shared_width)
    grad_keys = jnp.concatenate(
        [local_keys[:root_rows] + root_key_part, local_keys[root_rows:]], axis=0
    ).astype(jnp.bfloat16)
    grad_values = jnp.concatenate(
        [local_values[:root_rows] + root_value_part, local_values[root_rows:]], axis=0
    ).astype(jnp.bfloat16)
    prefix_grad_keys = prompt_sums[0].astype(jnp.bfloat16)
    prefix_grad_values = prompt_sums[1].astype(jnp.bfloat16)
    return (grad_queries, grad_keys, grad_values, prefix_grad_keys, prefix_grad_values)


def solution(mesh):
    placed = (
        P(("groups", "servers"), None),
        P(None, "heads"),
        P(("groups", "servers"), "heads"),
        P(("groups", "servers"), "heads"),
        P("heads", ("groups", "servers")),
        P(("groups", "servers"), "heads"),
        P(("groups", "servers"), "heads"),
        P(("groups", "servers"), "heads"),
        P(("groups", "servers"), "heads"),
        P("groups", None),
        P("groups"),
        P("groups"),
    )
    return jax.shard_map(
        local,
        mesh=mesh,
        in_specs=placed,
        out_specs=(
            P(("groups", "servers"), "heads"),
            P(("groups", "servers"), "heads"),
            P(("groups", "servers"), "heads"),
            P(("groups", "servers"), "heads"),
            P(("groups", "servers"), "heads"),
        ),
        check_vma=False,
    )
```

profile of v0, /device:TPU:0, one launch (start us, length us, event | category | flops | bytes accessed | tf_op | source)
XLA Modules:
  0.0 282.1 jit_solution(4056299993716482109)
XLA Ops:
  8.8 4.5 %convolution_convert_fusion = bf16[512,1024]{1,0:T(8,128)(2,1)S(1)} fusion(bf16[512,2048]{1,0:T(8,128)(2,1)S(1)} %copy-done, bf16[2048,1024]{1,0:T(8,128)(2,1)} %param.21), kind=kOutput, calls=%fused_computation.132 | convolution fusion | flops 2148007936 | bytes 7340032 | tf_op jit(solution)/shard_map/dot_general | solution.py:102
  17.8 2.5 copy.20
  20.3 14.8 %all_gather.12 = bf16[128,128]{1,0:T(8,128)(2,1)S(1)} all-gather(bf16[32,128]{1,0:T(8,128)(2,1)S(1)} %copy-done.16), channel_id=1, replica_groups=mesh['groups'=2,'servers'=4,'heads'=4] {'servers'}, dimensions={0}, use_global_device_ids=true | all-gather | bytes 40960 | tf_op jit(solution)/shard_map/all_gather | solution.py:114
  35.1 13.1 %all_gather.13 = bf16[128,128]{1,0:T(8,128)(2,1)S(1)} all-gather(bf16[32,128]{1,0:T(8,128)(2,1)S(1)} %copy-done.17), channel_id=1, replica_groups=mesh['groups'=2,'servers'=4,'heads'=4] {'servers'}, dimensions={0}, use_global_device_ids=true | all-gather | bytes 40960 | tf_op jit(solution)/shard_map/all_gather | solution.py:115
  48.2 2.5 multiply_reduce_fusion
  52.2 34.4 %while.48 = (s32[]{:T(128)}, f32[128,1,128]{2,0,1:T(8,128)}, f32[128,1,128]{2,0,1:T(8,128)}, f32[4,128,8,128]{3,2,1,0:T(8,128)}, s32[4]{0:T(128)S(1)}, /*index=5...) while((s32[]{:T(128)}, f32[128,1,128]{2,0,1:T(8,128)}, ...), condition=%wide.region_2.3_spmd.clone, body=%wide.region_1.2_spmd.clone.sunk | while | flops 168771584 | bytes 4334310 | solution.py:75
  58.9 1.9 fusion.184
  67.5 1.9 fusion.184
  76.1 1.9 fusion.184
  90.3 1.9 slice_bitcast_fusion
  92.2 1.9 slice_bitcast_fusion.1
  94.1 14.2 %all_gather.14 = bf16[1024,128]{1,0:T(8,128)(2,1)S(1)} all-gather(bf16[256,128]{1,0:T(8,128)(2,1)S(1)} %slice-done.1), channel_id=1, replica_groups=mesh['groups'=2,'servers'=4,'heads'=4] {'servers'}, dimensions={0}, use_global_device_ids=true | all-gather | bytes 327680 | tf_op jit(solution)/shard_map/all_gather | solution.py:175
  108.3 14.1 %all_gather.15 = bf16[1024,128]{1,0:T(8,128)(2,1)S(1)} all-gather(bf16[256,128]{1,0:T(8,128)(2,1)S(1)} %slice-done), channel_id=1, replica_groups=mesh['groups'=2,'servers'=4,'heads'=4] {'servers'}, dimensions={0}, use_global_device_ids=true | all-gather | bytes 327680 | tf_op jit(solution)/shard_map/all_gather | solution.py:176
  122.3 4.3 %gather_fusion = bf16[1024,128]{1,0:T(8,128)(2,1)} fusion(bf16[1024,128]{1,0:T(8,128)(2,1)S(1)} %all_gather.14, s32[1024]{0:T(1024)S(1)} %fusion.100), kind=kCustom, calls=%fused_computation.clone | custom fusion | bytes 528384 | tf_op jit(solution)/shard_map/jit(_take)/gather | solution.py:180
  126.6 4.3 %gather_fusion.1 = bf16[1024,128]{1,0:T(8,128)(2,1)} fusion(bf16[1024,128]{1,0:T(8,128)(2,1)S(1)} %all_gather.15, s32[1024]{0:T(1024)S(1)} %fusion.100), kind=kCustom, calls=%fused_computation.1.clone | custom fusion | bytes 528384 | tf_op jit(solution)/shard_map/jit(_take)/gather | solution.py:183
  131.0 1.9 copy.25
  134.1 1.9 broadcast_select_fusion
  136.1 56.4 %while.49 = (s32[]{:T(128)}, f32[1024,1,128]{2,0,1:T(8,128)S(1)}, f32[1024,1,128]{2,0,1:T(8,128)}, f32[2,128,8,128]{3,2,1,0:T(8,128)}, s32[2]{0:T(128)S(1)}, /*i...) while((s32[]{:T(128)}, f32[1024,1,128]{2,0,1:T(8,128)S(1)}, ...), condition=%wide.region_6.8_spmd.clone, body=%wide.region_5.7_spmd.clone.sunk | while | flops 1353864192 | bytes 51641432 | solution.py:75
  138.0 10.0 %and_select_fusion.4 = (s32[128]{0:T(128)S(1)}, s32[128]{0:T(128)S(1)}) fusion(s32[]{:T(128)} %bitcast.344, s32[]{:T(128)} %bitcast.345, s32[]{:T(128)} %bitcast.346, s32[]{:T(128)} %bitcast.347, s32[]{:T(128)} %bitcast.348, s32[]{:T(128)} %bitcast.349, s32[]{:T(128)} %bitcast.350, s32[]{:T(128)} %bitcast.351, s32[]{:T(128)} %bitcast.352, ...), kind=kLoop, calls=%fused_computation.89.clone.1 | loop fusion | flops 9216 | bytes 1092 | tf_op jit(solution)/shard_map/while/body/eval_jaxpr/jit(_take)/select_n | solution.py:167
  148.9 2.6 fusion.196
  151.8 3.9 %multiply_convert_fusion.4 = bf16[1024,1024]{1,0:T(8,128)(2,1)S(1)} fusion(f32[1024,1024]{1,0:T(8,128)} %fusion.196, bf16[1024,128]{1,0:T(8,128)(2,1)} %get-tuple-element.918, f32[1024]{0:T(1024)S(1)} %sub.266, f32[1024]{0:T(1024)S(1)} %sub.267, pred[128,1024]{1,0:T(8,128)(4,1)} %compare_and_fusion.5, bf16[256,8,128]{2,1,0:T(8,128)(2,1)} %get-tuple-element.917, ...), kind=kOutput, calls=%fused_computation.35.clone.1 | convolution fusion | flops 274726912 | bytes 6955012 | tf_op jit(solution)/shard_map/while/body/eval_jaxpr/dot_general | solution.py:56
  158.5 2.6 fusion.199
  161.5 2.3 fusion.200
  165.7 10.0 %and_select_fusion.4 = (s32[128]{0:T(128)S(1)}, s32[128]{0:T(128)S(1)}) fusion(s32[]{:T(128)} %bitcast.344, s32[]{:T(128)} %bitcast.345, s32[]{:T(128)} %bitcast.346, s32[]{:T(128)} %bitcast.347, s32[]{:T(128)} %bitcast.348, s32[]{:T(128)} %bitcast.349, s32[]{:T(128)} %bitcast.350, s32[]{:T(128)} %bitcast.351, s32[]{:T(128)} %bitcast.352, ...), kind=kLoop, calls=%fused_computation.89.clone.1 | loop fusion | flops 9216 | bytes 1092 | tf_op jit(solution)/shard_map/while/body/eval_jaxpr/jit(_take)/select_n | solution.py:167
  176.6 2.7 fusion.196
  179.5 3.9 %multiply_convert_fusion.4 = bf16[1024,1024]{1,0:T(8,128)(2,1)S(1)} fusion(f32[1024,1024]{1,0:T(8,128)} %fusion.196, bf16[1024,128]{1,0:T(8,128)(2,1)} %get-tuple-element.918, f32[1024]{0:T(1024)S(1)} %sub.266, f32[1024]{0:T(1024)S(1)} %sub.267, pred[128,1024]{1,0:T(8,128)(4,1)} %compare_and_fusion.5, bf16[256,8,128]{2,1,0:T(8,128)(2,1)} %get-tuple-element.917, ...), kind=kOutput, calls=%fused_computation.35.clone.1 | convolution fusion | flops 274726912 | bytes 6955012 | tf_op jit(solution)/shard_map/while/body/eval_jaxpr/dot_general | solution.py:56
  186.2 2.6 fusion.199
  189.2 3.3 %fusion.200 = f32[1024,1,128]{2,0,1:T(8,128)} fusion(f32[1024,1024]{1,0:T(8,128)S(1)} %copy-done.2, f32[1024]{0:T(1024)S(1)} %sub.267, pred[128,1024]{1,0:T(8,128)(4,1)S(1)} %copy-done.9, f32[1024,1,128]{2,0,1:T(8,128)} %get-tuple-element.894, pred[]{:T(512)S(6)} %compare.245, bf16[256,8,128]{2,1,0:T(8,128)(2,1)S(1)} %copy-done.14, s32[]{:T(128)S(6)} %select_n.283), kind=kOutput, calls=%fused_computation.46.clone.1 | convolution fusion | flops 272891904 | bytes 5640197 | tf_op jit(solution)/shard_map/while/body/eval_jaxpr/dot_general | solution.py:67
  192.5 6.7 %scatter_custom_fusion.1 = f32[1024,128]{1,0:T(8,128)} fusion(s32[1024]{0:T(1024)S(1)} %bitcast.386, f32[1024,1,128]{2,0,1:T(8,128)} %get-tuple-element.322, f32[]{:T(128)} %constant.217.clone.1), kind=kCustom, calls=%fused_computation.140 | custom fusion | flops 131072 | bytes 1048580 | tf_op jit(solution)/shard_map/scatter-add | solution.py:197
  199.3 6.8 %scatter_custom_fusion = f32[1024,128]{1,0:T(8,128)} fusion(s32[1024]{0:T(1024)S(1)} %bitcast.387, f32[1024,1,128]{2,0,1:T(8,128)S(1)} %get-tuple-element.320, f32[]{:T(128)} %constant.217.clone.1), kind=kCustom, calls=%fused_computation.142 | custom fusion | flops 131072 | bytes 1048580 | tf_op jit(solution)/shard_map/scatter-add | solution.py:192
  207.6 56.9 %while.50 = (s32[]{:T(128)}, f32[512,1,128]{2,0,1:T(8,128)S(1)}, f32[512,1,128]{2,0,1:T(8,128)}, f32[4,128,8,128]{3,2,1,0:T(8,128)}, s32[4]{0:T(128)S(1)}, /*ind...) while((s32[]{:T(128)}, f32[512,1,128]{2,0,1:T(8,128)S(1)}, ...), condition=%wide.region_4.5_spmd.clone.clone, body=%wide.region_3.4_spmd.clone.clone.sunk | while | flops 675414016 | bytes 13156130 | solution.py:75
  210.1 3.0 %exponential_select_fusion.3 = f32[1024,512]{1,0:T(8,128)} fusion(bf16[512,128]{1,0:T(8,128)(2,1)S(1)} %get-tuple-element.1011, f32[1024]{0:T(1024)S(1)} %sub.272, pred[128,512]{1,0:T(8,128)(4,1)S(1)} %compare_and_fusion.6, bf16[512,8,128]{2,1,0:T(8,128)(2,1)} %get-tuple-element.1010, s32[]{:T(128)S(6)} %select_n.285), kind=kOutput, calls=%fused_computation.105.clone.1 | convolution fusion | flops 135790592 | bytes 2560004 | tf_op jit(solution)/shard_map/while/body/eval_jaxpr/dot_general | solution.py:51
  213.2 2.2 multiply_convert_fusion.5
  215.4 2.1 fusion.214
  219.0 2.8 fusion.213
  224.3 3.0 %exponential_select_fusion.3 = f32[1024,512]{1,0:T(8,128)} fusion(bf16[512,128]{1,0:T(8,128)(2,1)S(1)} %get-tuple-element.1011, f32[1024]{0:T(1024)S(1)} %sub.272, pred[128,512]{1,0:T(8,128)(4,1)S(1)} %compare_and_fusion.6, bf16[512,8,128]{2,1,0:T(8,128)(2,1)} %get-tuple-element.1010, s32[]{:T(128)S(6)} %select_n.285), kind=kOutput, calls=%fused_computation.105.clone.1 | convolution fusion | flops 135790592 | bytes 2560004 | tf_op jit(solution)/shard_map/while/body/eval_jaxpr/dot_general | solution.py:51
  227.4 2.1 multiply_convert_fusion.5
  229.5 2.1 fusion.214
  233.2 2.9 %fusion.213 = f32[512,1,128]{2,0,1:T(8,128)} fusion(f32[1024,512]{1,0:T(8,128)} %exponential_select_fusion.3, f32[512,1,128]{2,0,1:T(8,128)} %get-tuple-element.988, bf16[512,8,128]{2,1,0:T(8,128)(2,1)} %get-tuple-element.1013, s32[]{:T(128)S(6)} %select_n.285, pred[]{:T(512)S(6)} %compare.246), kind=kOutput, calls=%fused_computation.112.clone.1 | convolution fusion | flops 134873088 | bytes 2883589 | tf_op jit(solution)/shard_map/while/body/eval_jaxpr/dot_general | solution.py:67
  238.6 3.0 %exponential_select_fusion.3 = f32[1024,512]{1,0:T(8,128)} fusion(bf16[512,128]{1,0:T(8,128)(2,1)S(1)} %get-tuple-element.1011, f32[1024]{0:T(1024)S(1)} %sub.272, pred[128,512]{1,0:T(8,128)(4,1)S(1)} %compare_and_fusion.6, bf16[512,8,128]{2,1,0:T(8,128)(2,1)} %get-tuple-element.1010, s32[]{:T(128)S(6)} %select_n.285), kind=kOutput, calls=%fused_computation.105.clone.1 | convolution fusion | flops 135790592 | bytes 2560004 | tf_op jit(solution)/shard_map/while/body/eval_jaxpr/dot_general | solution.py:51
  241.6 2.2 multiply_convert_fusion.5
  243.8 2.1 fusion.214
  247.4 2.9 %fusion.213 = f32[512,1,128]{2,0,1:T(8,128)} fusion(f32[1024,512]{1,0:T(8,128)} %exponential_select_fusion.3, f32[512,1,128]{2,0,1:T(8,128)} %get-tuple-element.988, bf16[512,8,128]{2,1,0:T(8,128)(2,1)} %get-tuple-element.1013, s32[]{:T(128)S(6)} %select_n.285, pred[]{:T(512)S(6)} %compare.246), kind=kOutput, calls=%fused_computation.112.clone.1 | convolution fusion | flops 134873088 | bytes 2883589 | tf_op jit(solution)/shard_map/while/body/eval_jaxpr/dot_general | solution.py:67
  252.8 3.0 %exponential_select_fusion.3 = f32[1024,512]{1,0:T(8,128)} fusion(bf16[512,128]{1,0:T(8,128)(2,1)S(1)} %get-tuple-element.1011, f32[1024]{0:T(1024)S(1)} %sub.272, pred[128,512]{1,0:T(8,128)(4,1)S(1)} %compare_and_fusion.6, bf16[512,8,128]{2,1,0:T(8,128)(2,1)} %get-tuple-element.1010, s32[]{:T(128)S(6)} %select_n.285), kind=kOutput, calls=%fused_computation.105.clone.1 | convolution fusion | flops 135790592 | bytes 2560004 | tf_op jit(solution)/shard_map/while/body/eval_jaxpr/dot_general | solution.py:51
  255.9 2.1 multiply_convert_fusion.5
  258.0 2.1 fusion.214
  261.7 2.9 %fusion.213 = f32[512,1,128]{2,0,1:T(8,128)} fusion(f32[1024,512]{1,0:T(8,128)} %exponential_select_fusion.3, f32[512,1,128]{2,0,1:T(8,128)} %get-tuple-element.988, bf16[512,8,128]{2,1,0:T(8,128)(2,1)} %get-tuple-element.1013, s32[]{:T(128)S(6)} %select_n.285, pred[]{:T(512)S(6)} %compare.246), kind=kOutput, calls=%fused_computation.112.clone.1 | convolution fusion | flops 134873088 | bytes 2883589 | tf_op jit(solution)/shard_map/while/body/eval_jaxpr/dot_general | solution.py:67
  264.5 2.4 add.263
  (202 shorter events, 73.4 us)
Async XLA Ops:
  7.2 1.6 copy-start
  7.2 262.5 %reduce-scatter.9.cloned.1.call-start = ((), (), s32[]{:S(2)}) async-start(), calls=%async_computation.6 | async-start | bytes 81920 | tf_op jit(solution)/shard_map/reduce_scatter | solution.py:128
  13.3 1.0 copy-start.10
  13.3 2.3 copy-start.13
  15.8 1.8 copy-start.15
  17.7 2.6 copy-start.16
  17.7 17.4 %copy-start.17 = (bf16[32,128]{1,0:T(8,128)(2,1)S(1)}, bf16[32,128]{1,0:T(8,128)(2,1)}, u32[]{:S(2)}) copy-start(bf16[32,128]{1,0:T(8,128)(2,1)} %param.28) | copy-start | bytes 24580
  52.2 35.8 %copy-start.19 = (s32[64,1]{0,1:T(1,128)S(1)}, s32[64,1]{0,1:T(1,128)}, u32[]{:S(2)}) copy-start(s32[64,1]{0,1:T(1,128)} %param.29) | copy-start | bytes 772
  52.2 36.5 %copy-start.18 = (s32[64]{0:T(128)S(1)}, s32[64]{0:T(128)}, u32[]{:S(2)}) copy-start(s32[64]{0:T(128)} %param.30) | copy-start | bytes 772
  86.6 21.7 %copy-start.4 = (f32[8,512]{0,1:T(8,128)}, f32[8,512]{0,1:T(8,128)S(1)}, u32[]{:S(2)}) copy-start(f32[8,512]{0,1:T(8,128)S(1)} %get-tuple-element.1025) | copy-start | bytes 49156
  86.6 40.0 %copy-start.5 = (f32[8,512]{0,1:T(8,128)}, f32[8,512]{0,1:T(8,128)S(1)}, u32[]{:S(2)}) copy-start(f32[8,512]{0,1:T(8,128)S(1)} %get-tuple-element.1026) | copy-start | bytes 49156
  86.6 7.5 %slice-start.1 = ((bf16[512,128]{1,0:T(8,128)(2,1)}), bf16[256,128]{1,0:T(8,128)(2,1)S(1)}, s32[]{:S(2)}) async-start(bf16[512,128]{1,0:T(8,128)(2,1)} %param.25), calls=%async_computation.9 | async-start | bytes 131072 | tf_op jit(solution)/shard_map/slice | solution.py:172
  86.6 21.7 %slice-start = ((bf16[512,128]{1,0:T(8,128)(2,1)}), bf16[256,128]{1,0:T(8,128)(2,1)S(1)}, s32[]{:S(2)}) async-start(bf16[512,128]{1,0:T(8,128)(2,1)} %param.26), calls=%async_computation.8 | async-start | bytes 131072 | tf_op jit(solution)/shard_map/slice | solution.py:173
  86.6 184.4 %reduce-scatter.11.cloned.1.call-start = ((), (), s32[]{:S(2)}) async-start(), calls=%async_computation.7 | async-start | bytes 81920 | tf_op jit(solution)/shard_map/reduce_scatter | solution.py:131
  87.4 185.0 %reduce-scatter.7.cloned.1.call-start = ((), (), s32[]{:S(2)}) async-start(), calls=%async_computation.5 | async-start | bytes 655360 | tf_op jit(solution)/shard_map/reduce_scatter | solution.py:201
  126.6 7.4 %copy-start.20 = (s32[64]{0:T(128)S(1)}, s32[64]{0:T(128)}, u32[]{:S(2)}) copy-start(s32[64]{0:T(128)} %param.31) | copy-start | bytes 772
  148.9 2.7 copy-start.11
  148.9 2.7 copy-start.12
  155.6 1.4 copy-start.1
  158.5 2.8 copy-start.2
  158.5 2.8 copy-start.9
  158.5 3.0 %copy-start.14 = (bf16[256,8,128]{2,1,0:T(8,128)(2,1)S(1)}, bf16[256,8,128]{2,1,0:T(8,128)(2,1)}, u32[]{:S(2)}) copy-start(bf16[256,8,128]{2,1,0:T(8,128)(2,1)} %get-tuple-element.917) | copy-start | bytes 1572868 | tf_op jit(solution)/shard_map/while
  176.6 2.7 copy-start.11
  176.6 2.7 copy-start.12
  183.3 1.4 copy-start.1
  186.2 2.8 copy-start.2
  186.2 2.8 copy-start.9
  186.2 3.0 %copy-start.14 = (bf16[256,8,128]{2,1,0:T(8,128)(2,1)S(1)}, bf16[256,8,128]{2,1,0:T(8,128)(2,1)}, u32[]{:S(2)}) copy-start(bf16[256,8,128]{2,1,0:T(8,128)(2,1)} %get-tuple-element.917) | copy-start | bytes 1572868 | tf_op jit(solution)/shard_map/while
  199.2 8.4 %copy-start.6 = (bf16[512,128]{1,0:T(8,128)(2,1)S(1)}, bf16[512,128]{1,0:T(8,128)(2,1)}, u32[]{:S(2)}) copy-start(bf16[512,128]{1,0:T(8,128)(2,1)} %param.26) | copy-start | bytes 393220
  199.2 8.4 %copy-start.7 = (bf16[512,128]{1,0:T(8,128)(2,1)S(1)}, bf16[512,128]{1,0:T(8,128)(2,1)}, u32[]{:S(2)}) copy-start(bf16[512,128]{1,0:T(8,128)(2,1)} %param.25) | copy-start | bytes 393220
  199.2 74.7 %reduce-scatter.5.cloned.1.call-start = ((), (), s32[]{:S(2)}) async-start(), calls=%async_computation.4 | async-start | bytes 655360 | tf_op jit(solution)/shard_map/reduce_scatter | solution.py:200
  219.0 2.8 copy-start.8
  233.2 2.9 %copy-start.8 = (bf16[512,128]{1,0:T(8,128)(2,1)S(1)}, bf16[512,128]{1,0:T(8,128)(2,1)}, u32[]{:S(2)}) copy-start(bf16[512,128]{1,0:T(8,128)(2,1)} %get-tuple-element.1044) | copy-start | bytes 393220 | tf_op jit(solution)/shard_map/while
  247.4 2.9 %copy-start.8 = (bf16[512,128]{1,0:T(8,128)(2,1)S(1)}, bf16[512,128]{1,0:T(8,128)(2,1)}, u32[]{:S(2)}) copy-start(bf16[512,128]{1,0:T(8,128)(2,1)} %get-tuple-element.1044) | copy-start | bytes 393220 | tf_op jit(solution)/shard_map/while
  261.7 2.9 %copy-start.8 = (bf16[512,128]{1,0:T(8,128)(2,1)S(1)}, bf16[512,128]{1,0:T(8,128)(2,1)}, u32[]{:S(2)}) copy-start(bf16[512,128]{1,0:T(8,128)(2,1)} %get-tuple-element.1044) | copy-start | bytes 393220 | tf_op jit(solution)/shard_map/while
  268.4 1.3 copy-start.3
Sparse Core Ops, SparseCore 0:
  86.8 20.0 reduce-scatter.8
  109.2 17.1 reduce-scatter.10
  199.3 23.3 reduce-scatter.6
  224.8 19.8 reduce-scatter.4
where the time goes:
time: 284 us; the launch traced here: 282 us
  matrix products  106 us (37%)
  blocking collectives  56.1 us (20%)
  other arithmetic  51.8 us (18%)
  local copies, waits for them, and re-layouts  45.9 us (16%)
  between operations  14 us (5%)
  loops' own time  6.92 us (2%)
    dot_general x10, matrix products, block_step(): lax.dot_general(weights_low, out_flat, across, preferred_element_type=jnp...  24.4 us
    dot_general x10, matrix products, block_step(): lax.dot_general(query_flat, key_list[0], contract, preferred_element_type...  22.1 us
    dot_general x10, matrix products, block_step(): lax.dot_general(out_flat, value_list[0], contract, preferred_element_type...  21.1 us
    select_n x2, other arithmetic, parent_rows(): child_limit = jnp.take(my_offsets, child_ids, axis=0)  20.1 us
    dot_general x10, matrix products, block_step(): lax.dot_general(score_grads, query_flat, across, preferred_element_type=j...  18.6 us
    unnamed x39, local copies, waits for them, and re-layouts  15.8 us
    dot_general x10, matrix products, block_step(): jnp.dot(score_grads, key_list[0], preferred_element_type=jnp.float32)  15.7 us
    all_gather x1, blocking collectives, local(): lax.all_gather(prefix_keys, 'servers', axis=0, tiled=True)  14.8 us
  transfers between devices with their start and end apart: 4, of which 0 were waited for; matrix products, arithmetic and copies ran while one was open for 53% of the time, Pallas kernels for 0%

commit v1 on v0

v1 whole, which is shorter than its diff:
```python
import jax
import jax.numpy as jnp
from jax import lax
from jax.experimental import pallas as pl
from jax.experimental.pallas import tpu as pltpu
from jax.sharding import PartitionSpec as P

HD = 128
CH_DEV = 16
ROOTS_DEV = 4
RLEN = 64
CLEN = 16
ROOT_ROWS = ROOTS_DEV * RLEN
BLOCK = 64
PER = BLOCK // CLEN
SCALE = HD ** (-0.5)
NT = (((1,), (1,)), ((), ()))
NN = (((1,), (0,)), ((), ()))
TN = (((0,), (0,)), ((), ()))
F32 = jnp.float32
BF16 = jnp.bfloat16
VMEM = pl.BlockSpec(memory_space=pltpu.VMEM)
SMEM = pl.BlockSpec(memory_space=pltpu.SMEM)


def dot(left, right, numbers):
    return lax.dot_general(left, right, numbers, preferred_element_type=F32)


def out_grad_body(grad_ref, weight_ref, attn_ref, out_ref, delta_ref, columns_ref):
    step = pl.program_id(0)
    wide = jnp.dot(grad_ref[...], weight_ref[...], preferred_element_type=F32).astype(BF16)
    out_ref[...] = wide
    products = wide.astype(F32) * attn_ref[...].astype(F32)
    per_step = products.shape[1] // HD
    lane = lax.broadcasted_iota(jnp.int32, columns_ref.shape, 1)

    @pl.when(step == 0)
    def _():
        columns_ref[...] = jnp.zeros(columns_ref.shape, F32)

    columns = columns_ref[...]
    for head in range(per_step):
        total = jnp.sum(products[:, head * HD : (head + 1) * HD], axis=1, keepdims=True)
        columns = jnp.where(lane == step * per_step + head, total, columns)
    columns_ref[...] = columns

    @pl.when(step == pl.num_programs(0) - 1)
    def _():
        delta_ref[...] = jnp.transpose(columns)[: delta_ref.shape[0]]


def out_grad_call(grad_out, out_weight, attn_out):
    rows, model = grad_out.shape
    cols = out_weight.shape[1]
    heads = cols // HD
    width = 2 * HD
    return pl.pallas_call(
        out_grad_body,
        grid=(cols // width,),
        in_specs=[
            pl.BlockSpec((rows, model), lambda i: (0, 0)),
            pl.BlockSpec((model, width), lambda i: (0, i)),
            pl.BlockSpec((rows, width), lambda i: (0, i)),
        ],
        out_specs=[
            pl.BlockSpec((rows, width), lambda i: (0, i)),
            pl.BlockSpec((heads, rows), lambda i: (0, 0)),
        ],
        out_shape=[
            jax.ShapeDtypeStruct((rows, cols), BF16),
            jax.ShapeDtypeStruct((heads, rows), F32),
        ],
        scratch_shapes=[pltpu.VMEM((rows, HD), F32)],
        name="out_grad",
    )(grad_out, out_weight, attn_out)


def stacked(ref, start, heads):
    return jnp.concatenate(
        [ref[start : start + BLOCK, head * HD : (head + 1) * HD] for head in range(heads)], axis=0
    )


def row_of(ref, start, heads):
    return jnp.concatenate([ref[head : head + 1, start : start + BLOCK] for head in range(heads)], axis=1)


def pair_grads(key_part, value_part, query, out, lse, delta, allowed):
    scores = dot(key_part, query, NT) * SCALE
    weights = jnp.exp(scores - lse)
    if allowed is not None:
        weights = jnp.where(allowed, weights, 0.0)
    weight_grads = dot(value_part, out, NT)
    score_grads = (weights * (weight_grads - delta)).astype(BF16)
    value_grad = dot(weights.astype(BF16), out, NN)
    key_grad = dot(score_grads, query, NN) * SCALE
    query_grad = dot(score_grads, key_part, TN)
    return query_grad, key_grad, value_grad


def attend_body(shard_count, part_rows, prompt_rows, extra_prompt, *refs):
    (slot_ref, limit_ref, q_ref, out_ref, lse_ref, delta_ref, key_ref, value_ref) = refs[:8]
    shards = refs[8 : 8 + shard_count]
    refs = refs[8 + shard_count :]
    if extra_prompt:
        extra_ref, refs = refs[0], refs[1:]
    (gq_ref, child_ref, keys_out, values_out, prompt_out, *send_refs) = refs[: 5 + len(refs) - 5 - 3]
    pool_ref, sums_ref, prompt_ref = refs[-3:]
    heads = lse_ref.shape[0]
    tokens = q_ref.shape[0]
    cols = heads * BLOCK
    pool_at = 0
    for shard in shards:
        pool_ref[pool_at : pool_at + shard.shape[0]] = shard[...]
        pool_at += shard.shape[0]
    pool_shards = pool_at // part_rows
    own = prompt_rows
    for index in range(pool_shards):
        at = index * part_rows + 2 * ROOT_ROWS
        prompt_ref[0, index * own : (index + 1) * own] = pool_ref[at : at + own]
        prompt_ref[1, index * own : (index + 1) * own] = pool_ref[at + own : at + 2 * own]
    if extra_prompt:
        prompt_ref[0, pool_shards * own : (pool_shards + 1) * own] = extra_ref[0:own]
        prompt_ref[1, pool_shards * own : (pool_shards + 1) * own] = extra_ref[own : 2 * own]
    sums_ref[...] = jnp.zeros(sums_ref.shape, F32)
    prompt_count = prompt_ref.shape[1]
    chunk = 128
    key_index = lax.broadcasted_iota(jnp.int32, (BLOCK, cols), 0)
    token_index = lax.broadcasted_iota(jnp.int32, (BLOCK, cols), 1) % BLOCK
    root_allowed = key_index <= token_index
    child_allowed = root_allowed & (key_index // CLEN == token_index // CLEN)
    in_child = token_index // CLEN
    prompt_keys = [jnp.zeros((chunk, HD), F32) for _ in range(prompt_count // chunk)]
    prompt_values = [jnp.zeros((chunk, HD), F32) for _ in range(prompt_count // chunk)]
    for block in range(tokens // BLOCK):
        start = block * BLOCK
        query = stacked(q_ref, start, heads)
        out = stacked(out_ref, start, heads)
        lse = row_of(lse_ref, start, heads)
        delta = row_of(delta_ref, start, heads)
        in_root = start < ROOT_ROWS
        total, key_grad, value_grad = pair_grads(
            key_ref[start : start + BLOCK],
            value_ref[start : start + BLOCK],
            query,
            out,
            lse,
            delta,
            root_allowed if in_root else child_allowed,
        )
        keys_out[start : start + BLOCK] = key_grad
        values_out[start : start + BLOCK] = value_grad
        for part in range(prompt_count // chunk):
            query_grad, key_grad, value_grad = pair_grads(
                prompt_ref[0, part * chunk : (part + 1) * chunk],
                prompt_ref[1, part * chunk : (part + 1) * chunk],
                query,
                out,
                lse,
                delta,
                None,
            )
            total = total + query_grad
            prompt_keys[part] = prompt_keys[part] + key_grad
            prompt_values[part] = prompt_values[part] + value_grad
        if not in_root:
            first = (start - ROOT_ROWS) // CLEN
            bases = [pl.multiple_of(slot_ref[first + k], BLOCK) for k in range(PER)]
            key_part = jnp.concatenate([pool_ref[pl.ds(at, RLEN)] for at in bases], axis=0)
            value_part = jnp.concatenate([pool_ref[pl.ds(at + ROOT_ROWS, RLEN)] for at in bases], axis=0)
            allowed = jnp.concatenate(
                [(key_index < limit_ref[first + k]) & (in_child == k) for k in range(PER)], axis=0
            )
            query_grad, key_grad, value_grad = pair_grads(
                key_part, value_part, query, out, lse, delta, allowed
            )
            total = total + query_grad
            for k in range(PER):
                at = bases[k]
                rows = slice(k * RLEN, (k + 1) * RLEN)
                sums_ref[pl.ds(at, RLEN)] = sums_ref[pl.ds(at, RLEN)] + key_grad[rows]
                sums_ref[pl.ds(at + ROOT_ROWS, RLEN)] = (
                    sums_ref[pl.ds(at + ROOT_ROWS, RLEN)] + value_grad[rows]
                )
        total = total * SCALE
        for head in range(heads):
            piece = total[head * BLOCK : (head + 1) * BLOCK]
            if in_root:
                gq_ref[start : start + BLOCK, head * HD : (head + 1) * HD] = piece.astype(BF16)
            else:
                child_ref[start - ROOT_ROWS : start - ROOT_ROWS + BLOCK, head * HD : (head + 1) * HD] = piece
    key_all = jnp.concatenate(prompt_keys, axis=0)
    value_all = jnp.concatenate(prompt_values, axis=0)
    for index in range(pool_shards):
        at = index * part_rows + 2 * ROOT_ROWS
        sums_ref[at : at + own] = key_all[index * own : (index + 1) * own]
        sums_ref[at + own : at + 2 * own] = value_all[index * own : (index + 1) * own]
    if extra_prompt:
        keys_out[0:ROOT_ROWS] = keys_out[0:ROOT_ROWS] + sums_ref[0:ROOT_ROWS]
        values_out[0:ROOT_ROWS] = values_out[0:ROOT_ROWS] + sums_ref[ROOT_ROWS : 2 * ROOT_ROWS]
        prompt_out[...] = sums_ref[2 * ROOT_ROWS : part_rows]
        for index in range(1, pool_shards):
            send_refs[index - 1][...] = sums_ref[index * part_rows : (index + 1) * part_rows].astype(BF16)
        send_refs[-1][0:own] = key_all[pool_shards * own :].astype(BF16)
        send_refs[-1][own : 2 * own] = value_all[pool_shards * own :].astype(BF16)
    else:
        prompt_out[...] = jnp.zeros(prompt_out.shape, F32)
        send_refs[0][...] = sums_ref[...]


def attend_call(slots, limits, queries, out_grad, lse, delta, keys, values, shards, extra, prompt_rows):
    tokens, width = queries.shape
    part_rows = 2 * ROOT_ROWS + 2 * prompt_rows
    pool_rows = sum(shard.shape[0] for shard in shards)
    pool_shards = pool_rows // part_rows
    extra_prompt = extra is not None
    prompt_count = (pool_shards + (1 if extra_prompt else 0)) * prompt_rows
    shapes = [
        jax.ShapeDtypeStruct((tokens, width), BF16),
        jax.ShapeDtypeStruct((tokens - ROOT_ROWS, width), F32),
        jax.ShapeDtypeStruct((tokens, HD), F32),
        jax.ShapeDtypeStruct((tokens, HD), F32),
        jax.ShapeDtypeStruct((2 * prompt_rows, HD), F32),
    ]
    if extra_prompt:
        shapes += [jax.ShapeDtypeStruct((part_rows, HD), BF16)] * (pool_shards - 1)
        shapes += [jax.ShapeDtypeStruct((2 * prompt_rows, HD), BF16)]
    else:
        shapes += [jax.ShapeDtypeStruct((pool_rows, HD), F32)]
    operands = [slots, limits, queries, out_grad, lse, delta, keys, values, *shards]
    if extra_prompt:
        operands.append(extra)

    def body(*refs):
        attend_body(len(shards), part_rows, prompt_rows, extra_prompt, *refs)

    return pl.pallas_call(
        body,
        in_specs=[SMEM, SMEM] + [VMEM] * (len(operands) - 2),
        out_specs=[VMEM] * len(shapes),
        out_shape=shapes,
        scratch_shapes=[
            pltpu.VMEM((pool_rows, HD), BF16),
            pltpu.VMEM((pool_rows, HD), F32),
            pltpu.VMEM((2, prompt_count, HD), BF16),
        ],
        name="attend",
    )(*operands)


def far_body(base_ref, limit_ref, q_ref, out_ref, lse_ref, delta_ref, shard_ref, child_ref, prompt_ref, gq_in, send_ref, gq_ref):
    heads = lse_ref.shape[0]
    cols = heads * BLOCK
    key_index = lax.broadcasted_iota(jnp.int32, (ROOT_ROWS, cols), 0)
    in_child = (lax.broadcasted_iota(jnp.int32, (1, cols), 1) % BLOCK) // CLEN
    key_part = shard_ref[0:ROOT_ROWS]
    value_part = shard_ref[ROOT_ROWS : 2 * ROOT_ROWS]
    key_total = jnp.zeros((ROOT_ROWS, HD), F32)
    value_total = jnp.zeros((ROOT_ROWS, HD), F32)
    for block in range(child_ref.shape[0] // BLOCK):
        start = block * BLOCK
        first = start // CLEN
        low = jnp.zeros((1, cols), jnp.int32)
        high = jnp.zeros((1, cols), jnp.int32)
        for k in range(PER):
            low = jnp.where(in_child == k, base_ref[first + k], low)
            high = jnp.where(in_child == k, base_ref[first + k] + limit_ref[first + k], high)
        allowed = (key_index >= low) & (key_index < high)
        query_grad, key_grad, value_grad = pair_grads(
            key_part,
            value_part,
            stacked(q_ref, ROOT_ROWS + start, heads),
            stacked(out_ref, ROOT_ROWS + start, heads),
            row_of(lse_ref, ROOT_ROWS + start, heads),
            row_of(delta_ref, ROOT_ROWS + start, heads),
            allowed,
        )
        key_total = key_total + key_grad
        value_total = value_total + value_grad
        query_grad = query_grad * SCALE
        for head in range(heads):
            columns = slice(head * HD, (head + 1) * HD)
            gq_ref[start : start + BLOCK, columns] = (
                child_ref[start : start + BLOCK, columns] + query_grad[head * BLOCK : (head + 1) * BLOCK]
            ).astype(BF16)
    send_ref[0:ROOT_ROWS] = key_total.astype(BF16)
    send_ref[ROOT_ROWS : 2 * ROOT_ROWS] = value_total.astype(BF16)
    send_ref[2 * ROOT_ROWS :] = prompt_ref[...]


def far_call(bases, limits, queries, out_grad, lse, delta, shard, child, prompt, gq):
    tokens, width = queries.shape
    return pl.pallas_call(
        far_body,
        grid=(1,),
        in_specs=[SMEM, SMEM] + [VMEM] * 7 + [pl.BlockSpec(memory_space=pl.ANY)],
        out_specs=[VMEM, pl.BlockSpec((tokens - ROOT_ROWS, width), lambda i: (1, 0))],
        out_shape=[jax.ShapeDtypeStruct(shard.shape, BF16), jax.ShapeDtypeStruct(gq.shape, BF16)],
        input_output_aliases={9: 1},
        name="attend_far",
    )(bases, limits, queries, out_grad, lse, delta, shard, child, prompt, gq)


def finish_body(key_ref, value_ref, prompt_ref, *refs):
    parts = refs[:-4]
    keys_out, values_out, prefix_keys_out, prefix_values_out = refs[-4:]
    own = prefix_keys_out.shape[0]
    total = parts[0][...].astype(F32)
    for part in parts[1:]:
        total = total + part[...].astype(F32)
    keys_out[0:ROOT_ROWS] = (key_ref[0:ROOT_ROWS] + total[0:ROOT_ROWS]).astype(BF16)
    keys_out[ROOT_ROWS:] = key_ref[ROOT_ROWS:].astype(BF16)
    values_out[0:ROOT_ROWS] = (value_ref[0:ROOT_ROWS] + total[ROOT_ROWS : 2 * ROOT_ROWS]).astype(BF16)
    values_out[ROOT_ROWS:] = value_ref[ROOT_ROWS:].astype(BF16)
    at = 2 * ROOT_ROWS
    prefix_keys_out[...] = (prompt_ref[0:own] + total[at : at + own]).astype(BF16)
    prefix_values_out[...] = (prompt_ref[own : 2 * own] + total[at + own : at + 2 * own]).astype(BF16)


def finish_call(key_sums, value_sums, prompt_sums, parts):
    own = prompt_sums.shape[0] // 2
    shapes = [jax.ShapeDtypeStruct(key_sums.shape, BF16)] * 2 + [jax.ShapeDtypeStruct((own, HD), BF16)] * 2
    return pl.pallas_call(
        finish_body,
        in_specs=[VMEM] * (3 + len(parts)),
        out_specs=[VMEM] * 4,
        out_shape=shapes,
        name="finish",
    )(key_sums, value_sums, prompt_sums, *parts)


def local(
    grad_out,
    out_weight,
    queries,
    attn_out,
    lse,
    keys,
    values,
    prefix_keys,
    prefix_values,
    fork_owner,
    fork_root,
    fork_offset,
):
    servers_count = lax.axis_size("servers")
    my_index = lax.axis_index("servers")
    prompt_rows = prefix_keys.shape[0]
    part_rows = 2 * ROOT_ROWS + 2 * prompt_rows
    own_part = jnp.concatenate([keys[:ROOT_ROWS], values[:ROOT_ROWS], prefix_keys, prefix_values], axis=0)
    start = my_index * CH_DEV
    my_owners = lax.dynamic_slice_in_dim(fork_owner[:, 0], start, CH_DEV, 0)
    my_roots = lax.dynamic_slice_in_dim(fork_root, start, CH_DEV, 0)
    my_offsets = lax.dynamic_slice_in_dim(fork_offset, start, CH_DEV, 0)
    if servers_count == 4:
        pairs = [[(i, i ^ d) for i in range(4)] for d in range(4)]
        part_two = lax.ppermute(own_part, "servers", pairs[2])
        part_one = lax.ppermute(own_part, "servers", pairs[1])
        prompt_far = lax.ppermute(own_part[2 * ROOT_ROWS :], "servers", pairs[3])
        part_far = lax.ppermute(part_two, "servers", pairs[1])
        out_grad, delta = out_grad_call(grad_out, out_weight, attn_out)
        where = my_owners ^ my_index
        near = where < 3
        slots = jnp.where(near, where * part_rows + my_roots * RLEN, 0)
        near_limits = jnp.where(near, my_offsets, 0)
        far_limits = jnp.where(near, 0, my_offsets)
        gq, child, key_sums, value_sums, prompt_sums, send_one, send_two, prompt_send = attend_call(
            slots,
            near_limits,
            queries,
            out_grad,
            lse,
            delta,
            keys,
            values,
            [own_part, part_one, part_two],
            prompt_far,
            prompt_rows,
        )
        back_one = lax.ppermute(send_one, "servers", pairs[1])
        back_two = lax.ppermute(send_two, "servers", pairs[2])
        send_far, grad_queries = far_call(
            my_roots * RLEN, far_limits, queries, out_grad, lse, delta, part_far, child, prompt_send, gq
        )
        back_far = lax.ppermute(send_far, "servers", pairs[3])
        parts = [back_one, back_two, back_far]
    else:
        all_parts = lax.all_gather(own_part, "servers", axis=0, tiled=True)
        out_grad, delta = out_grad_call(grad_out, out_weight, attn_out)
        slots = my_owners * part_rows + my_roots * RLEN
        gq, child, key_sums, value_sums, prompt_sums, sends = attend_call(
            slots, my_offsets, queries, out_grad, lse, delta, keys, values, [all_parts], None, prompt_rows
        )
        grad_queries = jnp.concatenate([gq[:ROOT_ROWS], child.astype(BF16)], axis=0)
        parts = [lax.psum_scatter(sends, "servers", scatter_dimension=0, tiled=True)]
    grads = finish_call(key_sums, value_sums, prompt_sums, parts)
    return (grad_queries, *grads)


def solution(mesh):
    placed = (
        P(("groups", "servers"), None),
        P(None, "heads"),
        P(("groups", "servers"), "heads"),
        P(("groups", "servers"), "heads"),
        P("heads", ("groups", "servers")),
        P(("groups", "servers"), "heads"),
        P(("groups", "servers"), "heads"),
        P(("groups", "servers"), "heads"),
        P(("groups", "servers"), "heads"),
        P("groups", None),
        P("groups"),
        P("groups"),
    )
    return jax.shard_map(
        local,
        mesh=mesh,
        in_specs=placed,
        out_specs=(P(("groups", "servers"), "heads"),) * 5,
        check_vma=False,
    )
```

time: 284 us -> 53.4 us (0.19)
  matrix products: 106 us -> 0 us
  blocking collectives: 56.1 us -> 0 us
  other arithmetic: 51.8 us -> 4.04 us
  local copies, waits for them, and re-layouts: 45.9 us -> 3.65 us
  Pallas kernels: 0 us -> 23 us
  between operations: 14 us -> 0.7 us
  waiting for transfers between devices: 0.77 us -> 11.3 us
  starting transfers between devices: 0.16 us -> 10.2 us
  loops' own time: 6.92 us -> 0 us
    dot_general x51 -> x0, matrix products: 106 us -> none  [the longest x10 24.4 us: block_step(): lax.dot_general(weights_low, out_flat, across, preferred_element_type=jnp...]
    all_gather x4 -> x0, blocking collectives: 56.1 us -> none  [the longest x1 14.8 us: local(): lax.all_gather(prefix_keys, 'servers', axis=0, tiled=True)]
    pallas_call x0 -> x4, Pallas kernels: none -> 23 us  [the longest x1 8.75 us: attend_call(): pl.pallas_call(body, in_specs=[SMEM, SMEM] + [VMEM] * (len(operands) - 2)...]
    select_n x7 -> x2, other arithmetic: 22 us -> 2.6 us  [the longest x1 1.35 us: local(): slots = jnp.where(near, where * part_rows + my_roots * RLEN, 0)]
    unnamed x39 -> x16, local copies, waits for them, and re-layouts: 15.8 us -> 1.96 us
    scatter-add x2 -> x0, other arithmetic: 13.5 us -> none  [the longest x1 6.83 us: local(): dense_keys = jnp.zeros((all_roots[0].shape[0], shared_width), jnp.float32...]
    ppermute x0 -> x7, waiting for transfers between devices: none -> 11.3 us  [the longest x1 5.7 us: local(): back_far = lax.ppermute(send_far, 'servers', pairs[3])]
    ppermute x0 -> x7, starting transfers between devices: none -> 10.2 us  [the longest x1 3.09 us: local(): part_one = lax.ppermute(own_part, 'servers', pairs[1])]
  transfers between devices with their start and end apart: 4 -> 7, of which waited for: 0 -> 3; matrix products, arithmetic and copies ran while one was open for 53% -> 6% of each run, Pallas kernels for 0% -> 40%
where the time goes in v1:
time: 53.4 us; the launch traced here: 52.9 us
  Pallas kernels  23 us (43%)
  waiting for transfers between devices  11.3 us (21%)
  starting transfers between devices  10.2 us (19%)
  other arithmetic  4.04 us (8%)
  local copies, waits for them, and re-layouts  3.65 us (7%)
  between operations  0.7 us (1%)
    pallas_call x1, Pallas kernels, attend_call(): pl.pallas_call(body, in_specs=[SMEM, SMEM] + [VMEM] * (len(operands) - 2)...  8.75 us
    pallas_call x1, Pallas kernels, out_grad_call(): pl.pallas_call(out_grad_body, grid=(cols // width,), in_specs=[pl.BlockSp...  7.45 us
    ppermute x1, waiting for transfers between devices, local(): back_far = lax.ppermute(send_far, 'servers', pairs[3])  5.7 us
    ppermute x1, waiting for transfers between devices, local(): part_two = lax.ppermute(own_part, 'servers', pairs[2])  5.41 us
    pallas_call x1, Pallas kernels, far_call(): pl.pallas_call(far_body, grid=(1,), in_specs=[SMEM, SMEM] + [VMEM] * 7 +...  4.9 us
    ppermute x1, starting transfers between devices, local(): part_one = lax.ppermute(own_part, 'servers', pairs[1])  3.09 us
    ppermute x1, starting transfers between devices, local(): part_two = lax.ppermute(own_part, 'servers', pairs[2])  2.59 us
    ppermute x1, starting transfers between devices, local(): back_one = lax.ppermute(send_one, 'servers', pairs[1])  2.02 us
  transfers between devices with their start and end apart: 7, of which 3 were waited for; matrix products, arithmetic and copies ran while one was open for 6% of the time, Pallas kernels for 40%

profile of v1, /device:TPU:0, one launch (start us, length us, event | category | flops | bytes accessed | tf_op | source)
XLA Modules:
  0.0 52.9 jit_solution(5673662262096328630)
XLA Ops:
  0.6 0.8 %slice.8 = bf16[256,128]{1,0:T(8,128)(2,1)S(1)} slice(bf16[512,128]{1,0:T(8,128)(2,1)} %refs_6_.1), slice={[0:256], [0:128]} | slice | bytes 131072 | tf_op jit(solution)/shard_map/slice | solution.py:351
  1.5 0.8 %slice.9 = bf16[256,128]{1,0:T(8,128)(2,1)S(1)} slice(bf16[512,128]{1,0:T(8,128)(2,1)} %refs_7_.1), slice={[0:256], [0:128]} | slice | bytes 131072 | tf_op jit(solution)/shard_map/slice | solution.py:351
  2.3 0.7 %pad_maximum_fusion.refs_8_ = bf16[576,128]{1,0:T(8,128)(2,1)S(1)} fusion(bf16[32,128]{1,0:T(8,128)(2,1)} %param.20, bf16[32,128]{1,0:T(8,128)(2,1)} %param.19, bf16[256,128]{1,0:T(8,128)(2,1)S(1)} %slice.9, bf16[256,128]{1,0:T(8,128)(2,1)S(1)} %slice.8), kind=kLoop, calls=%fused_computation | loop fusion | flops 589824 | bytes 294912 | tf_op jit(solution)/shard_map/concatenate | solution.py:351
  3.0 0.0 copy-start
  3.1 3.1 %collective-permute-start.2 = (bf16[576,128]{1,0:T(8,128)(2,1)S(1)}, bf16[576,128]{1,0:T(8,128)(2,1)S(1)}, u32[]{:S(2)}, u32[]{:S(2)}) collective-permute-start(bf16[576,128]{1,0:T(8,128)(2,1)S(1)} %pad_maximum_fusion.refs_8_), channel_id=1, source_target_pairs={{0,4},{4,0},{8,12},{12,8},{1,5},{5,1},{9,13},{13,9},{2,6},{6,2},{1... | collective-permute-start | bytes 442376 | tf_op jit(solution)/shard_map/ppermute | solution.py:359
  6.1 2.6 %collective-permute-start = (bf16[576,128]{1,0:T(8,128)(2,1)S(1)}, bf16[576,128]{1,0:T(8,128)(2,1)S(1)}, u32[]{:S(2)}, u32[]{:S(2)}) collective-permute-start(bf16[576,128]{1,0:T(8,128)(2,1)S(1)} %pad_maximum_fusion.refs_8_), channel_id=1, source_target_pairs={{0,8},{4,12},{8,0},{12,4},{1,9},{5,13},{9,1},{13,5},{2,10},{6,14},... | collective-permute-start | bytes 442376 | tf_op jit(solution)/shard_map/ppermute | solution.py:358
  8.7 0.7 %pad_maximum_fusion.1 = bf16[64,128]{1,0:T(8,128)(2,1)S(1)} fusion(bf16[32,128]{1,0:T(8,128)(2,1)} %param.20, bf16[32,128]{1,0:T(8,128)(2,1)} %param.19), kind=kLoop, calls=%fused_computation.1 | loop fusion | flops 32768 | bytes 32768 | tf_op jit(solution)/shard_map/concatenate | solution.py:351
  9.5 0.0 collective-permute-start.3
  9.5 1.3 %bitcast_select_fusion = (s32[16]{0:T(128)}, s32[16,1]{0,1:T(1,128)S(1)}) fusion(s32[64]{0:T(128)} %param.23, s32[]{:T(128)S(6)} %select_n.16, s32[]{:T(128)S(6)} %axis_index.15, s32[64,1]{0,1:T(1,128)} %param.21), kind=kLoop, calls=%fused_computation.2 | loop fusion | flops 48 | bytes 264 | tf_op jit(solution)/shard_map/jit(_where)/select_n | solution.py:366
  10.7 5.4 %collective-permute-done.refs_10_ = bf16[576,128]{1,0:T(8,128)(2,1)S(1)} collective-permute-done((bf16[576,128]{1,0:T(8,128)(2,1)S(1)}, bf16[576,128]{1,0:T(8,128)(2,1)S(1)}, u32[]{:S(2)}, u32[]{:S(2)}) %collective-permute-start) | collective-permute-done | bytes 147488 | tf_op jit(solution)/shard_map/ppermute | solution.py:358
  16.1 0.0 copy-start.5
  16.1 0.1 collective-permute-start.1
  16.2 1.3 %bitcast_select_fusion.1 = (s32[16]{0:T(128)}, s32[16]{0:T(128)}, s32[16]{0:T(128)}) fusion(s32[16,1]{0,1:T(1,128)S(1)} %get-tuple-element.38, s32[64]{0:T(128)} %param.22, s32[]{:T(128)S(6)} %select_n.16, s32[64]{0:T(128)} %param.23), kind=kLoop, calls=%fused_computation.3 | loop fusion | flops 96 | bytes 388 | tf_op jit(solution)/shard_map/jit(_where)/select_n | solution.py:365
  17.5 7.5 %out_grad.1 = (bf16[512,1024]{1,0:T(8,128)(2,1)}, f32[8,512]{1,0:T(8,128)}) custom-call(bf16[512,2048]{1,0:T(8,128)(2,1)} %grad_ref.1, bf16[2048,1024]{1,0:T(8,128)(2,1)} %weight_ref.1, bf16[512,1024]{1,0:T(8,128)(2,1)} %attn_ref.1), custom_call_target="tpu_custom_call" | custom-call | tf_op jit(solution)/shard_map/out_grad/pallas_call | solution.py:58
  25.0 0.0 collective-permute-done.3.refs_11_
  25.0 0.0 copy-start.7
  25.0 0.0 collective-permute-done.2.refs_9_
  25.0 0.0 copy-start.6
  25.0 0.0 copy-done
  25.0 0.0 copy-done.5
  25.0 0.6 %copy-done.7 = bf16[64,128]{1,0:T(8,128)(2,1)} copy-done((bf16[64,128]{1,0:T(8,128)(2,1)}, bf16[64,128]{1,0:T(8,128)(2,1)S(1)}, u32[]{:S(2)}) %copy-start.7) | copy-done | bytes 16408
  25.6 0.1 copy-done.6
  25.7 8.7 %attend.1 = (bf16[512,1024]{1,0:T(8,128)(2,1)}, f32[256,1024]{1,0:T(8,128)}, f32[512,128]{1,0:T(8,128)}, f32[512,128]{1,0:T(8,128)}, f32[64,128]{1,0:T(8,128)}, ...) custom-call(s32[16]{0:T(128)} %get-tuple-element.39.refs_0_, ...), custom_call_target="tpu_custom_call" | custom-call | tf_op jit(solution)/shard_map/attend/pallas_call | solution.py:238
  34.4 2.0 %collective-permute-start.4 = (bf16[576,128]{1,0:T(8,128)(2,1)}, bf16[576,128]{1,0:T(8,128)(2,1)S(1)}, u32[]{:S(2)}, u32[]{:S(2)}) collective-permute-start(bf16[576,128]{1,0:T(8,128)(2,1)} %get-tuple-element.30), channel_id=1, source_target_pairs={{0,4},{4,0},{8,12},{12,8},{1,5},{5,1},{9,13},{13,9},{2,6},{6,2},{1... | collective-permute-start | bytes 442376 | tf_op jit(solution)/shard_map/ppermute | solution.py:381
  36.4 1.0 %collective-permute-start.5 = (bf16[576,128]{1,0:T(8,128)(2,1)}, bf16[576,128]{1,0:T(8,128)(2,1)S(1)}, u32[]{:S(2)}, u32[]{:S(2)}) collective-permute-start(bf16[576,128]{1,0:T(8,128)(2,1)} %get-tuple-element.31), channel_id=1, source_target_pairs={{0,8},{4,12},{8,0},{12,4},{1,9},{5,13},{9,1},{13,5},{2,10},{6,14},... | collective-permute-start | bytes 442376 | tf_op jit(solution)/shard_map/ppermute | solution.py:382
  37.5 0.0 collective-permute-done.1.shard_ref
  37.5 0.0 copy-start.1
  37.5 0.7 %copy-done.1 = bf16[576,128]{1,0:T(8,128)(2,1)} copy-done((bf16[576,128]{1,0:T(8,128)(2,1)}, bf16[576,128]{1,0:T(8,128)(2,1)S(1)}, u32[]{:S(2)}) %copy-start.1) | copy-done | bytes 147480
  38.2 4.9 %attend_far.1 = (bf16[576,128]{1,0:T(8,128)(2,1)}, bf16[512,1024]{1,0:T(8,128)(2,1)}) custom-call(s32[16]{0:T(128)} %get-tuple-element.40.base_ref, s32[16]{0:T(128)} %get-tuple-element.41.limit_ref, bf16[512,1024]{1,0:T(8,128)(2,1)} %q_ref.1, bf16[512,1024]{1,0:T(8,128)(2,1)} %get-tuple-element.21.refs_3_.out_ref, ...), custom_call_target="tpu_custom_call", output_to_operand_aliasing={{1}: (9, {})} | custom-call | tf_op jit(solution)/shard_map/attend_far/pallas_call | solution.py:294
  43.1 1.4 %collective-permute-start.6 = (bf16[576,128]{1,0:T(8,128)(2,1)}, bf16[576,128]{1,0:T(8,128)(2,1)S(1)}, u32[]{:S(2)}, u32[]{:S(2)}) collective-permute-start(bf16[576,128]{1,0:T(8,128)(2,1)} %get-tuple-element.32), channel_id=1, source_target_pairs={{0,12},{4,8},{8,4},{12,0},{1,13},{5,9},{9,5},{13,1},{2,14},{6,10},... | collective-permute-start | bytes 442376 | tf_op jit(solution)/shard_map/ppermute | solution.py:386
  44.5 0.0 collective-permute-done.4.refs_0_
  44.5 0.0 copy-start.2
  44.5 0.1 collective-permute-done.5.refs_1_
  44.6 0.0 copy-start.3
  44.6 5.7 %collective-permute-done.6.refs_2_ = bf16[576,128]{1,0:T(8,128)(2,1)S(1)} collective-permute-done((bf16[576,128]{1,0:T(8,128)(2,1)}, bf16[576,128]{1,0:T(8,128)(2,1)S(1)}, u32[]{:S(2)}, u32[]{:S(2)}) %collective-permute-start.6) | collective-permute-done | bytes 147488 | tf_op jit(solution)/shard_map/ppermute | solution.py:386
  50.3 0.0 copy-start.4
  50.3 0.0 copy-done.2
  50.3 0.0 copy-done.3
  50.3 0.6 %copy-done.4 = bf16[576,128]{1,0:T(8,128)(2,1)} copy-done((bf16[576,128]{1,0:T(8,128)(2,1)}, bf16[576,128]{1,0:T(8,128)(2,1)S(1)}, u32[]{:S(2)}) %copy-start.4) | copy-done | bytes 147480
  51.0 1.9 %finish.1 = (bf16[512,128]{1,0:T(8,128)(2,1)}, bf16[512,128]{1,0:T(8,128)(2,1)}, bf16[32,128]{1,0:T(8,128)(2,1)}, bf16[32,128]{1,0:T(8,128)(2,1)}) custom-call(f32[512,128]{1,0:T(8,128)} %get-tuple-element.27.key_ref, f32[512,128]{1,0:T(8,128)} %get-tuple-element.28.value_ref, f32[64,128]{1,0:T(8,128)} %get-tuple-element.29.prompt_ref, ...), custom_call_target="tpu_custom_call" | custom-call | tf_op jit(solution)/shard_map/finish/pallas_call | solution.py:324
Async XLA Ops:
  3.0 22.0 %copy-start = (bf16[576,128]{1,0:T(8,128)(2,1)}, bf16[576,128]{1,0:T(8,128)(2,1)S(1)}, u32[]{:S(2)}) copy-start(bf16[576,128]{1,0:T(8,128)(2,1)S(1)} %pad_maximum_fusion.refs_8_) | copy-start | bytes 442372
  3.1 21.9 %collective-permute-start.2 = (bf16[576,128]{1,0:T(8,128)(2,1)S(1)}, bf16[576,128]{1,0:T(8,128)(2,1)S(1)}, u32[]{:S(2)}, u32[]{:S(2)}) collective-permute-start(bf16[576,128]{1,0:T(8,128)(2,1)S(1)} %pad_maximum_fusion.refs_8_), channel_id=1, source_target_pairs={{0,4},{4,0},{8,12},{12,8},{1,5},{5,1},{9,13},{13,9},{2,6},{6,2},{1... | collective-permute-start | bytes 442376 | tf_op jit(solution)/shard_map/ppermute | solution.py:359
  6.1 10.0 %collective-permute-start = (bf16[576,128]{1,0:T(8,128)(2,1)S(1)}, bf16[576,128]{1,0:T(8,128)(2,1)S(1)}, u32[]{:S(2)}, u32[]{:S(2)}) collective-permute-start(bf16[576,128]{1,0:T(8,128)(2,1)S(1)} %pad_maximum_fusion.refs_8_), channel_id=1, source_target_pairs={{0,8},{4,12},{8,0},{12,4},{1,9},{5,13},{9,1},{13,5},{2,10},{6,14},... | collective-permute-start | bytes 442376 | tf_op jit(solution)/shard_map/ppermute | solution.py:358
  9.5 15.5 %collective-permute-start.3 = (bf16[64,128]{1,0:T(8,128)(2,1)S(1)}, bf16[64,128]{1,0:T(8,128)(2,1)S(1)}, u32[]{:S(2)}, u32[]{:S(2)}) collective-permute-start(bf16[64,128]{1,0:T(8,128)(2,1)S(1)} %pad_maximum_fusion.1), channel_id=1, source_target_pairs={{0,12},{4,8},{8,4},{12,0},{1,13},{5,9},{9,5},{13,1},{2,14},{6,10},... | collective-permute-start | bytes 49160 | tf_op jit(solution)/shard_map/ppermute | solution.py:360
  16.1 8.9 %copy-start.5 = (bf16[576,128]{1,0:T(8,128)(2,1)}, bf16[576,128]{1,0:T(8,128)(2,1)S(1)}, u32[]{:S(2)}) copy-start(bf16[576,128]{1,0:T(8,128)(2,1)S(1)} %collective-permute-done.refs_10_) | copy-start | bytes 442372
  16.1 21.4 %collective-permute-start.1 = (bf16[576,128]{1,0:T(8,128)(2,1)S(1)}, bf16[576,128]{1,0:T(8,128)(2,1)S(1)}, u32[]{:S(2)}, u32[]{:S(2)}) collective-permute-start(bf16[576,128]{1,0:T(8,128)(2,1)S(1)} %collective-permute-done.refs_10_), channel_id=1, source_target_pairs={{0,4},{4,0},{8,12},{12,8},{1,5},{5,1},{9,13},{13,9},{2,6},{6,2},{1... | collective-permute-start | bytes 442376 | tf_op jit(solution)/shard_map/ppermute | solution.py:361
  25.0 0.6 %copy-start.7 = (bf16[64,128]{1,0:T(8,128)(2,1)}, bf16[64,128]{1,0:T(8,128)(2,1)S(1)}, u32[]{:S(2)}) copy-start(bf16[64,128]{1,0:T(8,128)(2,1)S(1)} %collective-permute-done.3.refs_11_) | copy-start | bytes 49156
  25.0 0.7 %copy-start.6 = (bf16[576,128]{1,0:T(8,128)(2,1)}, bf16[576,128]{1,0:T(8,128)(2,1)S(1)}, u32[]{:S(2)}) copy-start(bf16[576,128]{1,0:T(8,128)(2,1)S(1)} %collective-permute-done.2.refs_9_) | copy-start | bytes 442372
  34.4 10.0 %collective-permute-start.4 = (bf16[576,128]{1,0:T(8,128)(2,1)}, bf16[576,128]{1,0:T(8,128)(2,1)S(1)}, u32[]{:S(2)}, u32[]{:S(2)}) collective-permute-start(bf16[576,128]{1,0:T(8,128)(2,1)} %get-tuple-element.30), channel_id=1, source_target_pairs={{0,4},{4,0},{8,12},{12,8},{1,5},{5,1},{9,13},{13,9},{2,6},{6,2},{1... | collective-permute-start | bytes 442376 | tf_op jit(solution)/shard_map/ppermute | solution.py:381
  36.4 8.2 %collective-permute-start.5 = (bf16[576,128]{1,0:T(8,128)(2,1)}, bf16[576,128]{1,0:T(8,128)(2,1)S(1)}, u32[]{:S(2)}, u32[]{:S(2)}) collective-permute-start(bf16[576,128]{1,0:T(8,128)(2,1)} %get-tuple-element.31), channel_id=1, source_target_pairs={{0,8},{4,12},{8,0},{12,4},{1,9},{5,13},{9,1},{13,5},{2,10},{6,14},... | collective-permute-start | bytes 442376 | tf_op jit(solution)/shard_map/ppermute | solution.py:382
  37.5 0.7 %copy-start.1 = (bf16[576,128]{1,0:T(8,128)(2,1)}, bf16[576,128]{1,0:T(8,128)(2,1)S(1)}, u32[]{:S(2)}) copy-start(bf16[576,128]{1,0:T(8,128)(2,1)S(1)} %collective-permute-done.1.shard_ref) | copy-start | bytes 442372
  43.1 7.3 %collective-permute-start.6 = (bf16[576,128]{1,0:T(8,128)(2,1)}, bf16[576,128]{1,0:T(8,128)(2,1)S(1)}, u32[]{:S(2)}, u32[]{:S(2)}) collective-permute-start(bf16[576,128]{1,0:T(8,128)(2,1)} %get-tuple-element.32), channel_id=1, source_target_pairs={{0,12},{4,8},{8,4},{12,0},{1,13},{5,9},{9,5},{13,1},{2,14},{6,10},... | collective-permute-start | bytes 442376 | tf_op jit(solution)/shard_map/ppermute | solution.py:386
  44.5 5.9 %copy-start.2 = (bf16[576,128]{1,0:T(8,128)(2,1)}, bf16[576,128]{1,0:T(8,128)(2,1)S(1)}, u32[]{:S(2)}) copy-start(bf16[576,128]{1,0:T(8,128)(2,1)S(1)} %collective-permute-done.4.refs_0_) | copy-start | bytes 442372
  44.6 5.7 %copy-start.3 = (bf16[576,128]{1,0:T(8,128)(2,1)}, bf16[576,128]{1,0:T(8,128)(2,1)S(1)}, u32[]{:S(2)}) copy-start(bf16[576,128]{1,0:T(8,128)(2,1)S(1)} %collective-permute-done.5.refs_1_) | copy-start | bytes 442372
  50.3 0.6 %copy-start.4 = (bf16[576,128]{1,0:T(8,128)(2,1)}, bf16[576,128]{1,0:T(8,128)(2,1)S(1)}, u32[]{:S(2)}) copy-start(bf16[576,128]{1,0:T(8,128)(2,1)S(1)} %collective-permute-done.6.refs_2_) | copy-start | bytes 442372

commit v2 on v1

v2 whole, which is shorter than its diff:
```python
import math

import jax
import jax.numpy as jnp
from jax import lax
from jax.experimental import pallas as pl
from jax.experimental.pallas import tpu as pltpu
from jax.sharding import PartitionSpec as P

HD = 128
CH_DEV = 16
ROOTS_DEV = 4
RLEN = 64
CLEN = 16
ROOT_ROWS = ROOTS_DEV * RLEN
BLOCK = 64
PER = BLOCK // CLEN
UNIT_HEADS = 4
UNIT = UNIT_HEADS * BLOCK
SCALE = HD ** (-0.5)
LOG2E = math.log2(math.e)
NT = (((1,), (1,)), ((), ()))
NN = (((1,), (0,)), ((), ()))
TN = (((0,), (0,)), ((), ()))
F32 = jnp.float32
BF16 = jnp.bfloat16
VMEM = pl.BlockSpec(memory_space=pltpu.VMEM)
SMEM = pl.BlockSpec(memory_space=pltpu.SMEM)
ANY = pl.BlockSpec(memory_space=pl.ANY)


def params(mib):
    return pltpu.CompilerParams(vmem_limit_bytes=mib * 1024 * 1024)


def cost(micros):
    return pl.CostEstimate(flops=micros << 30, transcendentals=0, bytes_accessed=1 << 16)


def pinned(array):
    return pltpu.with_memory_space_constraint(array, pltpu.VMEM)


def unmoved(array):
    return pltpu.with_memory_space_constraint(array, pltpu.HBM)


def pinned_scalars(array):
    return pltpu.with_memory_space_constraint(array, pltpu.SMEM)


def kept(shape, dtype):
    return pltpu.VMEM(shape, dtype)


def dot(left, right, numbers):
    return lax.dot_general(left, right, numbers, preferred_element_type=F32)


def pack_body(key_ref, value_ref, prefix_key_ref, prefix_value_ref, part_ref, prompt_ref, sems):
    own = prefix_key_ref.shape[0]
    at = 2 * ROOT_ROWS
    copies = [
        (key_ref.at[0:ROOT_ROWS], part_ref.at[0:ROOT_ROWS]),
        (value_ref.at[0:ROOT_ROWS], part_ref.at[ROOT_ROWS:at]),
        (prefix_key_ref, part_ref.at[at : at + own]),
        (prefix_value_ref, part_ref.at[at + own : at + 2 * own]),
        (prefix_key_ref, prompt_ref.at[0:own]),
        (prefix_value_ref, prompt_ref.at[own : 2 * own]),
    ]
    started = [pltpu.make_async_copy(a, b, sems.at[i]) for i, (a, b) in enumerate(copies)]
    for copy in started:
        copy.start()
    for copy in started:
        copy.wait()


def pack_call(keys, values, prefix_keys, prefix_values):
    own = prefix_keys.shape[0]
    return pl.pallas_call(
        pack_body,
        in_specs=[ANY] * 4,
        out_specs=[VMEM] * 2,
        out_shape=[kept((2 * ROOT_ROWS + 2 * own, HD), BF16), kept((2 * own, HD), BF16)],
        scratch_shapes=[pltpu.SemaphoreType.DMA((6,))],
        compiler_params=params(4),
        cost_estimate=cost(8),
        name="pack",
    )(*(unmoved(x) for x in (keys, values, prefix_keys, prefix_values)))


def out_grad_body(grad_ref, weight_ref, attn_ref, out_ref, delta_ref):
    rows, cols = out_ref.shape
    width = 2 * HD
    lane = lax.broadcasted_iota(jnp.int32, (rows, HD), 1)
    columns = jnp.zeros((rows, HD), F32)
    for step in range(cols // width):
        part = slice(step * width, (step + 1) * width)
        wide = jnp.dot(grad_ref[...], weight_ref[:, part], preferred_element_type=F32).astype(BF16)
        out_ref[:, part] = wide
        products = wide.astype(F32) * attn_ref[:, part].astype(F32)
        for head in range(width // HD):
            total = jnp.sum(products[:, head * HD : (head + 1) * HD], axis=1, keepdims=True)
            columns = jnp.where(lane == step * (width // HD) + head, total, columns)
    delta_ref[...] = jnp.transpose(columns)[: delta_ref.shape[0]]


def out_grad_call(grad_out, out_weight, attn_out):
    rows = grad_out.shape[0]
    cols = out_weight.shape[1]
    return pl.pallas_call(
        out_grad_body,
        in_specs=[VMEM] * 3,
        out_specs=[VMEM] * 2,
        out_shape=[kept((rows, cols), BF16), kept((cols // HD, rows), F32)],
        compiler_params=params(12),
        cost_estimate=cost(6),
        name="out_grad",
    )(pinned(grad_out), pinned(out_weight), pinned(attn_out))


def stacked(ref, start, first):
    return jnp.concatenate(
        [ref[start : start + BLOCK, head * HD : (head + 1) * HD] for head in range(first, first + UNIT_HEADS)],
        axis=0,
    )


def row_of(ref, start, first):
    return jnp.concatenate(
        [ref[head : head + 1, start : start + BLOCK] for head in range(first, first + UNIT_HEADS)], axis=1
    )


def pair_grads(key_part, value_part, query, out, lse, delta, mask):
    weights = mask(jnp.exp2(dot(key_part, query, NT) * (SCALE * LOG2E) - lse * LOG2E))
    weight_grads = dot(value_part, out, NT)
    score_grads = (weights * (weight_grads - delta)).astype(BF16)
    return dot(score_grads, query, NN), dot(weights.astype(BF16), out, NN), score_grads


def places(owner_ref, root_ref, limit_ref, pool_shards, part_rows):
    my_index = lax.axis_index("servers")
    count = lax.axis_size("servers")
    bases, limits = [], []
    for child in range(CH_DEV):
        at = my_index * CH_DEV + child
        slot = owner_ref[at] ^ my_index if count == 4 else owner_ref[at]
        inside = slot < pool_shards
        base = jnp.where(inside, slot * part_rows, 0) + root_ref[at] * RLEN
        bases.append(pl.multiple_of(base, BLOCK))
        limits.append(jnp.where(inside, limit_ref[at], 0))
    return bases, limits


def attend_body(shard_count, part_rows, prompt_rows, has_far, *refs):
    (owner_ref, root_ref, limit_ref, q_ref, out_ref, lse_ref, delta_ref) = refs[:7]
    shards = refs[7 : 7 + shard_count]
    refs = refs[7 + shard_count :]
    if has_far:
        far_ref, refs = refs[0], refs[1:]
    root_ds_ref, child_ds_ref, key_pool_ref, own_ref, *send_refs = refs[:-3]
    pool_ref, sums_ref, values_ref = refs[-3:]
    heads = lse_ref.shape[0]
    tokens = q_ref.shape[0]
    pool_at = 0
    for shard in shards:
        pool_ref[pool_at : pool_at + shard.shape[0]] = shard[...]
        pool_at += shard.shape[0]
    pool_shards = pool_at // part_rows
    bases, limits = places(owner_ref, root_ref, limit_ref, pool_shards, part_rows)
    own = prompt_rows
    prompt_keys, prompt_values = [], []
    for index in range(pool_shards):
        at = index * part_rows + 2 * ROOT_ROWS
        prompt_keys.append(pool_ref[at : at + own])
        prompt_values.append(pool_ref[at + own : at + 2 * own])
    if has_far:
        prompt_keys.append(far_ref[0:own])
        prompt_values.append(far_ref[own : 2 * own])
    prompt_count = own * len(prompt_keys)
    sums_ref[...] = jnp.zeros(sums_ref.shape, F32)
    blocks = key_pool_ref.shape[0]
    for block in range(blocks):
        key_pool_ref[block, 0:prompt_count] = jnp.concatenate(prompt_keys, axis=0)
        for k in range(PER):
            base = bases[block * PER + k]
            at = prompt_count + k * RLEN
            key_pool_ref[block, at : at + RLEN] = pool_ref[pl.ds(base, RLEN)]
            values_ref[block, at : at + RLEN] = pool_ref[pl.ds(base + ROOT_ROWS, RLEN)]
    values_ref[0, 0:prompt_count] = jnp.concatenate(prompt_values, axis=0)
    for block in range(1, blocks):
        values_ref[block, 0:prompt_count] = values_ref[0, 0:prompt_count]
    key_index = lax.broadcasted_iota(jnp.int32, (RLEN, UNIT), 0)
    in_child = (lax.broadcasted_iota(jnp.int32, (RLEN, UNIT), 1) % BLOCK) // CLEN
    prompt_key_sum = jnp.zeros((prompt_count, HD), F32)
    prompt_value_sum = jnp.zeros((prompt_count, HD), F32)
    for block in range(blocks):
        start = ROOT_ROWS + block * BLOCK
        key_sum = jnp.zeros((PER * RLEN, HD), F32)
        value_sum = jnp.zeros((PER * RLEN, HD), F32)

        def mask(weights):
            pieces = [weights[0:prompt_count]]
            for k in range(PER):
                at = prompt_count + k * RLEN
                allowed = (key_index < limits[block * PER + k]) & (in_child == k)
                pieces.append(jnp.where(allowed, weights[at : at + RLEN], 0.0))
            return jnp.concatenate(pieces, axis=0)

        for unit in range(heads // UNIT_HEADS):
            first = unit * UNIT_HEADS
            key_grad, value_grad, score_grads = pair_grads(
                key_pool_ref[block],
                values_ref[block],
                stacked(q_ref, start, first),
                stacked(out_ref, start, first),
                row_of(lse_ref, start, first),
                row_of(delta_ref, start, first),
                mask,
            )
            child_ds_ref[block, unit] = score_grads
            prompt_key_sum = prompt_key_sum + key_grad[0:prompt_count]
            prompt_value_sum = prompt_value_sum + value_grad[0:prompt_count]
            key_sum = key_sum + key_grad[prompt_count:]
            value_sum = value_sum + value_grad[prompt_count:]
        for k in range(PER):
            base = bases[block * PER + k]
            rows = slice(k * RLEN, (k + 1) * RLEN)
            sums_ref[pl.ds(base, RLEN)] = sums_ref[pl.ds(base, RLEN)] + key_sum[rows] * SCALE
            at = base + ROOT_ROWS
            sums_ref[pl.ds(at, RLEN)] = sums_ref[pl.ds(at, RLEN)] + value_sum[rows]
    for block in range(ROOT_ROWS // BLOCK):
        start = block * BLOCK
        for unit in range(heads // UNIT_HEADS):
            first = unit * UNIT_HEADS
            key_grad, value_grad, score_grads = pair_grads(
                key_pool_ref[0, 0:prompt_count],
                values_ref[0, 0:prompt_count],
                stacked(q_ref, start, first),
                stacked(out_ref, start, first),
                row_of(lse_ref, start, first),
                row_of(delta_ref, start, first),
                lambda weights: weights,
            )
            root_ds_ref[block, unit] = score_grads
            prompt_key_sum = prompt_key_sum + key_grad
            prompt_value_sum = prompt_value_sum + value_grad
    prompt_key_sum = prompt_key_sum * SCALE
    for index in range(pool_shards):
        at = index * part_rows + 2 * ROOT_ROWS
        sums_ref[at : at + own] = prompt_key_sum[index * own : (index + 1) * own]
        sums_ref[at + own : at + 2 * own] = prompt_value_sum[index * own : (index + 1) * own]
    if has_far:
        own_ref[...] = sums_ref[0:part_rows]
        for index in range(1, pool_shards):
            send_refs[index - 1][...] = sums_ref[index * part_rows : (index + 1) * part_rows].astype(BF16)
        send_refs[-1][0:own] = prompt_key_sum[pool_shards * own :].astype(BF16)
        send_refs[-1][own : 2 * own] = prompt_value_sum[pool_shards * own :].astype(BF16)
    else:
        own_ref[...] = sums_ref[...]


def attend_call(forks, queries, out_grad, lse, delta, shards, far_prompt, prompt_rows):
    tokens, width = queries.shape
    heads = width // HD
    part_rows = 2 * ROOT_ROWS + 2 * prompt_rows
    pool_rows = sum(shard.shape[0] for shard in shards)
    pool_shards = pool_rows // part_rows
    has_far = far_prompt is not None
    prompt_count = (pool_shards + (1 if has_far else 0)) * prompt_rows
    units = heads // UNIT_HEADS
    blocks = (tokens - ROOT_ROWS) // BLOCK
    child_keys = prompt_count + PER * RLEN
    shapes = [
        kept((ROOT_ROWS // BLOCK, units, prompt_count, UNIT), BF16),
        kept((blocks, units, child_keys, UNIT), BF16),
        kept((blocks, child_keys, HD), BF16),
    ]
    operands = [pinned(x) for x in (queries, out_grad, lse, delta, *shards)]
    if has_far:
        operands.append(pinned(far_prompt))
        shapes.append(kept((part_rows, HD), F32))
        shapes += [kept((part_rows, HD), BF16)] * (pool_shards - 1)
        shapes.append(kept((2 * prompt_rows, HD), BF16))
    else:
        shapes.append(jax.ShapeDtypeStruct((pool_rows, HD), F32))

    def body(*refs):
        attend_body(len(shards), part_rows, prompt_rows, has_far, *refs)

    return pl.pallas_call(
        body,
        in_specs=[SMEM] * 3 + [VMEM] * len(operands),
        out_specs=[VMEM] * len(shapes),
        out_shape=shapes,
        scratch_shapes=[
            pltpu.VMEM((pool_rows, HD), BF16),
            pltpu.VMEM((pool_rows, HD), F32),
            pltpu.VMEM((blocks, child_keys, HD), BF16),
        ],
        compiler_params=params(16 if has_far else 40),
        cost_estimate=cost(5),
        name="attend",
    )(*forks, *operands)


def far_body(owner_ref, root_ref, limit_ref, q_ref, out_ref, lse_ref, delta_ref, shard_ref, prompt_ref, send_ref, ds_ref):
    heads = lse_ref.shape[0]
    my_index = lax.axis_index("servers")
    key_index = lax.broadcasted_iota(jnp.int32, (ROOT_ROWS, UNIT), 0)
    in_child = (lax.broadcasted_iota(jnp.int32, (1, UNIT), 1) % BLOCK) // CLEN
    key_part = shard_ref[0:ROOT_ROWS]
    value_part = shard_ref[ROOT_ROWS : 2 * ROOT_ROWS]
    key_total = jnp.zeros((ROOT_ROWS, HD), F32)
    value_total = jnp.zeros((ROOT_ROWS, HD), F32)
    for block in range(ds_ref.shape[0]):
        start = ROOT_ROWS + block * BLOCK
        low = jnp.zeros((1, UNIT), jnp.int32)
        high = jnp.zeros((1, UNIT), jnp.int32)
        for k in range(PER):
            at = my_index * CH_DEV + block * PER + k
            base = root_ref[at] * RLEN
            limit = jnp.where((owner_ref[at] ^ my_index) == 3, limit_ref[at], 0)
            low = jnp.where(in_child == k, base, low)
            high = jnp.where(in_child == k, base + limit, high)
        allowed = (key_index >= low) & (key_index < high)
        for unit in range(heads // UNIT_HEADS):
            first = unit * UNIT_HEADS
            key_grad, value_grad, score_grads = pair_grads(
                key_part,
                value_part,
                stacked(q_ref, start, first),
                stacked(out_ref, start, first),
                row_of(lse_ref, start, first),
                row_of(delta_ref, start, first),
                lambda weights: jnp.where(allowed, weights, 0.0),
            )
            ds_ref[block, unit] = score_grads
            key_total = key_total + key_grad
            value_total = value_total + value_grad
    send_ref[0:ROOT_ROWS] = (key_total * SCALE).astype(BF16)
    send_ref[ROOT_ROWS : 2 * ROOT_ROWS] = value_total.astype(BF16)
    send_ref[2 * ROOT_ROWS :] = prompt_ref[...]


def far_call(forks, queries, out_grad, lse, delta, shard, prompt):
    tokens, width = queries.shape
    blocks = (tokens - ROOT_ROWS) // BLOCK
    units = width // HD // UNIT_HEADS
    return pl.pallas_call(
        far_body,
        in_specs=[SMEM] * 3 + [VMEM] * 6,
        out_specs=[VMEM] * 2,
        out_shape=[kept(shard.shape, BF16), kept((blocks, units, ROOT_ROWS, UNIT), BF16)],
        compiler_params=params(12),
        cost_estimate=cost(3),
        name="attend_far",
    )(*forks, *(pinned(x) for x in (queries, out_grad, lse, delta, shard, prompt)))


def own_body(has_far, *refs):
    (q_ref, out_ref, lse_ref, delta_ref, key_ref, value_ref, root_ds_ref, child_ds_ref, key_pool_ref) = refs[:9]
    refs = refs[9:]
    if has_far:
        (far_ds_ref, far_ref), refs = refs[:2], refs[2:]
    gq_ref, keys_out, values_out, gq_vmem, sems = refs
    heads = lse_ref.shape[0]
    tokens = q_ref.shape[0]
    prompt_count = root_ds_ref.shape[2]
    key_index = lax.broadcasted_iota(jnp.int32, (BLOCK, UNIT), 0)
    token_index = lax.broadcasted_iota(jnp.int32, (BLOCK, UNIT), 1) % BLOCK
    root_allowed = key_index <= token_index
    child_allowed = root_allowed & (key_index // CLEN == token_index // CLEN)
    copies = []
    for block in range(tokens // BLOCK):
        start = block * BLOCK
        rows = slice(start, start + BLOCK)
        in_root = start < ROOT_ROWS
        allowed = root_allowed if in_root else child_allowed
        child = block - ROOT_ROWS // BLOCK
        key_sum = jnp.zeros((BLOCK, HD), F32)
        value_sum = jnp.zeros((BLOCK, HD), F32)
        key_parts = [key_ref[rows], key_pool_ref[0, 0:prompt_count] if in_root else key_pool_ref[child]]
        if has_far and not in_root:
            key_parts.append(far_ref[0:ROOT_ROWS])
        key_all = jnp.concatenate(key_parts, axis=0)
        for unit in range(heads // UNIT_HEADS):
            first = unit * UNIT_HEADS
            key_grad, value_grad, score_grads = pair_grads(
                key_ref[rows],
                value_ref[rows],
                stacked(q_ref, start, first),
                stacked(out_ref, start, first),
                row_of(lse_ref, start, first),
                row_of(delta_ref, start, first),
                lambda weights: jnp.where(allowed, weights, 0.0),
            )
            key_sum = key_sum + key_grad
            value_sum = value_sum + value_grad
            parts = [score_grads, root_ds_ref[block, unit] if in_root else child_ds_ref[child, unit]]
            if has_far and not in_root:
                parts.append(far_ds_ref[child, unit])
            total = dot(jnp.concatenate(parts, axis=0), key_all, TN) * SCALE
            for index in range(UNIT_HEADS):
                head = first + index
                gq_vmem[rows, head * HD : (head + 1) * HD] = total[index * BLOCK : (index + 1) * BLOCK].astype(BF16)
        keys_out[rows] = key_sum * SCALE
        values_out[rows] = value_sum
        copy = pltpu.make_async_copy(gq_vmem.at[rows], gq_ref.at[rows], sems.at[block])
        copy.start()
        copies.append(copy)
    for copy in copies:
        copy.wait()


def own_call(queries, out_grad, lse, delta, keys, values, root_ds, child_ds, key_pool, far):
    tokens, width = queries.shape
    operands = [pinned(x) for x in (queries, out_grad, lse, delta, keys, values, root_ds, child_ds, key_pool, *far)]

    def body(*refs):
        own_body(bool(far), *refs)

    return pl.pallas_call(
        body,
        in_specs=[VMEM] * len(operands),
        out_specs=[ANY, VMEM, VMEM],
        out_shape=[
            jax.ShapeDtypeStruct((tokens, width), BF16),
            kept((tokens, HD), F32),
            kept((tokens, HD), F32),
        ],
        scratch_shapes=[pltpu.VMEM((tokens, width), BF16), pltpu.SemaphoreType.DMA((tokens // BLOCK,))],
        compiler_params=params(12 if far else 20),
        cost_estimate=cost(5),
        name="attend_own",
    )(*operands)


def finish_body(key_ref, value_ref, *refs):
    parts = refs[:-4]
    keys_out, values_out, prefix_keys_out, prefix_values_out = refs[-4:]
    own = prefix_keys_out.shape[0]
    total = parts[0][...].astype(F32)
    for part in parts[1:]:
        total = total + part[...].astype(F32)
    keys_out[0:ROOT_ROWS] = (key_ref[0:ROOT_ROWS] + total[0:ROOT_ROWS]).astype(BF16)
    keys_out[ROOT_ROWS:] = key_ref[ROOT_ROWS:].astype(BF16)
    values_out[0:ROOT_ROWS] = (value_ref[0:ROOT_ROWS] + total[ROOT_ROWS : 2 * ROOT_ROWS]).astype(BF16)
    values_out[ROOT_ROWS:] = value_ref[ROOT_ROWS:].astype(BF16)
    at = 2 * ROOT_ROWS
    prefix_keys_out[...] = total[at : at + own].astype(BF16)
    prefix_values_out[...] = total[at + own : at + 2 * own].astype(BF16)


def finish_call(key_sums, value_sums, parts):
    own = (parts[0].shape[0] - 2 * ROOT_ROWS) // 2
    shapes = [jax.ShapeDtypeStruct(key_sums.shape, BF16)] * 2 + [jax.ShapeDtypeStruct((own, HD), BF16)] * 2
    return pl.pallas_call(
        finish_body,
        in_specs=[VMEM] * (2 + len(parts)),
        out_specs=[VMEM] * 4,
        out_shape=shapes,
        compiler_params=params(8),
        cost_estimate=cost(1),
        name="finish",
    )(*(pinned(x) for x in (key_sums, value_sums, *parts)))


def local(
    grad_out,
    out_weight,
    queries,
    attn_out,
    lse,
    keys,
    values,
    prefix_keys,
    prefix_values,
    fork_owner,
    fork_root,
    fork_offset,
):
    prompt_rows = prefix_keys.shape[0]
    own_part, own_prompt = pack_call(keys, values, prefix_keys, prefix_values)
    forks = [pinned_scalars(x) for x in (fork_owner.reshape(-1), fork_root, fork_offset)]
    if lax.axis_size("servers") == 4:
        pairs = [[(i, i ^ d) for i in range(4)] for d in range(4)]
        part_two = lax.ppermute(own_part, "servers", pairs[2])
        part_one = lax.ppermute(own_part, "servers", pairs[1])
        prompt_far = lax.ppermute(own_prompt, "servers", pairs[3])
        out_grad, delta = out_grad_call(grad_out, out_weight, attn_out)
        part_two, delta = lax.optimization_barrier((part_two, delta))
        part_far = lax.ppermute(part_two, "servers", pairs[1])
        root_ds, child_ds, key_pool, own_sums, send_one, send_two, prompt_send = attend_call(
            forks, queries, out_grad, lse, delta, [own_part, part_one, part_two], prompt_far, prompt_rows
        )
        back_two = lax.ppermute(send_two, "servers", pairs[2])
        back_one = lax.ppermute(send_one, "servers", pairs[1])
        send_far, far_ds = far_call(forks, queries, out_grad, lse, delta, part_far, prompt_send)
        back_far = lax.ppermute(send_far, "servers", pairs[3])
        grad_queries, key_sums, value_sums = own_call(
            queries, out_grad, lse, delta, keys, values, root_ds, child_ds, key_pool, (far_ds, part_far)
        )
        parts = [own_sums, back_one, back_two, back_far]
    else:
        all_parts = lax.all_gather(own_part, "servers", axis=0, tiled=True)
        out_grad, delta = out_grad_call(grad_out, out_weight, attn_out)
        root_ds, child_ds, key_pool, sends = attend_call(
            forks, queries, out_grad, lse, delta, [all_parts], None, prompt_rows
        )
        grad_queries, key_sums, value_sums = own_call(
            queries, out_grad, lse, delta, keys, values, root_ds, child_ds, key_pool, ()
        )
        parts = [lax.psum_scatter(sends, "servers", scatter_dimension=0, tiled=True)]
    grads = finish_call(key_sums, value_sums, parts)
    return (grad_queries, *grads)


def solution(mesh):
    placed = (
        P(("groups", "servers"), None),
        P(None, "heads"),
        P(("groups", "servers"), "heads"),
        P(("groups", "servers"), "heads"),
        P("heads", ("groups", "servers")),
        P(("groups", "servers"), "heads"),
        P(("groups", "servers"), "heads"),
        P(("groups", "servers"), "heads"),
        P(("groups", "servers"), "heads"),
        P("groups", None),
        P("groups"),
        P("groups"),
    )
    return jax.shard_map(
        local,
        mesh=mesh,
        in_specs=placed,
        out_specs=(P(("groups", "servers"), "heads"),) * 5,
        check_vma=False,
    )
```

time: 53.4 us -> 34.2 us (0.64)
  Pallas kernels: 23 us -> 15.7 us
  waiting for transfers between devices: 11.3 us -> 7.14 us
  other arithmetic: 4.04 us -> 0 us
  local copies, waits for them, and re-layouts: 3.65 us -> 0.04 us
    pallas_call x4 -> x6, Pallas kernels: 23 us -> 15.7 us  [the longest x1 4.36 us: attend_call(): pl.pallas_call(body, in_specs=[SMEM] * 3 + [VMEM] * len(operands), out_sp...]
    ppermute x1, waiting for transfers between devices: 5.7 us -> 0.01 us  [local(): back_far = lax.ppermute(send_far, 'servers', pairs[3])]
    select_n x2 -> x0, other arithmetic: 2.6 us -> none  [the longest x1 1.35 us: local(): slots = jnp.where(near, where * part_rows + my_roots * RLEN, 0)]
    ppermute x1, waiting for transfers between devices: 0.15 us -> 2.52 us  [local(): back_two = lax.ppermute(send_two, 'servers', pairs[2])]
    unnamed x16 -> x20, local copies, waits for them, and re-layouts: 1.96 us -> 0.04 us
    slice x2 -> x0, local copies, waits for them, and re-layouts: 1.69 us -> none  [the longest x1 0.85 us: local(): keys[:ROOT_ROWS]]
    concatenate x2 -> x0, other arithmetic: 1.44 us -> none  [local(): jnp.concatenate([keys[:ROOT_ROWS], values[:ROOT_ROWS], prefix_keys, prefi...]
    ppermute x1, waiting for transfers between devices: 5.41 us -> 4.61 us  [local(): part_two = lax.ppermute(own_part, 'servers', pairs[2])]
  transfers between devices with their start and end apart: 7 -> 7, of which waited for: 3 -> 2; matrix products, arithmetic and copies ran while one was open for 6% -> 0% of each run, Pallas kernels for 40% -> 41%
where the time goes in v2:
time: 34.2 us; the launch traced here: 34 us
  Pallas kernels  15.7 us (46%)
  starting transfers between devices  10.4 us (30%)
  waiting for transfers between devices  7.14 us (21%)
  between operations  0.78 us (2%)
    ppermute x1, waiting for transfers between devices, local(): part_two = lax.ppermute(own_part, 'servers', pairs[2])  4.61 us
    pallas_call x1, Pallas kernels, attend_call(): pl.pallas_call(body, in_specs=[SMEM] * 3 + [VMEM] * len(operands), out_sp...  4.36 us
    pallas_call x1, Pallas kernels, own_call(): pl.pallas_call(body, in_specs=[VMEM] * len(operands), out_specs=[ANY, VME...  4.3 us
    ppermute x1, starting transfers between devices, local(): part_one = lax.ppermute(own_part, 'servers', pairs[1])  3.09 us
    pallas_call x1, Pallas kernels, out_grad_call(): pl.pallas_call(out_grad_body, in_specs=[VMEM] * 3, out_specs=[VMEM] * 2,...  2.65 us
    ppermute x1, starting transfers between devices, local(): part_two = lax.ppermute(own_part, 'servers', pairs[2])  2.59 us
    pallas_call x1, Pallas kernels, far_call(): pl.pallas_call(far_body, in_specs=[SMEM] * 3 + [VMEM] * 6, out_specs=[VME...  2.57 us
    ppermute x1, waiting for transfers between devices, local(): back_two = lax.ppermute(send_two, 'servers', pairs[2])  2.52 us
  transfers between devices with their start and end apart: 7, of which 2 were waited for; matrix products, arithmetic and copies ran while one was open for 0% of the time, Pallas kernels for 41%

profile of v2, /device:TPU:0, one launch (start us, length us, event | category | flops | bytes accessed | tf_op | source)
XLA Modules:
  0.0 34.0 jit_solution(5894398316781409342)
XLA Ops:
  0.6 0.0 copy-start.2
  0.6 0.0 copy-start
  0.7 0.0 copy-start.1
  0.7 1.1 %pack.1 = (bf16[576,128]{1,0:T(8,128)(2,1)S(1)}, bf16[64,128]{1,0:T(8,128)(2,1)S(1)}) custom-call(bf16[512,128]{1,0:T(8,128)(2,1)} %refs_4_.1, bf16[512,128]{1,0:T(8,128)(2,1)} %refs_5_.3, bf16[32,128]{1,0:T(8,128)(2,1)} %prefix_key_ref.1, bf16[32,128]{1,0:T(8,128)(2,1)} %prefix_value_ref.1), custom_call_target="tpu_custom_call" | custom-call | flops 8589934592 | bytes 65536 | tf_op jit(solution)/shard_map/pack/pallas_call | solution.py:80
  1.8 3.1 %collective-permute-start.1 = (bf16[576,128]{1,0:T(8,128)(2,1)S(1)}, bf16[576,128]{1,0:T(8,128)(2,1)S(1)}, u32[]{:S(2)}, u32[]{:S(2)}) collective-permute-start(bf16[576,128]{1,0:T(8,128)(2,1)S(1)} %get-tuple-element.28.refs_7_), channel_id=1, source_target_pairs={{0,4},{4,0},{8,12},{12,8},{1,5},{5,1},{9,13},{13,9},{2,6},{6,2},{1... | collective-permute-start | bytes 442376 | tf_op jit(solution)/shard_map/ppermute | solution.py:490
  4.8 2.6 %collective-permute-start = (bf16[576,128]{1,0:T(8,128)(2,1)S(1)}, bf16[576,128]{1,0:T(8,128)(2,1)S(1)}, u32[]{:S(2)}, u32[]{:S(2)}) collective-permute-start(bf16[576,128]{1,0:T(8,128)(2,1)S(1)} %get-tuple-element.28.refs_7_), channel_id=1, source_target_pairs={{0,8},{4,12},{8,0},{12,4},{1,9},{5,13},{9,1},{13,5},{2,10},{6,14},... | collective-permute-start | bytes 442376 | tf_op jit(solution)/shard_map/ppermute | solution.py:489
  7.4 0.0 copy-start.3
  7.4 0.0 copy-start.6
  7.4 0.0 copy-start.7
  7.4 0.0 copy-start.8
  7.4 0.0 copy-start.9
  7.5 0.1 collective-permute-start.2
  7.5 0.0 copy-done.2
  7.5 0.0 copy-done
  7.6 0.0 copy-done.1
  7.6 2.7 %out_grad.1 = (bf16[512,1024]{1,0:T(8,128)(2,1)S(1)}, f32[8,512]{1,0:T(8,128)S(1)}) custom-call(bf16[512,2048]{1,0:T(8,128)(2,1)S(1)} %copy-done.1, bf16[2048,1024]{1,0:T(8,128)(2,1)S(1)} %copy-done, bf16[512,1024]{1,0:T(8,128)(2,1)S(1)} %copy-done.2), custom_call_target="tpu_custom_call" | custom-call | flops 6442450944 | bytes 65536 | tf_op jit(solution)/shard_map/out_grad/pallas_call | solution.py:111
  10.2 4.6 %collective-permute-done.refs_9_ = bf16[576,128]{1,0:T(8,128)(2,1)S(1)} collective-permute-done((bf16[576,128]{1,0:T(8,128)(2,1)S(1)}, bf16[576,128]{1,0:T(8,128)(2,1)S(1)}, u32[]{:S(2)}, u32[]{:S(2)}) %collective-permute-start) | collective-permute-done | bytes 147488 | tf_op jit(solution)/shard_map/ppermute | solution.py:489
  14.8 0.1 collective-permute-start.3
  14.9 0.0 collective-permute-done.2.refs_10_
  14.9 0.0 collective-permute-done.1.refs_8_
  14.9 0.0 copy-done.3
  14.9 0.0 copy-done.6
  14.9 0.0 copy-done.7
  14.9 0.0 copy-done.8
  14.9 0.0 copy-done.9
  14.9 4.4 %attend.1 = (bf16[4,2,128,256]{3,2,1,0:T(8,128)(2,1)S(1)}, bf16[4,2,384,256]{3,2,1,0:T(8,128)(2,1)S(1)}, bf16[4,384,128]{2,1,0:T(8,128)(2,1)S(1)}, f32[576,128]{...) custom-call(s32[64]{0:T(128)S(1)} %bitcast.1, ...), custom_call_target="tpu_custom_call" | custom-call | flops 5368709120 | bytes 65536 | tf_op jit(solution)/shard_map/attend/pallas_call | solution.py:292
  19.3 2.0 %collective-permute-start.4 = (bf16[576,128]{1,0:T(8,128)(2,1)S(1)}, bf16[576,128]{1,0:T(8,128)(2,1)S(1)}, u32[]{:S(2)}, u32[]{:S(2)}) collective-permute-start(bf16[576,128]{1,0:T(8,128)(2,1)S(1)} %get-tuple-element.42), channel_id=1, source_target_pairs={{0,4},{4,0},{8,12},{12,8},{1,5},{5,1},{9,13},{13,9},{2,6},{6,2},{1... | collective-permute-start | bytes 442376 | tf_op jit(solution)/shard_map/ppermute | solution.py:499
  21.3 1.1 %collective-permute-start.5 = (bf16[576,128]{1,0:T(8,128)(2,1)S(1)}, bf16[576,128]{1,0:T(8,128)(2,1)S(1)}, u32[]{:S(2)}, u32[]{:S(2)}) collective-permute-start(bf16[576,128]{1,0:T(8,128)(2,1)S(1)} %get-tuple-element.43), channel_id=1, source_target_pairs={{0,8},{4,12},{8,0},{12,4},{1,9},{5,13},{9,1},{13,5},{2,10},{6,14},... | collective-permute-start | bytes 442376 | tf_op jit(solution)/shard_map/ppermute | solution.py:498
  22.4 0.0 collective-permute-done.3.shard_ref.refs_10_
  22.4 0.0 copy-start.4
  22.4 0.0 copy-start.5
  22.4 2.6 %attend_far.1 = (bf16[576,128]{1,0:T(8,128)(2,1)S(1)}, bf16[4,2,256,256]{3,2,1,0:T(8,128)(2,1)S(1)}) custom-call(s32[64]{0:T(128)S(1)} %bitcast.2, s32[64]{0:T(128)S(1)} %copy-done.8, s32[64]{0:T(128)S(1)} %copy-done.9, bf16[512,1024]{1,0:T(8,128)(2,1)S(1)} %copy-done.3, bf16[512,1024]{1,0:T(8,128)(2,1)S(1)} %get-tuple-element.27.refs_4_.out_ref.refs_1_, ...), custom_call_target="tpu_custom_call" | custom-call | flops 3221225472 | bytes 65536 | tf_op jit(solution)/shard_map/attend_far/pallas_call | solution.py:351
  25.0 1.5 %collective-permute-start.6 = (bf16[576,128]{1,0:T(8,128)(2,1)S(1)}, bf16[576,128]{1,0:T(8,128)(2,1)S(1)}, u32[]{:S(2)}, u32[]{:S(2)}) collective-permute-start(bf16[576,128]{1,0:T(8,128)(2,1)S(1)} %get-tuple-element.44), channel_id=1, source_target_pairs={{0,12},{4,8},{8,4},{12,0},{1,13},{5,9},{9,5},{13,1},{2,14},{6,10},... | collective-permute-start | bytes 442376 | tf_op jit(solution)/shard_map/ppermute | solution.py:501
  26.4 0.0 copy-done.4
  26.4 0.0 copy-done.5
  26.4 4.3 %attend_own.1 = (bf16[512,1024]{1,0:T(8,128)(2,1)}, f32[512,128]{1,0:T(8,128)S(1)}, f32[512,128]{1,0:T(8,128)S(1)}) custom-call(bf16[512,1024]{1,0:T(8,128)(2,1)S(1)} %copy-done.3, bf16[512,1024]{1,0:T(8,128)(2,1)S(1)} %get-tuple-element.27.refs_4_.out_ref.refs_1_, f32[8,512]{1,0:T(8,128)S(1)} %copy-done.6, ...), custom_call_target="tpu_custom_call" | custom-call | flops 5368709120 | bytes 65536 | tf_op jit(solution)/shard_map/attend_own/pallas_call | solution.py:424
  30.7 0.0 collective-permute-done.4.refs_1_
  30.8 2.5 %collective-permute-done.5.refs_2_ = bf16[576,128]{1,0:T(8,128)(2,1)S(1)} collective-permute-done((bf16[576,128]{1,0:T(8,128)(2,1)S(1)}, bf16[576,128]{1,0:T(8,128)(2,1)S(1)}, u32[]{:S(2)}, u32[]{:S(2)}) %collective-permute-start.5) | collective-permute-done | bytes 147488 | tf_op jit(solution)/shard_map/ppermute | solution.py:498
  33.3 0.0 collective-permute-done.6.refs_3_
  33.3 0.8 %finish.1 = (bf16[512,128]{1,0:T(8,128)(2,1)}, bf16[512,128]{1,0:T(8,128)(2,1)}, bf16[32,128]{1,0:T(8,128)(2,1)}, bf16[32,128]{1,0:T(8,128)(2,1)}) custom-call(f32[512,128]{1,0:T(8,128)S(1)} %get-tuple-element.39.key_ref, f32[512,128]{1,0:T(8,128)S(1)} %get-tuple-element.40.value_ref, f32[576,128]{1,0:T(8,128)S(1)} %get-tuple-element.41.refs_0_, ...), custom_call_target="tpu_custom_call" | custom-call | flops 1073741824 | bytes 65536 | tf_op jit(solution)/shard_map/finish/pallas_call | solution.py:459
Async XLA Ops:
  0.6 6.9 %copy-start.2 = (bf16[512,1024]{1,0:T(8,128)(2,1)S(1)}, bf16[512,1024]{1,0:T(8,128)(2,1)}, u32[]{:S(2)}) copy-start(bf16[512,1024]{1,0:T(8,128)(2,1)} %attn_ref.1) | copy-start | bytes 3145732
  0.6 6.9 %copy-start = (bf16[2048,1024]{1,0:T(8,128)(2,1)S(1)}, bf16[2048,1024]{1,0:T(8,128)(2,1)}, u32[]{:S(2)}) copy-start(bf16[2048,1024]{1,0:T(8,128)(2,1)} %weight_ref.1) | copy-start | bytes 12582916
  0.7 6.9 %copy-start.1 = (bf16[512,2048]{1,0:T(8,128)(2,1)S(1)}, bf16[512,2048]{1,0:T(8,128)(2,1)}, u32[]{:S(2)}) copy-start(bf16[512,2048]{1,0:T(8,128)(2,1)} %grad_ref.1) | copy-start | bytes 6291460
  1.8 13.1 %collective-permute-start.1 = (bf16[576,128]{1,0:T(8,128)(2,1)S(1)}, bf16[576,128]{1,0:T(8,128)(2,1)S(1)}, u32[]{:S(2)}, u32[]{:S(2)}) collective-permute-start(bf16[576,128]{1,0:T(8,128)(2,1)S(1)} %get-tuple-element.28.refs_7_), channel_id=1, source_target_pairs={{0,4},{4,0},{8,12},{12,8},{1,5},{5,1},{9,13},{13,9},{2,6},{6,2},{1... | collective-permute-start | bytes 442376 | tf_op jit(solution)/shard_map/ppermute | solution.py:490
  4.8 10.0 %collective-permute-start = (bf16[576,128]{1,0:T(8,128)(2,1)S(1)}, bf16[576,128]{1,0:T(8,128)(2,1)S(1)}, u32[]{:S(2)}, u32[]{:S(2)}) collective-permute-start(bf16[576,128]{1,0:T(8,128)(2,1)S(1)} %get-tuple-element.28.refs_7_), channel_id=1, source_target_pairs={{0,8},{4,12},{8,0},{12,4},{1,9},{5,13},{9,1},{13,5},{2,10},{6,14},... | collective-permute-start | bytes 442376 | tf_op jit(solution)/shard_map/ppermute | solution.py:489
  7.4 7.5 %copy-start.3 = (bf16[512,1024]{1,0:T(8,128)(2,1)S(1)}, bf16[512,1024]{1,0:T(8,128)(2,1)}, u32[]{:S(2)}) copy-start(bf16[512,1024]{1,0:T(8,128)(2,1)} %refs_0_.1) | copy-start | bytes 3145732
  7.4 7.5 %copy-start.6 = (f32[8,512]{1,0:T(8,128)S(1)}, f32[8,512]{1,0:T(8,128)}, u32[]{:S(2)}) copy-start(f32[8,512]{1,0:T(8,128)} %refs_2_.3) | copy-start | bytes 49156
  7.4 7.5 %copy-start.7 = (s32[64,1]{0,1:T(1,128)S(1)}, s32[64,1]{0,1:T(1,128)}, u32[]{:S(2)}) copy-start(s32[64,1]{0,1:T(1,128)} %param.21) | copy-start | bytes 772
  7.4 7.5 %copy-start.8 = (s32[64]{0:T(128)S(1)}, s32[64]{0:T(128)}, u32[]{:S(2)}) copy-start(s32[64]{0:T(128)} %root_ref.1) | copy-start | bytes 772
  7.4 7.5 %copy-start.9 = (s32[64]{0:T(128)S(1)}, s32[64]{0:T(128)}, u32[]{:S(2)}) copy-start(s32[64]{0:T(128)} %limit_ref.1) | copy-start | bytes 772
  7.5 7.4 %collective-permute-start.2 = (bf16[64,128]{1,0:T(8,128)(2,1)S(1)}, bf16[64,128]{1,0:T(8,128)(2,1)S(1)}, u32[]{:S(2)}, u32[]{:S(2)}) collective-permute-start(bf16[64,128]{1,0:T(8,128)(2,1)S(1)} %get-tuple-element.32), channel_id=1, source_target_pairs={{0,12},{4,8},{8,4},{12,0},{1,13},{5,9},{9,5},{13,1},{2,14},{6,10},... | collective-permute-start | bytes 49160 | tf_op jit(solution)/shard_map/ppermute | solution.py:491
  14.8 7.6 %collective-permute-start.3 = (bf16[576,128]{1,0:T(8,128)(2,1)S(1)}, bf16[576,128]{1,0:T(8,128)(2,1)S(1)}, u32[]{:S(2)}, u32[]{:S(2)}) collective-permute-start(bf16[576,128]{1,0:T(8,128)(2,1)S(1)} %collective-permute-done.refs_9_), channel_id=1, source_target_pairs={{0,4},{4,0},{8,12},{12,8},{1,5},{5,1},{9,13},{13,9},{2,6},{6,2},{1... | collective-permute-start | bytes 442376 | tf_op jit(solution)/shard_map/ppermute | solution.py:494
  19.3 11.5 %collective-permute-start.4 = (bf16[576,128]{1,0:T(8,128)(2,1)S(1)}, bf16[576,128]{1,0:T(8,128)(2,1)S(1)}, u32[]{:S(2)}, u32[]{:S(2)}) collective-permute-start(bf16[576,128]{1,0:T(8,128)(2,1)S(1)} %get-tuple-element.42), channel_id=1, source_target_pairs={{0,4},{4,0},{8,12},{12,8},{1,5},{5,1},{9,13},{13,9},{2,6},{6,2},{1... | collective-permute-start | bytes 442376 | tf_op jit(solution)/shard_map/ppermute | solution.py:499
  21.3 11.9 %collective-permute-start.5 = (bf16[576,128]{1,0:T(8,128)(2,1)S(1)}, bf16[576,128]{1,0:T(8,128)(2,1)S(1)}, u32[]{:S(2)}, u32[]{:S(2)}) collective-permute-start(bf16[576,128]{1,0:T(8,128)(2,1)S(1)} %get-tuple-element.43), channel_id=1, source_target_pairs={{0,8},{4,12},{8,0},{12,4},{1,9},{5,13},{9,1},{13,5},{2,10},{6,14},... | collective-permute-start | bytes 442376 | tf_op jit(solution)/shard_map/ppermute | solution.py:498
  22.4 4.0 %copy-start.4 = (bf16[512,128]{1,0:T(8,128)(2,1)S(1)}, bf16[512,128]{1,0:T(8,128)(2,1)}, u32[]{:S(2)}) copy-start(bf16[512,128]{1,0:T(8,128)(2,1)} %refs_4_.1) | copy-start | bytes 393220
  22.4 4.0 %copy-start.5 = (bf16[512,128]{1,0:T(8,128)(2,1)S(1)}, bf16[512,128]{1,0:T(8,128)(2,1)}, u32[]{:S(2)}) copy-start(bf16[512,128]{1,0:T(8,128)(2,1)} %refs_5_.3) | copy-start | bytes 393220
  25.0 8.3 %collective-permute-start.6 = (bf16[576,128]{1,0:T(8,128)(2,1)S(1)}, bf16[576,128]{1,0:T(8,128)(2,1)S(1)}, u32[]{:S(2)}, u32[]{:S(2)}) collective-permute-start(bf16[576,128]{1,0:T(8,128)(2,1)S(1)} %get-tuple-element.44), channel_id=1, source_target_pairs={{0,12},{4,8},{8,4},{12,0},{1,13},{5,9},{9,5},{13,1},{2,14},{6,10},... | collective-permute-start | bytes 442376 | tf_op jit(solution)/shard_map/ppermute | solution.py:501

commit v3 on v0

v3 whole, which is shorter than its diff:
```python
import math

import jax
import jax.numpy as jnp
from jax import lax
from jax.experimental import pallas as pl
from jax.experimental.pallas import tpu as pltpu
from jax.sharding import PartitionSpec as P

HD = 128
CH_DEV = 16
ROOTS_DEV = 4
RLEN = 64
CLEN = 16
ROOT_ROWS = ROOTS_DEV * RLEN
BLOCK = 64
UNIT = 256
UNIT_HEADS = UNIT // BLOCK
PAIR = 2
SCALE = HD ** (-0.5)
LOG2E = math.log2(math.e)
NT = (((1,), (1,)), ((), ()))
NN = (((1,), (0,)), ((), ()))
TN = (((0,), (0,)), ((), ()))
F32 = jnp.float32
BF16 = jnp.bfloat16
VMEM = pl.BlockSpec(memory_space=pltpu.VMEM)
SMEM = pl.BlockSpec(memory_space=pltpu.SMEM)
ANY = pl.BlockSpec(memory_space=pl.ANY)


def params(mib):
    return pltpu.CompilerParams(vmem_limit_bytes=mib * 1024 * 1024)


COSTS = {
    "pack": 8,
    "repeat": 8,
    "out_grad": 6,
    "attend_near": 3,
    "attend_parent": 3,
    "attend_prompt": 0.1,
    "attend_far": 0.1,
    "attend_own": 0.1,
    "query_grads": 1,
    "finish": 0.1,
}


def cost(name):
    micros = COSTS[name]
    return pl.CostEstimate(flops=int(micros * (1 << 30)), transcendentals=0, bytes_accessed=1 << 16)


def pinned(array):
    return pltpu.with_memory_space_constraint(array, pltpu.VMEM)


def unmoved(array):
    return pltpu.with_memory_space_constraint(array, pltpu.HBM)


def pinned_scalars(array):
    return pltpu.with_memory_space_constraint(array, pltpu.SMEM)


def kept(shape, dtype):
    return pltpu.VMEM(shape, dtype)


def dot(left, right, numbers):
    return lax.dot_general(left, right, numbers, preferred_element_type=F32)


def pack_body(key_ref, value_ref, prefix_key_ref, prefix_value_ref, part_ref, sems):
    own = prefix_key_ref.shape[0]
    at = 2 * ROOT_ROWS
    copies = [
        (key_ref.at[0:ROOT_ROWS], part_ref.at[0:ROOT_ROWS]),
        (value_ref.at[0:ROOT_ROWS], part_ref.at[ROOT_ROWS:at]),
        (prefix_key_ref, part_ref.at[at : at + own]),
        (prefix_value_ref, part_ref.at[at + own : at + 2 * own]),
    ]
    started = [pltpu.make_async_copy(a, b, sems.at[i]) for i, (a, b) in enumerate(copies)]
    for copy in started:
        copy.start()
    for copy in started:
        copy.wait()


def pack_call(keys, values, prefix_keys, prefix_values):
    own = prefix_keys.shape[0]
    return pl.pallas_call(
        pack_body,
        in_specs=[ANY] * 4,
        out_specs=VMEM,
        out_shape=kept((2 * ROOT_ROWS + 2 * own, HD), BF16),
        scratch_shapes=[pltpu.SemaphoreType.DMA((4,))],
        compiler_params=params(4),
        cost_estimate=cost("pack"),
        name="pack",
    )(*(unmoved(x) for x in (keys, values, prefix_keys, prefix_values)))


def repeat_body(part_ref, part_out, prompt_out):
    part_out[...] = part_ref[...]
    prompt_out[...] = part_ref[2 * ROOT_ROWS :]


def repeat_call(part):
    return pl.pallas_call(
        repeat_body,
        in_specs=[VMEM],
        out_specs=[VMEM] * 2,
        out_shape=[kept(part.shape, BF16), kept((part.shape[0] - 2 * ROOT_ROWS, HD), BF16)],
        compiler_params=params(4),
        cost_estimate=cost("repeat"),
        name="repeat",
    )(pinned(part))


def unit_rows(array):
    heads, tokens = array.shape
    rows = []
    for start in range(0, ROOT_ROWS, BLOCK):
        for first in range(0, heads, UNIT_HEADS):
            picked = range(first, first + UNIT_HEADS)
            rows.append([array[head : head + 1, start : start + BLOCK] for head in picked])
    for start in range(ROOT_ROWS, tokens, PAIR * CLEN):
        starts = range(start, start + PAIR * CLEN, CLEN)
        rows.append([array[head : head + 1, at : at + CLEN] for at in starts for head in range(heads)])
    return [jnp.concatenate(row, axis=1) for row in rows]


def out_grad_body(
    grad_ref, weight_ref, attn_ref, lse_ref, owner_ref, root_ref, offset_ref, out_ref, lse_out, delta_out, forks_out
):
    rows, cols = out_ref.shape
    width = 2 * HD
    lane = lax.broadcasted_iota(jnp.int32, (rows, HD), 1)
    columns = jnp.zeros((rows, HD), F32)
    start = lax.axis_index("servers") * CH_DEV
    for child in range(CH_DEV):
        at = start + child
        forks_out[child] = (owner_ref[at] * ROOTS_DEV + root_ref[at]) * (2 * RLEN) + offset_ref[at]
    for unit, row in enumerate(unit_rows(lse_ref[...] * LOG2E)):
        lse_out[unit : unit + 1] = row
    for step in range(cols // width):
        part = slice(step * width, (step + 1) * width)
        wide = jnp.dot(grad_ref[...], weight_ref[:, part], preferred_element_type=F32).astype(BF16)
        out_ref[:, part] = wide
        products = wide.astype(F32) * attn_ref[:, part].astype(F32)
        for head in range(width // HD):
            total = jnp.sum(products[:, head * HD : (head + 1) * HD], axis=1, keepdims=True)
            columns = jnp.where(lane == step * (width // HD) + head, total, columns)
    for unit, row in enumerate(unit_rows(jnp.transpose(columns)[: cols // HD])):
        delta_out[unit : unit + 1] = row


def out_grad_call(grad_out, out_weight, attn_out, lse, *forks):
    rows = grad_out.shape[0]
    cols = out_weight.shape[1]
    units = rows * (cols // HD) // UNIT
    return pl.pallas_call(
        out_grad_body,
        in_specs=[VMEM] * 4 + [SMEM] * 3,
        out_specs=[VMEM] * 3 + [SMEM],
        out_shape=[
            kept((rows, cols), BF16),
            kept((units, UNIT), F32),
            kept((units, UNIT), F32),
            pltpu.SMEM((CH_DEV,), jnp.int32),
        ],
        compiler_params=params(12),
        cost_estimate=cost("out_grad"),
        name="out_grad",
    )(*(pinned(x) for x in (grad_out, out_weight, attn_out, lse)), *forks)


def unit_counts(tokens, heads):
    roots = ROOT_ROWS * heads // UNIT
    return roots, roots + (tokens - ROOT_ROWS) * heads // UNIT


def unit_tiles(tokens, heads, unit):
    roots, _ = unit_counts(tokens, heads)
    if unit < roots:
        block, part = divmod(unit, heads // UNIT_HEADS)
        picked = range(part * UNIT_HEADS, (part + 1) * UNIT_HEADS)
        return [(block * BLOCK, BLOCK, head) for head in picked]
    return [tile for k in range(PAIR) for tile in child_tiles(heads, (unit - roots) * PAIR + k)]


def child_tiles(heads, child):
    return [(ROOT_ROWS + child * CLEN, CLEN, head) for head in range(heads)]


def tiled(ref, tiles):
    return jnp.concatenate(
        [ref[start : start + rows, head * HD : (head + 1) * HD] for start, rows, head in tiles], axis=0
    )


def swept(jobs, load, parts, mask, keep, ahead=1):
    ready = []
    for job in [*jobs, *[None] * ahead]:
        if job is not None:
            query, out, lse, delta = load(job)
            keys, values = parts(job)
            ready.append((job, query, out, lse, delta, dot(keys, query, NT), dot(values, out, NT)))
        if job is not None and len(ready) <= ahead:
            continue
        done, query, out, lse, delta, scores, weight_grads = ready.pop(0)
        weights = mask(done, jnp.exp2(scores * (SCALE * LOG2E) - lse))
        score_grads = (weights * (weight_grads - delta)).astype(BF16)
        keep(done, dot(score_grads, query, NN), dot(weights.astype(BF16), out, NN), score_grads)


def unit_loader(q_ref, out_ref, lse_ref, delta_ref):
    tokens, heads = q_ref.shape[0], q_ref.shape[1] // HD

    def load(unit):
        tiles = unit_tiles(tokens, heads, unit)
        row = slice(unit, unit + 1)
        return tiled(q_ref, tiles), tiled(out_ref, tiles), lse_ref[row], delta_ref[row]

    return load


def child_loader(q_ref, out_ref, lse_ref, delta_ref):
    tokens, heads = q_ref.shape[0], q_ref.shape[1] // HD
    roots, _ = unit_counts(tokens, heads)

    def load(child):
        tiles = child_tiles(heads, child)
        unit, place = roots + child // PAIR, child % PAIR * heads * CLEN
        row, lanes = slice(unit, unit + 1), slice(place, place + heads * CLEN)
        return tiled(q_ref, tiles), tiled(out_ref, tiles), lse_ref[row, lanes], delta_ref[row, lanes]

    return load


def prompt_body(piece_rows, is_part, q_ref, out_ref, lse_ref, delta_ref, *refs):
    value_ref = refs[-1]
    if is_part:
        *pieces, ds_ref, key_ref, sums_ref, two_ref = refs[:-1]
    else:
        *pieces, ds_ref, key_ref, sums_ref = refs[:-1]
    own = piece_rows // 2
    count = 0
    for piece in pieces:
        first = 2 * ROOT_ROWS if is_part and piece.shape[0] > piece_rows else 0
        for at in range(first, piece.shape[0], piece_rows):
            key_ref[count : count + own] = piece[at : at + own]
            value_ref[count : count + own] = piece[at + own : at + piece_rows]
            count += own
    sums = [jnp.zeros((count, HD), F32), jnp.zeros((count, HD), F32)]

    def keep(unit, key_grad, value_grad, score_grads):
        ds_ref[unit] = score_grads
        sums[0] = sums[0] + key_grad
        sums[1] = sums[1] + value_grad

    swept(
        range(ds_ref.shape[0]),
        unit_loader(q_ref, out_ref, lse_ref, delta_ref),
        lambda unit: (key_ref[...], value_ref[...]),
        lambda unit, weights: weights,
        keep,
    )

    def store(ref, at, index):
        rows = slice(index * own, (index + 1) * own)
        ref[at : at + own] = (sums[0][rows] * SCALE).astype(ref.dtype)
        ref[at + own : at + piece_rows] = sums[1][rows].astype(ref.dtype)

    for index in range(count // own):
        store(sums_ref, index * piece_rows, index)
    if is_part:
        store(two_ref, 0, 2)


def prompt_call(shared, pieces, piece_rows, is_part):
    count = lax.axis_size("servers") * piece_rows // 2
    units = shared[2].shape[0]
    operands = [*shared, *pieces]
    shapes = [
        kept((units, count, UNIT), BF16),
        kept((count, HD), BF16),
        kept((2 * count, HD), F32),
    ]
    if is_part:
        shapes.append(kept((piece_rows, HD), BF16))

    def body(*refs):
        prompt_body(piece_rows, is_part, *refs)

    return pl.pallas_call(
        body,
        in_specs=[VMEM] * len(operands),
        out_specs=[VMEM] * len(shapes),
        out_shape=shapes,
        scratch_shapes=[pltpu.VMEM((count, HD), BF16)],
        compiler_params=params(12 if is_part else 20),
        cost_estimate=cost("attend_prompt"),
        name="attend_prompt",
    )(*(pinned(x) for x in operands))


def parent_body(held, has_prompt, fork_ref, q_ref, out_ref, lse_ref, delta_ref, *refs):
    is_part = held is not None
    count = len(held) if is_part else 1
    shards, refs = refs[:count], refs[count:]
    if has_prompt:
        prompt_ref, refs = refs[0], refs[1:]
    ds_ref, key_ref, *sum_refs = refs[:-2]
    grads_ref, sums_ref = refs[-2:]
    heads = q_ref.shape[1] // HD
    part = 2 * ROOT_ROWS
    my_index = lax.axis_index("servers")
    bases, limits = {}, {}

    def parts(child):
        fork = fork_ref[child]
        limit = fork & (2 * RLEN - 1)
        row = pl.multiple_of(((fork >> 7) & (ROOTS_DEV - 1)) * RLEN, RLEN)
        owner = fork >> 9
        if is_part:
            slot = owner ^ my_index
            is_last = slot == held[1]
            bases[child] = pl.multiple_of(jnp.where(is_last, part, 0) + row, RLEN)
            limits[child] = jnp.where(is_last | (slot == held[0]), limit, 0)
            at = row + ROOT_ROWS
            keys = jnp.where(is_last, shards[1][pl.ds(row, RLEN)], shards[0][pl.ds(row, RLEN)])
            values = jnp.where(is_last, shards[1][pl.ds(at, RLEN)], shards[0][pl.ds(at, RLEN)])
        else:
            bases[child] = pl.multiple_of(owner * part + row, RLEN)
            limits[child] = limit
            keys = shards[0][pl.ds(bases[child], RLEN)]
            values = shards[0][pl.ds(bases[child] + ROOT_ROWS, RLEN)]
        key_ref[child] = keys
        return keys, values

    key_index = lax.broadcasted_iota(jnp.int32, (RLEN, heads * CLEN), 0)

    def keep(child, key_grad, value_grad, score_grads):
        ds_ref[child] = score_grads
        grads_ref[child, 0:RLEN] = key_grad * SCALE
        grads_ref[child, RLEN:] = value_grad

    swept(
        range(CH_DEV),
        child_loader(q_ref, out_ref, lse_ref, delta_ref),
        parts,
        lambda child, weights: jnp.where(key_index < limits[child], weights, 0.0),
        keep,
        2,
    )
    sums_ref[...] = jnp.zeros(sums_ref.shape, F32)
    for child in range(CH_DEV):
        base = bases[child]
        sums_ref[pl.ds(base, RLEN)] = sums_ref[pl.ds(base, RLEN)] + grads_ref[child, 0:RLEN]
        base = base + ROOT_ROWS
        sums_ref[pl.ds(base, RLEN)] = sums_ref[pl.ds(base, RLEN)] + grads_ref[child, RLEN:]
    for index, ref in enumerate(sum_refs):
        first = index * part
        size = part if is_part else ref.shape[0]
        ref[0:size] = sums_ref[first : first + size].astype(ref.dtype)
        if is_part and ref.shape[0] > part:
            rows = ref.shape[0] - part
            first = held[index] * rows
            ref[part:] = prompt_ref[first : first + rows].astype(ref.dtype)


def parent_call(forks, shared, shards, held=None, sums=(), prompt_sums=None, name="attend_parent"):
    is_part = held is not None
    rows = 2 * ROOT_ROWS * len(shards) if is_part else shards[0].shape[0]
    columns = shared[0].shape[1] // HD * CLEN
    shapes = [kept((CH_DEV, RLEN, columns), BF16), kept((CH_DEV, RLEN, HD), BF16)]
    operands = [*shared, *shards]
    if is_part:
        shapes += sums
        if prompt_sums is not None:
            operands.append(prompt_sums)
    else:
        shapes.append(jax.ShapeDtypeStruct((rows, HD), F32))

    def body(*refs):
        parent_body(held, prompt_sums is not None, *refs)

    return pl.pallas_call(
        body,
        in_specs=[SMEM] + [VMEM] * len(operands),
        out_specs=[VMEM] * len(shapes),
        out_shape=shapes,
        scratch_shapes=[
            pltpu.VMEM((CH_DEV, 2 * RLEN, HD), F32),
            pltpu.VMEM((rows, HD), F32),
        ],
        compiler_params=params(8 if is_part else 40),
        cost_estimate=cost(name),
        name=name,
    )(pinned_scalars(forks), *(pinned(x) for x in operands))


def own_rows(tokens, heads, unit):
    roots, _ = unit_counts(tokens, heads)
    if unit < roots:
        start = unit // (heads // UNIT_HEADS) * BLOCK
        return slice(start, start + BLOCK)
    start = ROOT_ROWS + (unit - roots) * PAIR * CLEN
    return slice(start, start + PAIR * CLEN)


def own_body(q_ref, out_ref, lse_ref, delta_ref, key_ref, value_ref, root_ds_ref, child_ds_ref, keys_out, values_out):
    tokens, heads = q_ref.shape[0], q_ref.shape[1] // HD
    roots, units = unit_counts(tokens, heads)
    per_block = heads // UNIT_HEADS
    key_index = lax.broadcasted_iota(jnp.int32, (BLOCK, UNIT), 0)
    column = lax.broadcasted_iota(jnp.int32, (BLOCK, UNIT), 1)
    root_allowed = key_index <= column % BLOCK
    key_index, column = key_index[: PAIR * CLEN], column[: PAIR * CLEN]
    child_allowed = (key_index // CLEN == column // (heads * CLEN)) & (key_index % CLEN <= column % CLEN)
    totals = [None, None]

    def parts(unit):
        rows = own_rows(tokens, heads, unit)
        return key_ref[rows], value_ref[rows]

    def keep(unit, key_grad, value_grad, score_grads):
        rows = own_rows(tokens, heads, unit)
        if unit >= roots:
            child_ds_ref[unit - roots] = score_grads
            keys_out[rows] = key_grad * SCALE
            values_out[rows] = value_grad
            return
        root_ds_ref[unit] = score_grads
        totals[0] = key_grad if unit % per_block == 0 else totals[0] + key_grad
        totals[1] = value_grad if unit % per_block == 0 else totals[1] + value_grad
        if unit % per_block == per_block - 1:
            keys_out[rows] = totals[0] * SCALE
            values_out[rows] = totals[1]

    swept(
        range(units),
        unit_loader(q_ref, out_ref, lse_ref, delta_ref),
        parts,
        lambda unit, weights: jnp.where(root_allowed if unit < roots else child_allowed, weights, 0.0),
        keep,
    )


def own_call(shared, keys, values):
    tokens, width = shared[0].shape
    roots, units = unit_counts(tokens, width // HD)
    return pl.pallas_call(
        own_body,
        in_specs=[VMEM] * 6,
        out_specs=[VMEM] * 4,
        out_shape=[
            kept((roots, BLOCK, UNIT), BF16),
            kept((units - roots, PAIR * CLEN, UNIT), BF16),
            kept((tokens, HD), F32),
            kept((tokens, HD), F32),
        ],
        compiler_params=params(8),
        cost_estimate=cost("attend_own"),
        name="attend_own",
    )(*(pinned(x) for x in (*shared, keys, values)))


def query_body(has_back, key_ref, root_ds_ref, child_ds_ref, prompt_ref, prompt_ds_ref, *refs):
    if has_back:
        *parent_refs, sums_ref, back_ref, gq_ref, total_ref, gq_vmem, sems = refs
        total_ref[...] = sums_ref[...] + back_ref[...].astype(F32)
    else:
        *parent_refs, gq_ref, gq_vmem, sems = refs
    tokens, heads = gq_vmem.shape[0], gq_vmem.shape[1] // HD
    roots, units = unit_counts(tokens, heads)
    copies = []

    def store(tiles, total):
        at = 0
        for start, rows, head in tiles:
            piece = total[at : at + rows] * SCALE
            gq_vmem[start : start + rows, head * HD : (head + 1) * HD] = piece.astype(BF16)
            at += rows

    for unit in range(units):
        tiles = unit_tiles(tokens, heads, unit)
        own_ds = root_ds_ref[unit] if unit < roots else child_ds_ref[unit - roots]
        grads = jnp.concatenate([own_ds, prompt_ds_ref[unit]], axis=0)
        total = dot(grads, jnp.concatenate([key_ref[own_rows(tokens, heads, unit)], prompt_ref[...]], axis=0), TN)
        if unit < roots:
            store(tiles, total)
        else:
            columns = heads * CLEN
            for k in range(PAIR):
                child = (unit - roots) * PAIR + k
                grads = jnp.concatenate([ref[child] for ref in parent_refs[1::2]], axis=0)
                keys = jnp.concatenate([ref[child] for ref in parent_refs[0::2]], axis=0)
                store(child_tiles(heads, child), total[k * columns : (k + 1) * columns] + dot(grads, keys, TN))
        done = tiles[-1][0] + tiles[-1][1]
        first = len(copies) * BLOCK
        if done >= first + BLOCK and (unit + 1 >= roots or (unit + 1) % (heads // UNIT_HEADS) == 0):
            rows = slice(first, first + BLOCK)
            copy = pltpu.make_async_copy(gq_vmem.at[rows], gq_ref.at[rows], sems.at[len(copies)])
            copy.start()
            copies.append(copy)
    for copy in copies:
        copy.wait()


def query_call(tokens, width, operands, back=()):
    shapes = [jax.ShapeDtypeStruct((tokens, width), BF16), *(kept(x.shape, F32) for x in back[:1])]
    operands = [*operands, *back]

    def body(*refs):
        query_body(bool(back), *refs)

    return pl.pallas_call(
        body,
        in_specs=[VMEM] * len(operands),
        out_specs=[ANY, *[VMEM] * (len(shapes) - 1)],
        out_shape=shapes,
        scratch_shapes=[pltpu.VMEM((tokens, width), BF16), pltpu.SemaphoreType.DMA((tokens // BLOCK,))],
        compiler_params=params(12),
        cost_estimate=cost("query_grads"),
        name="query_grads",
    )(*(pinned(x) for x in operands))


def finish_body(key_ref, value_ref, *refs):
    parts = refs[:-4]
    keys_out, values_out, prefix_keys_out, prefix_values_out = refs[-4:]
    own = prefix_keys_out.shape[0]
    part = 2 * ROOT_ROWS
    total, prompt = [], []
    for ref in parts:
        rows = ref.shape[0]
        if rows >= part:
            total.append(ref[0:part].astype(F32))
        if rows != part:
            first = rows - 2 * own if rows > part else 0
            prompt.append(ref[first : first + 2 * own].astype(F32))
    total, prompt = sum(total[1:], total[0]), sum(prompt[1:], prompt[0])
    keys_out[0:ROOT_ROWS] = (key_ref[0:ROOT_ROWS] + total[0:ROOT_ROWS]).astype(BF16)
    keys_out[ROOT_ROWS:] = key_ref[ROOT_ROWS:].astype(BF16)
    values_out[0:ROOT_ROWS] = (value_ref[0:ROOT_ROWS] + total[ROOT_ROWS:]).astype(BF16)
    values_out[ROOT_ROWS:] = value_ref[ROOT_ROWS:].astype(BF16)
    prefix_keys_out[...] = prompt[0:own].astype(BF16)
    prefix_values_out[...] = prompt[own:].astype(BF16)


def finish_call(key_sums, value_sums, parts, own):
    shapes = [jax.ShapeDtypeStruct(key_sums.shape, BF16)] * 2 + [jax.ShapeDtypeStruct((own, HD), BF16)] * 2
    return pl.pallas_call(
        finish_body,
        in_specs=[VMEM] * (2 + len(parts)),
        out_specs=[VMEM] * 4,
        out_shape=shapes,
        compiler_params=params(8),
        cost_estimate=cost("finish"),
        name="finish",
    )(*(pinned(x) for x in (key_sums, value_sums, *parts)))


def local(
    grad_out,
    out_weight,
    queries,
    attn_out,
    lse,
    keys,
    values,
    prefix_keys,
    prefix_values,
    fork_owner,
    fork_root,
    fork_offset,
):
    own_part = pack_call(keys, values, prefix_keys, prefix_values)
    forks = [fork_owner.reshape(-1), fork_root, fork_offset]
    own = prefix_keys.shape[0]
    if lax.axis_size("servers") == 4:
        pairs = [[(i, i ^ d) for i in range(4)] for d in range(4)]
        part_two = lax.ppermute(own_part, "servers", pairs[2])
        later_part, later_prompt = repeat_call(own_part)
        prompt_far = lax.ppermute(later_prompt, "servers", pairs[3])
        part_one = lax.ppermute(later_part, "servers", pairs[1])
        out_grad, lse_rows, delta, forks = out_grad_call(grad_out, out_weight, attn_out, lse, *forks)
        part_two, delta = lax.optimization_barrier((part_two, delta))
        part_far = lax.ppermute(part_two, "servers", pairs[1])
        delta, prompt_far = lax.optimization_barrier((delta, prompt_far))
        part, whole = (2 * ROOT_ROWS, HD), (2 * ROOT_ROWS + 2 * own, HD)
        near_ds, near_keys, own_sums, send_two = parent_call(
            forks,
            (queries, out_grad, lse_rows, delta),
            [own_part, part_two],
            (0, 2),
            [kept(part, F32), kept(part, BF16)],
            None,
            "attend_near",
        )
        back_two = lax.ppermute(send_two, "servers", pairs[2])
        delta, own_sums = lax.optimization_barrier((delta, own_sums))
        prompt_ds, prompt_keys, prompt_sums, send_two_prompt = prompt_call(
            (queries, out_grad, lse_rows, delta), [own_part, part_one, part_two, prompt_far], 2 * own, True
        )
        far_ds, far_keys, send_far, send_one = parent_call(
            forks,
            (queries, out_grad, lse_rows, delta),
            [part_far, part_one],
            (3, 1),
            [kept(whole, BF16), kept(whole, BF16)],
            prompt_sums,
            "attend_far",
        )
        back_far = lax.ppermute(send_far, "servers", pairs[3])
        back_one = lax.ppermute(send_one, "servers", pairs[1])
        back_two_prompt = lax.ppermute(send_two_prompt, "servers", pairs[2])
        delta, far_ds = lax.optimization_barrier((delta, far_ds))
        shared = (queries, out_grad, lse_rows, delta)
        parents = (near_keys, near_ds, far_keys, far_ds)
        back = (own_sums, back_two)
        parts = [prompt_sums, back_far, back_one, back_two_prompt]
    else:
        count = lax.axis_size("servers")
        all_parts = lax.all_gather(own_part, "servers", axis=0, tiled=False)
        part = 2 * ROOT_ROWS
        all_roots = all_parts[:, :part].reshape(-1, HD)
        all_prompts = all_parts[:, part:].reshape(-1, HD)
        out_grad, lse_rows, delta, forks = out_grad_call(grad_out, out_weight, attn_out, lse, *forks)
        shared = (queries, out_grad, lse_rows, delta)
        prompt_ds, prompt_keys, prompt_sums = prompt_call(shared, [all_prompts], 2 * own, False)
        parent_ds, parent_keys, root_sums = parent_call(forks, shared, [all_roots])
        parents = (parent_keys, parent_ds)
        sends = jnp.concatenate(
            [root_sums.reshape(count, part, HD), prompt_sums.reshape(count, 2 * own, HD)], axis=1
        ).reshape(-1, HD)
        back = ()
        parts = [lax.psum_scatter(sends, "servers", scatter_dimension=0, tiled=True)]
    root_ds, child_ds, key_sums, value_sums = own_call(shared, keys, values)
    operands = (keys, root_ds, child_ds, prompt_keys, prompt_ds, *parents)
    grad_queries, *totals = query_call(*queries.shape, operands, back)
    parts = totals + parts
    grads = finish_call(key_sums, value_sums, parts, own)
    return (grad_queries, *grads)


def solution(mesh):
    placed = (
        P(("groups", "servers"), None),
        P(None, "heads"),
        P(("groups", "servers"), "heads"),
        P(("groups", "servers"), "heads"),
        P("heads", ("groups", "servers")),
        P(("groups", "servers"), "heads"),
        P(("groups", "servers"), "heads"),
        P(("groups", "servers"), "heads"),
        P(("groups", "servers"), "heads"),
        P("groups", None),
        P("groups"),
        P("groups"),
    )
    return jax.shard_map(
        local,
        mesh=mesh,
        in_specs=placed,
        out_specs=(P(("groups", "servers"), "heads"),) * 5,
        check_vma=False,
    )
```

time: 284 us -> 32.9 us (0.12)
  matrix products: 106 us -> 0 us
  blocking collectives: 56.1 us -> 0 us
  other arithmetic: 51.8 us -> 0 us
  local copies, waits for them, and re-layouts: 45.9 us -> 0.06 us
  starting transfers between devices: 0.16 us -> 14.3 us
  between operations: 14 us -> 0.82 us
  Pallas kernels: 0 us -> 12.8 us
  loops' own time: 6.92 us -> 0 us
  waiting for transfers between devices: 0.77 us -> 4.73 us
    dot_general x51 -> x0, matrix products: 106 us -> none  [the longest x10 24.4 us: block_step(): lax.dot_general(weights_low, out_flat, across, preferred_element_type=jnp...]
    all_gather x4 -> x0, blocking collectives: 56.1 us -> none  [the longest x1 14.8 us: local(): lax.all_gather(prefix_keys, 'servers', axis=0, tiled=True)]
    select_n x7 -> x0, other arithmetic: 22 us -> none  [the longest x2 20.1 us: parent_rows(): child_limit = jnp.take(my_offsets, child_ids, axis=0)]
    unnamed x39 -> x20, local copies, waits for them, and re-layouts: 15.8 us -> 0.06 us
    ppermute x0 -> x8, starting transfers between devices: none -> 14.3 us  [the longest x1 4.1 us: local(): part_two = lax.ppermute(own_part, 'servers', pairs[2])]
    scatter-add x2 -> x0, other arithmetic: 13.5 us -> none  [the longest x1 6.83 us: local(): dense_keys = jnp.zeros((all_roots[0].shape[0], shared_width), jnp.float32...]
    pallas_call x0 -> x9, Pallas kernels: none -> 12.8 us  [the longest x1 3.38 us: out_grad_call(): pl.pallas_call(out_grad_body, in_specs=[VMEM] * 4 + [SMEM] * 3, out_specs...]
    gather x4 -> x0, local copies, waits for them, and re-layouts: 10.1 us -> none  [the longest x1 4.33 us: local(): jnp.take(all_roots[1], flat_index, axis=0)]
  transfers between devices with their start and end apart: 4 -> 8, of which waited for: 0 -> 3; matrix products, arithmetic and copies ran while one was open for 53% -> 0% of each run, Pallas kernels for 0% -> 34%
where the time goes in v3:
time: 32.9 us; the launch traced here: 32.8 us
  starting transfers between devices  14.3 us (43%)
  Pallas kernels  12.8 us (39%)
  waiting for transfers between devices  4.73 us (14%)
  between operations  0.82 us (2%)
    ppermute x1, starting transfers between devices, local(): part_two = lax.ppermute(own_part, 'servers', pairs[2])  4.1 us
    pallas_call x1, Pallas kernels, out_grad_call(): pl.pallas_call(out_grad_body, in_specs=[VMEM] * 4 + [SMEM] * 3, out_specs...  3.38 us
    ppermute x1, starting transfers between devices, local(): back_two = lax.ppermute(send_two, 'servers', pairs[2])  3.19 us
    pallas_call x2, Pallas kernels, parent_call(): pl.pallas_call(body, in_specs=[SMEM] + [VMEM] * len(operands), out_specs=...  2.69 us
    ppermute x1, starting transfers between devices, local(): back_far = lax.ppermute(send_far, 'servers', pairs[3])  2.64 us
    ppermute x1, waiting for transfers between devices, local(): part_two = lax.ppermute(own_part, 'servers', pairs[2])  2.41 us
    ppermute x1, waiting for transfers between devices, local(): back_two_prompt = lax.ppermute(send_two_prompt, 'servers', pairs[2])  2.13 us
    pallas_call x1, Pallas kernels, prompt_call(): pl.pallas_call(body, in_specs=[VMEM] * len(operands), out_specs=[VMEM] *...  1.73 us
  transfers between devices with their start and end apart: 8, of which 3 were waited for; matrix products, arithmetic and copies ran while one was open for 0% of the time, Pallas kernels for 34%

profile of v3, /device:TPU:0, one launch (start us, length us, event | category | flops | bytes accessed | tf_op | source)
XLA Modules:
  0.0 32.8 jit_solution(11025830438050031070)
XLA Ops:
  0.6 0.9 %pack.1.part_ref.refs_5_.refs_4_ = bf16[576,128]{1,0:T(8,128)(2,1)S(1)} custom-call(bf16[512,128]{1,0:T(8,128)(2,1)} %refs_0_.3, bf16[512,128]{1,0:T(8,128)(2,1)} %value_ref.3, bf16[32,128]{1,0:T(8,128)(2,1)} %prefix_key_ref.1, bf16[32,128]{1,0:T(8,128)(2,1)} %prefix_value_ref.1), custom_call_target="tpu_custom_call" | custom-call | flops 8589934592 | bytes 65536 | tf_op jit(solution)/shard_map/pack/pallas_call | solution.py:93
  1.6 0.0 copy-start.3
  1.6 0.0 copy-start.4
  1.6 0.0 copy-start.5
  1.6 0.0 copy-start.6
  1.6 0.0 copy-start.7
  1.6 0.0 copy-start.8
  1.6 0.0 copy-start.9
  1.6 4.1 %collective-permute-start = (bf16[576,128]{1,0:T(8,128)(2,1)S(1)}, bf16[576,128]{1,0:T(8,128)(2,1)S(1)}, u32[]{:S(2)}, u32[]{:S(2)}) collective-permute-start(bf16[576,128]{1,0:T(8,128)(2,1)S(1)} %pack.1.part_ref.refs_5_.refs_4_), channel_id=1, source_target_pairs={{0,8},{4,12},{8,0},{12,4},{1,9},{5,13},{9,1},{13,5},{2,10},{6,14},... | collective-permute-start | bytes 442376 | tf_op jit(solution)/shard_map/ppermute | solution.py:587
  5.8 1.4 %collective-permute-start.1 = (bf16[64,128]{1,0:T(8,128)(2,1)S(1)}, bf16[64,128]{1,0:T(8,128)(2,1)S(1)}, u32[]{:S(2)}, u32[]{:S(2)}) collective-permute-start(bf16[64,128]{1,0:T(8,128)(2,1)S(1)} %get-tuple-element.45), channel_id=1, source_target_pairs={{0,12},{4,8},{8,4},{12,0},{1,13},{5,9},{9,5},{13,1},{2,14},{6,10},... | collective-permute-start | bytes 49160 | tf_op jit(solution)/shard_map/ppermute | solution.py:589
  7.2 0.3 collective-permute-start.3
  7.5 0.0 copy-done.3
  7.5 0.0 copy-done.4
  7.5 0.0 copy-done.5
  7.5 0.0 copy-done.6
  7.5 0.0 copy-done.7
  7.5 0.0 copy-done.8
  7.5 0.0 copy-done.9
  7.5 0.0 copy-start
  7.5 3.4 %out_grad.1 = (bf16[512,1024]{1,0:T(8,128)(2,1)S(1)}, f32[16,256]{1,0:T(8,128)S(1)}, f32[16,256]{1,0:T(8,128)S(1)}, s32[16]{0:T(128)S(4)}) custom-call(bf16[512,2048]{1,0:T(8,128)(2,1)S(1)} %copy-done.4, bf16[2048,1024]{1,0:T(8,128)(2,1)S(1)} %copy-done.3, bf16[512,1024]{1,0:T(8,128)(2,1)S(1)} %copy-done.5, f32[8,512]{1,0:T(8,128)S(1)} %copy-done.6, ...), custom_call_target="tpu_custom_call" | custom-call | flops 6442450944 | bytes 65536 | tf_op jit(solution)/shard_map/out_grad/pallas_call | solution.py:164
  10.9 2.4 %collective-permute-done.refs_6_ = bf16[576,128]{1,0:T(8,128)(2,1)S(1)} collective-permute-done((bf16[576,128]{1,0:T(8,128)(2,1)S(1)}, bf16[576,128]{1,0:T(8,128)(2,1)S(1)}, u32[]{:S(2)}, u32[]{:S(2)}) %collective-permute-start) | collective-permute-done | bytes 147488 | tf_op jit(solution)/shard_map/ppermute | solution.py:587
  13.3 0.0 collective-permute-done.1.refs_7_
  13.3 0.9 %collective-permute-start.2 = (bf16[576,128]{1,0:T(8,128)(2,1)S(1)}, bf16[576,128]{1,0:T(8,128)(2,1)S(1)}, u32[]{:S(2)}, u32[]{:S(2)}) collective-permute-start(bf16[576,128]{1,0:T(8,128)(2,1)S(1)} %collective-permute-done.refs_6_), channel_id=1, source_target_pairs={{0,4},{4,0},{8,12},{12,8},{1,5},{5,1},{9,13},{13,9},{2,6},{6,2},{1... | collective-permute-start | bytes 442376 | tf_op jit(solution)/shard_map/ppermute | solution.py:593
  14.2 0.0 copy-done
  14.2 1.3 %attend_near.1 = (bf16[16,64,128]{2,1,0:T(8,128)(2,1)S(1)}, bf16[16,64,128]{2,1,0:T(8,128)(2,1)S(1)}, f32[512,128]{1,0:T(8,128)S(1)}, bf16[512,128]{1,0:T(8,128)(2,1)S(1)}) custom-call(s32[16]{0:T(128)S(4)} %get-tuple-element.47.refs_0_, bf16[512,1024]{1,0:T(8,128)(2,1)S(1)} %copy-done, bf16[512,1024]{1,0:T(8,128)(2,1)S(1)} %get-tuple-element.41.refs_2_.refs_1_.out_ref, ...), custom_call_target="tpu_custom_call" | custom-call | flops 3221225472 | bytes 65536 | tf_op jit(solution)/shard_map/attend_near/pallas_call | solution.py:391
  15.6 0.0 copy-start.1
  15.6 0.0 copy-start.2
  15.6 3.2 %collective-permute-start.4 = (bf16[512,128]{1,0:T(8,128)(2,1)S(1)}, bf16[512,128]{1,0:T(8,128)(2,1)S(1)}, u32[]{:S(2)}, u32[]{:S(2)}) collective-permute-start(bf16[512,128]{1,0:T(8,128)(2,1)S(1)} %get-tuple-element.65), channel_id=1, source_target_pairs={{0,8},{4,12},{8,0},{12,4},{1,9},{5,13},{9,1},{13,5},{2,10},{6,14},... | collective-permute-start | bytes 393224 | tf_op jit(solution)/shard_map/ppermute | solution.py:605
  18.8 0.0 collective-permute-done.3.refs_5_.refs_6_
  18.8 1.7 %attend_prompt.1 = (bf16[16,128,256]{2,1,0:T(8,128)(2,1)S(1)}, bf16[128,128]{1,0:T(8,128)(2,1)S(1)}, f32[256,128]{1,0:T(8,128)S(1)}, bf16[64,128]{1,0:T(8,128)(2,1)S(1)}) custom-call(bf16[512,1024]{1,0:T(8,128)(2,1)S(1)} %copy-done, bf16[512,1024]{1,0:T(8,128)(2,1)S(1)} %get-tuple-element.41.refs_2_.refs_1_.out_ref, ...), custom_call_target="tpu_custom_call" | custom-call | flops 107374184 | bytes 65536 | tf_op jit(solution)/shard_map/attend_prompt/pallas_call | solution.py:298
  20.5 0.0 collective-permute-done.2.refs_5_
  20.5 1.4 %attend_far.1 = (bf16[16,64,128]{2,1,0:T(8,128)(2,1)S(1)}, bf16[16,64,128]{2,1,0:T(8,128)(2,1)S(1)}, bf16[576,128]{1,0:T(8,128)(2,1)S(1)}, bf16[576,128]{1,0:T(8,128)(2,1)S(1)}) custom-call(s32[16]{0:T(128)S(4)} %get-tuple-element.47.refs_0_, bf16[512,1024]{1,0:T(8,128)(2,1)S(1)} %copy-done, bf16[512,1024]{1,0:T(8,128)(2,1)S(1)} %get-tuple-element.41.refs_2_.refs_1_.out_ref, ...), custom_call_target="tpu_custom_call" | custom-call | flops 107374184 | bytes 65536 | tf_op jit(solution)/shard_map/attend_far/pallas_call | solution.py:391
  21.9 2.6 %collective-permute-start.5 = (bf16[576,128]{1,0:T(8,128)(2,1)S(1)}, bf16[576,128]{1,0:T(8,128)(2,1)S(1)}, u32[]{:S(2)}, u32[]{:S(2)}) collective-permute-start(bf16[576,128]{1,0:T(8,128)(2,1)S(1)} %get-tuple-element.70), channel_id=1, source_target_pairs={{0,12},{4,8},{8,4},{12,0},{1,13},{5,9},{9,5},{13,1},{2,14},{6,10},... | collective-permute-start | bytes 442376 | tf_op jit(solution)/shard_map/ppermute | solution.py:619
  24.5 0.3 collective-permute-start.6
  24.8 1.5 %collective-permute-start.7 = (bf16[64,128]{1,0:T(8,128)(2,1)S(1)}, bf16[64,128]{1,0:T(8,128)(2,1)S(1)}, u32[]{:S(2)}, u32[]{:S(2)}) collective-permute-start(bf16[64,128]{1,0:T(8,128)(2,1)S(1)} %get-tuple-element.72), channel_id=1, source_target_pairs={{0,8},{4,12},{8,0},{12,4},{1,9},{5,13},{9,1},{13,5},{2,10},{6,14},... | collective-permute-start | bytes 49160 | tf_op jit(solution)/shard_map/ppermute | solution.py:621
  26.3 0.0 copy-done.1
  26.3 0.0 copy-done.2
  26.3 1.7 %attend_own.1 = (bf16[8,64,256]{2,1,0:T(8,128)(2,1)S(1)}, bf16[8,32,256]{2,1,0:T(8,128)(2,1)S(1)}, f32[512,128]{1,0:T(8,128)S(1)}, f32[512,128]{1,0:T(8,128)S(1)}) custom-call(bf16[512,1024]{1,0:T(8,128)(2,1)S(1)} %copy-done, bf16[512,1024]{1,0:T(8,128)(2,1)S(1)} %get-tuple-element.41.refs_2_.refs_1_.out_ref, ...), custom_call_target="tpu_custom_call" | custom-call | flops 107374184 | bytes 65536 | tf_op jit(solution)/shard_map/attend_own/pallas_call | solution.py:456
  28.0 0.0 collective-permute-done.4.refs_10_
  28.1 1.7 %query_grads.1 = (bf16[512,1024]{1,0:T(8,128)(2,1)}, f32[512,128]{1,0:T(8,128)S(1)}) custom-call(bf16[512,128]{1,0:T(8,128)(2,1)S(1)} %copy-done.2, bf16[8,64,256]{2,1,0:T(8,128)(2,1)S(1)} %get-tuple-element.56.refs_1_, bf16[8,32,256]{2,1,0:T(8,128)(2,1)S(1)} %get-tuple-element.57.refs_2_, bf16[128,128]{1,0:T(8,128)(2,1)S(1)} %get-tuple-element.58.refs_3_, ...), custom_call_target="tpu_custom_call" | custom-call | flops 1073741824 | bytes 65536 | tf_op jit(solution)/shard_map/query_grads/pallas_call | solution.py:521
  29.7 2.1 %collective-permute-done.7.refs_4_ = bf16[64,128]{1,0:T(8,128)(2,1)S(1)} collective-permute-done((bf16[64,128]{1,0:T(8,128)(2,1)S(1)}, bf16[64,128]{1,0:T(8,128)(2,1)S(1)}, u32[]{:S(2)}, u32[]{:S(2)}) %collective-permute-start.7) | collective-permute-done | bytes 16416 | tf_op jit(solution)/shard_map/ppermute | solution.py:621
  31.8 0.0 collective-permute-done.5.refs_2_
  31.8 0.2 collective-permute-done.6.refs_3_
  32.0 0.7 %finish.1 = (bf16[512,128]{1,0:T(8,128)(2,1)}, bf16[512,128]{1,0:T(8,128)(2,1)}, bf16[32,128]{1,0:T(8,128)(2,1)}, bf16[32,128]{1,0:T(8,128)(2,1)}) custom-call(f32[512,128]{1,0:T(8,128)S(1)} %get-tuple-element.67.key_ref, f32[512,128]{1,0:T(8,128)S(1)} %get-tuple-element.68.value_ref, f32[512,128]{1,0:T(8,128)S(1)} %get-tuple-element.69.refs_0_, ...), custom_call_target="tpu_custom_call" | custom-call | flops 107374184 | bytes 65536 | tf_op jit(solution)/shard_map/finish/pallas_call | solution.py:557
  (1 shorter events, 0.0 us)
Async XLA Ops:
  1.6 5.9 %copy-start.3 = (bf16[2048,1024]{1,0:T(8,128)(2,1)S(1)}, bf16[2048,1024]{1,0:T(8,128)(2,1)}, u32[]{:S(2)}) copy-start(bf16[2048,1024]{1,0:T(8,128)(2,1)} %weight_ref.1) | copy-start | bytes 12582916
  1.6 5.9 %copy-start.4 = (bf16[512,2048]{1,0:T(8,128)(2,1)S(1)}, bf16[512,2048]{1,0:T(8,128)(2,1)}, u32[]{:S(2)}) copy-start(bf16[512,2048]{1,0:T(8,128)(2,1)} %grad_ref.1) | copy-start | bytes 6291460
  1.6 5.9 %copy-start.5 = (bf16[512,1024]{1,0:T(8,128)(2,1)S(1)}, bf16[512,1024]{1,0:T(8,128)(2,1)}, u32[]{:S(2)}) copy-start(bf16[512,1024]{1,0:T(8,128)(2,1)} %attn_ref.1) | copy-start | bytes 3145732
  1.6 5.9 %copy-start.6 = (f32[8,512]{1,0:T(8,128)S(1)}, f32[8,512]{1,0:T(8,128)}, u32[]{:S(2)}) copy-start(f32[8,512]{1,0:T(8,128)} %lse_ref.1) | copy-start | bytes 49156
  1.6 5.9 %copy-start.7 = (s32[64,1]{0,1:T(1,128)S(1)}, s32[64,1]{0,1:T(1,128)}, u32[]{:S(2)}) copy-start(s32[64,1]{0,1:T(1,128)} %param.21) | copy-start | bytes 772
  1.6 5.9 %copy-start.8 = (s32[64]{0:T(128)S(1)}, s32[64]{0:T(128)}, u32[]{:S(2)}) copy-start(s32[64]{0:T(128)} %root_ref.1) | copy-start | bytes 772
  1.6 5.9 %copy-start.9 = (s32[64]{0:T(128)S(1)}, s32[64]{0:T(128)}, u32[]{:S(2)}) copy-start(s32[64]{0:T(128)} %offset_ref.1) | copy-start | bytes 772
  1.6 11.7 %collective-permute-start = (bf16[576,128]{1,0:T(8,128)(2,1)S(1)}, bf16[576,128]{1,0:T(8,128)(2,1)S(1)}, u32[]{:S(2)}, u32[]{:S(2)}) collective-permute-start(bf16[576,128]{1,0:T(8,128)(2,1)S(1)} %pack.1.part_ref.refs_5_.refs_4_), channel_id=1, source_target_pairs={{0,8},{4,12},{8,0},{12,4},{1,9},{5,13},{9,1},{13,5},{2,10},{6,14},... | collective-permute-start | bytes 442376 | tf_op jit(solution)/shard_map/ppermute | solution.py:587
  5.8 7.6 %collective-permute-start.1 = (bf16[64,128]{1,0:T(8,128)(2,1)S(1)}, bf16[64,128]{1,0:T(8,128)(2,1)S(1)}, u32[]{:S(2)}, u32[]{:S(2)}) collective-permute-start(bf16[64,128]{1,0:T(8,128)(2,1)S(1)} %get-tuple-element.45), channel_id=1, source_target_pairs={{0,12},{4,8},{8,4},{12,0},{1,13},{5,9},{9,5},{13,1},{2,14},{6,10},... | collective-permute-start | bytes 49160 | tf_op jit(solution)/shard_map/ppermute | solution.py:589
  7.2 11.6 %collective-permute-start.3 = (bf16[576,128]{1,0:T(8,128)(2,1)S(1)}, bf16[576,128]{1,0:T(8,128)(2,1)S(1)}, u32[]{:S(2)}, u32[]{:S(2)}) collective-permute-start(bf16[576,128]{1,0:T(8,128)(2,1)S(1)} %get-tuple-element.51), channel_id=1, source_target_pairs={{0,4},{4,0},{8,12},{12,8},{1,5},{5,1},{9,13},{13,9},{2,6},{6,2},{1... | collective-permute-start | bytes 442376 | tf_op jit(solution)/shard_map/ppermute | solution.py:590
  7.5 6.7 %copy-start = (bf16[512,1024]{1,0:T(8,128)(2,1)S(1)}, bf16[512,1024]{1,0:T(8,128)(2,1)}, u32[]{:S(2)}) copy-start(bf16[512,1024]{1,0:T(8,128)(2,1)} %q_ref.1) | copy-start | bytes 3145732
  13.3 7.2 %collective-permute-start.2 = (bf16[576,128]{1,0:T(8,128)(2,1)S(1)}, bf16[576,128]{1,0:T(8,128)(2,1)S(1)}, u32[]{:S(2)}, u32[]{:S(2)}) collective-permute-start(bf16[576,128]{1,0:T(8,128)(2,1)S(1)} %collective-permute-done.refs_6_), channel_id=1, source_target_pairs={{0,4},{4,0},{8,12},{12,8},{1,5},{5,1},{9,13},{13,9},{2,6},{6,2},{1... | collective-permute-start | bytes 442376 | tf_op jit(solution)/shard_map/ppermute | solution.py:593
  15.6 10.8 %copy-start.1 = (bf16[512,128]{1,0:T(8,128)(2,1)S(1)}, bf16[512,128]{1,0:T(8,128)(2,1)}, u32[]{:S(2)}) copy-start(bf16[512,128]{1,0:T(8,128)(2,1)} %value_ref.3) | copy-start | bytes 393220
  15.6 10.8 %copy-start.2 = (bf16[512,128]{1,0:T(8,128)(2,1)S(1)}, bf16[512,128]{1,0:T(8,128)(2,1)}, u32[]{:S(2)}) copy-start(bf16[512,128]{1,0:T(8,128)(2,1)} %refs_0_.3) | copy-start | bytes 393220
  15.6 12.5 %collective-permute-start.4 = (bf16[512,128]{1,0:T(8,128)(2,1)S(1)}, bf16[512,128]{1,0:T(8,128)(2,1)S(1)}, u32[]{:S(2)}, u32[]{:S(2)}) collective-permute-start(bf16[512,128]{1,0:T(8,128)(2,1)S(1)} %get-tuple-element.65), channel_id=1, source_target_pairs={{0,8},{4,12},{8,0},{12,4},{1,9},{5,13},{9,1},{13,5},{2,10},{6,14},... | collective-permute-start | bytes 393224 | tf_op jit(solution)/shard_map/ppermute | solution.py:605
  21.9 10.0 %collective-permute-start.5 = (bf16[576,128]{1,0:T(8,128)(2,1)S(1)}, bf16[576,128]{1,0:T(8,128)(2,1)S(1)}, u32[]{:S(2)}, u32[]{:S(2)}) collective-permute-start(bf16[576,128]{1,0:T(8,128)(2,1)S(1)} %get-tuple-element.70), channel_id=1, source_target_pairs={{0,12},{4,8},{8,4},{12,0},{1,13},{5,9},{9,5},{13,1},{2,14},{6,10},... | collective-permute-start | bytes 442376 | tf_op jit(solution)/shard_map/ppermute | solution.py:619
  24.5 7.5 %collective-permute-start.6 = (bf16[576,128]{1,0:T(8,128)(2,1)S(1)}, bf16[576,128]{1,0:T(8,128)(2,1)S(1)}, u32[]{:S(2)}, u32[]{:S(2)}) collective-permute-start(bf16[576,128]{1,0:T(8,128)(2,1)S(1)} %get-tuple-element.71), channel_id=1, source_target_pairs={{0,4},{4,0},{8,12},{12,8},{1,5},{5,1},{9,13},{13,9},{2,6},{6,2},{1... | collective-permute-start | bytes 442376 | tf_op jit(solution)/shard_map/ppermute | solution.py:620
  24.8 7.0 %collective-permute-start.7 = (bf16[64,128]{1,0:T(8,128)(2,1)S(1)}, bf16[64,128]{1,0:T(8,128)(2,1)S(1)}, u32[]{:S(2)}, u32[]{:S(2)}) collective-permute-start(bf16[64,128]{1,0:T(8,128)(2,1)S(1)} %get-tuple-element.72), channel_id=1, source_target_pairs={{0,8},{4,12},{8,0},{12,4},{1,9},{5,13},{9,1},{13,5},{2,10},{6,14},... | collective-permute-start | bytes 49160 | tf_op jit(solution)/shard_map/ppermute | solution.py:621

commit v4 on v3

--- a/solution.py
+++ b/solution.py
@@ -42,8 +42,8 @@
     "attend_prompt": 0.1,
     "attend_far": 0.1,
     "attend_own": 0.1,
-    "query_grads": 1,
-    "finish": 0.1,
+    "query_grads": 0.3,
+    "finish": 0.01,
 }
 
 
@@ -277,7 +277,7 @@
     for index in range(count // own):
         store(sums_ref, index * piece_rows, index)
     if is_part:
-        store(two_ref, 0, 2)
+        store(two_ref, 0, 3)
 
 
 def prompt_call(shared, pieces, piece_rows, is_part):
@@ -584,41 +584,40 @@
     own = prefix_keys.shape[0]
     if lax.axis_size("servers") == 4:
         pairs = [[(i, i ^ d) for i in range(4)] for d in range(4)]
-        part_two = lax.ppermute(own_part, "servers", pairs[2])
+        part_two = lax.ppermute(own_part, "servers", pairs[3])
         later_part, later_prompt = repeat_call(own_part)
-        prompt_far = lax.ppermute(later_prompt, "servers", pairs[3])
+        prompt_far = lax.ppermute(later_prompt, "servers", pairs[2])
         part_one = lax.ppermute(later_part, "servers", pairs[1])
         out_grad, lse_rows, delta, forks = out_grad_call(grad_out, out_weight, attn_out, lse, *forks)
         part_two, delta = lax.optimization_barrier((part_two, delta))
         part_far = lax.ppermute(part_two, "servers", pairs[1])
-        delta, prompt_far = lax.optimization_barrier((delta, prompt_far))
         part, whole = (2 * ROOT_ROWS, HD), (2 * ROOT_ROWS + 2 * own, HD)
         near_ds, near_keys, own_sums, send_two = parent_call(
             forks,
             (queries, out_grad, lse_rows, delta),
             [own_part, part_two],
-            (0, 2),
+            (0, 3),
             [kept(part, F32), kept(part, BF16)],
             None,
             "attend_near",
         )
-        back_two = lax.ppermute(send_two, "servers", pairs[2])
+        back_two = lax.ppermute(send_two, "servers", pairs[3])
         delta, own_sums = lax.optimization_barrier((delta, own_sums))
         prompt_ds, prompt_keys, prompt_sums, send_two_prompt = prompt_call(
-            (queries, out_grad, lse_rows, delta), [own_part, part_one, part_two, prompt_far], 2 * own, True
+            (queries, out_grad, lse_rows, delta), [own_part, part_one, prompt_far, part_two], 2 * own, True
         )
         far_ds, far_keys, send_far, send_one = parent_call(
             forks,
             (queries, out_grad, lse_rows, delta),
             [part_far, part_one],
-            (3, 1),
+            (2, 1),
             [kept(whole, BF16), kept(whole, BF16)],
             prompt_sums,
             "attend_far",
         )
-        back_far = lax.ppermute(send_far, "servers", pairs[3])
+        back_far = lax.ppermute(send_far, "servers", pairs[2])
         back_one = lax.ppermute(send_one, "servers", pairs[1])
-        back_two_prompt = lax.ppermute(send_two_prompt, "servers", pairs[2])
+        back_two_prompt = lax.ppermute(send_two_prompt, "servers", pairs[3])
         delta, far_ds = lax.optimization_barrier((delta, far_ds))
         shared = (queries, out_grad, lse_rows, delta)
         parents = (near_keys, near_ds, far_keys, far_ds)

time: 32.9 us -> 30.8 us (0.936)
  waiting for transfers between devices: 4.73 us -> 1.14 us
  starting transfers between devices: 14.3 us -> 15.8 us
    ppermute x5, waiting for transfers between devices: 4.55 us -> 1.13 us  [the longest x1 0.97 us: local(): back_two_prompt = lax.ppermute(send_two_prompt, 'servers', pairs[3])]
    ppermute x1, starting transfers between devices: 0.88 us -> 2.99 us  [local(): part_far = lax.ppermute(part_two, 'servers', pairs[1])]
    ppermute x5, starting transfers between devices: 12.9 us -> 10.8 us  [the longest x1 5.11 us: local(): part_two = lax.ppermute(own_part, 'servers', pairs[3])]
    ppermute x1, starting transfers between devices: 0.3 us -> 1.44 us  [local(): back_one = lax.ppermute(send_one, 'servers', pairs[1])]
  transfers between devices with their start and end apart: 8 -> 8, of which waited for: 3 -> 2; matrix products, arithmetic and copies ran while one was open for 0% -> 0% of each run, Pallas kernels for 34% -> 36%
where the time goes in v4:
time: 30.8 us; the launch traced here: 30.6 us
  starting transfers between devices  15.8 us (51%)
  Pallas kernels  12.8 us (42%)
  waiting for transfers between devices  1.14 us (4%)
  between operations  0.83 us (3%)
    ppermute x1, starting transfers between devices, local(): part_two = lax.ppermute(own_part, 'servers', pairs[3])  5.11 us
    pallas_call x1, Pallas kernels, out_grad_call(): pl.pallas_call(out_grad_body, in_specs=[VMEM] * 4 + [SMEM] * 3, out_specs...  3.38 us
    ppermute x1, starting transfers between devices, local(): part_far = lax.ppermute(part_two, 'servers', pairs[1])  2.99 us
    pallas_call x2, Pallas kernels, parent_call(): pl.pallas_call(body, in_specs=[SMEM] + [VMEM] * len(operands), out_specs=...  2.69 us
    ppermute x1, starting transfers between devices, local(): back_two = lax.ppermute(send_two, 'servers', pairs[3])  2.58 us
    pallas_call x1, Pallas kernels, prompt_call(): pl.pallas_call(body, in_specs=[VMEM] * len(operands), out_specs=[VMEM] *...  1.74 us
    ppermute x1, starting transfers between devices, local(): back_far = lax.ppermute(send_far, 'servers', pairs[2])  1.72 us
    pallas_call x1, Pallas kernels, own_call(): pl.pallas_call(own_body, in_specs=[VMEM] * 6, out_specs=[VMEM] * 4, out_s...  1.69 us
  transfers between devices with their start and end apart: 8, of which 2 were waited for; matrix products, arithmetic and copies ran while one was open for 0% of the time, Pallas kernels for 36%

profile of v4, /device:TPU:0, one launch (start us, length us, event | category | flops | bytes accessed | tf_op | source)
XLA Modules:
  0.0 30.6 jit_solution(17471567008615767150)
XLA Ops:
  0.6 0.9 %pack.1.refs_5_.part_ref.refs_4_ = bf16[576,128]{1,0:T(8,128)(2,1)S(1)} custom-call(bf16[512,128]{1,0:T(8,128)(2,1)} %refs_0_.3, bf16[512,128]{1,0:T(8,128)(2,1)} %value_ref.3, bf16[32,128]{1,0:T(8,128)(2,1)} %prefix_key_ref.1, bf16[32,128]{1,0:T(8,128)(2,1)} %prefix_value_ref.1), custom_call_target="tpu_custom_call" | custom-call | flops 8589934592 | bytes 65536 | tf_op jit(solution)/shard_map/pack/pallas_call | solution.py:93
  1.6 0.0 copy-start.3
  1.6 0.0 copy-start.4
  1.6 0.0 copy-start.5
  1.6 0.0 copy-start.6
  1.6 0.0 copy-start.7
  1.6 0.0 copy-start.8
  1.6 0.0 copy-start.9
  1.6 5.1 %collective-permute-start = (bf16[576,128]{1,0:T(8,128)(2,1)S(1)}, bf16[576,128]{1,0:T(8,128)(2,1)S(1)}, u32[]{:S(2)}, u32[]{:S(2)}) collective-permute-start(bf16[576,128]{1,0:T(8,128)(2,1)S(1)} %pack.1.refs_5_.part_ref.refs_4_), channel_id=1, source_target_pairs={{0,12},{4,8},{8,4},{12,0},{1,13},{5,9},{9,5},{13,1},{2,14},{6,10},... | collective-permute-start | bytes 442376 | tf_op jit(solution)/shard_map/ppermute | solution.py:587
  6.8 0.1 collective-permute-start.3
  6.8 0.6 %collective-permute-start.2 = (bf16[576,128]{1,0:T(8,128)(2,1)S(1)}, bf16[576,128]{1,0:T(8,128)(2,1)S(1)}, u32[]{:S(2)}, u32[]{:S(2)}) collective-permute-start(bf16[576,128]{1,0:T(8,128)(2,1)S(1)} %get-tuple-element.47), channel_id=1, source_target_pairs={{0,4},{4,0},{8,12},{12,8},{1,5},{5,1},{9,13},{13,9},{2,6},{6,2},{1... | collective-permute-start | bytes 442376 | tf_op jit(solution)/shard_map/ppermute | solution.py:590
  7.4 0.0 copy-done.3
  7.4 0.0 copy-done.4
  7.4 0.0 copy-done.5
  7.4 0.0 copy-done.6
  7.4 0.0 copy-done.7
  7.4 0.0 copy-done.8
  7.5 0.0 copy-done.9
  7.5 0.0 copy-start
  7.5 3.4 %out_grad.1 = (bf16[512,1024]{1,0:T(8,128)(2,1)S(1)}, f32[16,256]{1,0:T(8,128)S(1)}, f32[16,256]{1,0:T(8,128)S(1)}, s32[16]{0:T(128)S(4)}) custom-call(bf16[512,2048]{1,0:T(8,128)(2,1)S(1)} %copy-done.4, bf16[2048,1024]{1,0:T(8,128)(2,1)S(1)} %copy-done.3, bf16[512,1024]{1,0:T(8,128)(2,1)S(1)} %copy-done.5, f32[8,512]{1,0:T(8,128)S(1)} %copy-done.6, ...), custom_call_target="tpu_custom_call" | custom-call | flops 6442450944 | bytes 65536 | tf_op jit(solution)/shard_map/out_grad/pallas_call | solution.py:164
  10.9 0.2 collective-permute-done.refs_6_.refs_7_
  11.0 3.0 %collective-permute-start.1 = (bf16[576,128]{1,0:T(8,128)(2,1)S(1)}, bf16[576,128]{1,0:T(8,128)(2,1)S(1)}, u32[]{:S(2)}, u32[]{:S(2)}) collective-permute-start(bf16[576,128]{1,0:T(8,128)(2,1)S(1)} %collective-permute-done.refs_6_.refs_7_), channel_id=1, source_target_pairs={{0,4},{4,0},{8,12},{12,8},{1,5},{5,1},{9,13},{13,9},{2,6},{6,2},{1... | collective-permute-start | bytes 442376 | tf_op jit(solution)/shard_map/ppermute | solution.py:593
  14.0 0.0 copy-done
  14.0 1.3 %attend_near.1 = (bf16[16,64,128]{2,1,0:T(8,128)(2,1)S(1)}, bf16[16,64,128]{2,1,0:T(8,128)(2,1)S(1)}, f32[512,128]{1,0:T(8,128)S(1)}, bf16[512,128]{1,0:T(8,128)(2,1)S(1)}) custom-call(s32[16]{0:T(128)S(4)} %get-tuple-element.43.refs_0_, bf16[512,1024]{1,0:T(8,128)(2,1)S(1)} %copy-done, bf16[512,1024]{1,0:T(8,128)(2,1)S(1)} %get-tuple-element.39.refs_2_.refs_1_.out_ref, ...), custom_call_target="tpu_custom_call" | custom-call | flops 3221225472 | bytes 65536 | tf_op jit(solution)/shard_map/attend_near/pallas_call | solution.py:391
  15.3 0.0 copy-start.1
  15.4 0.0 copy-start.2
  15.4 2.6 %collective-permute-start.4 = (bf16[512,128]{1,0:T(8,128)(2,1)S(1)}, bf16[512,128]{1,0:T(8,128)(2,1)S(1)}, u32[]{:S(2)}, u32[]{:S(2)}) collective-permute-start(bf16[512,128]{1,0:T(8,128)(2,1)S(1)} %get-tuple-element.61), channel_id=1, source_target_pairs={{0,12},{4,8},{8,4},{12,0},{1,13},{5,9},{9,5},{13,1},{2,14},{6,10},... | collective-permute-start | bytes 393224 | tf_op jit(solution)/shard_map/ppermute | solution.py:604
  17.9 0.0 collective-permute-done.3.refs_6_
  17.9 0.0 collective-permute-done.2.refs_5_.refs_6_
  18.0 1.7 %attend_prompt.1 = (bf16[16,128,256]{2,1,0:T(8,128)(2,1)S(1)}, bf16[128,128]{1,0:T(8,128)(2,1)S(1)}, f32[256,128]{1,0:T(8,128)S(1)}, bf16[64,128]{1,0:T(8,128)(2,1)S(1)}) custom-call(bf16[512,1024]{1,0:T(8,128)(2,1)S(1)} %copy-done, bf16[512,1024]{1,0:T(8,128)(2,1)S(1)} %get-tuple-element.39.refs_2_.refs_1_.out_ref, ...), custom_call_target="tpu_custom_call" | custom-call | flops 107374184 | bytes 65536 | tf_op jit(solution)/shard_map/attend_prompt/pallas_call | solution.py:298
  19.7 0.0 collective-permute-done.1.refs_5_
  19.7 1.4 %attend_far.1 = (bf16[16,64,128]{2,1,0:T(8,128)(2,1)S(1)}, bf16[16,64,128]{2,1,0:T(8,128)(2,1)S(1)}, bf16[576,128]{1,0:T(8,128)(2,1)S(1)}, bf16[576,128]{1,0:T(8,128)(2,1)S(1)}) custom-call(s32[16]{0:T(128)S(4)} %get-tuple-element.43.refs_0_, bf16[512,1024]{1,0:T(8,128)(2,1)S(1)} %copy-done, bf16[512,1024]{1,0:T(8,128)(2,1)S(1)} %get-tuple-element.39.refs_2_.refs_1_.out_ref, ...), custom_call_target="tpu_custom_call" | custom-call | flops 107374184 | bytes 65536 | tf_op jit(solution)/shard_map/attend_far/pallas_call | solution.py:391
  21.1 1.7 %collective-permute-start.5 = (bf16[576,128]{1,0:T(8,128)(2,1)S(1)}, bf16[576,128]{1,0:T(8,128)(2,1)S(1)}, u32[]{:S(2)}, u32[]{:S(2)}) collective-permute-start(bf16[576,128]{1,0:T(8,128)(2,1)S(1)} %get-tuple-element.66), channel_id=1, source_target_pairs={{0,8},{4,12},{8,0},{12,4},{1,9},{5,13},{9,1},{13,5},{2,10},{6,14},... | collective-permute-start | bytes 442376 | tf_op jit(solution)/shard_map/ppermute | solution.py:618
  22.8 1.4 %collective-permute-start.6 = (bf16[576,128]{1,0:T(8,128)(2,1)S(1)}, bf16[576,128]{1,0:T(8,128)(2,1)S(1)}, u32[]{:S(2)}, u32[]{:S(2)}) collective-permute-start(bf16[576,128]{1,0:T(8,128)(2,1)S(1)} %get-tuple-element.67), channel_id=1, source_target_pairs={{0,4},{4,0},{8,12},{12,8},{1,5},{5,1},{9,13},{13,9},{2,6},{6,2},{1... | collective-permute-start | bytes 442376 | tf_op jit(solution)/shard_map/ppermute | solution.py:619
  24.2 1.3 %collective-permute-start.7 = (bf16[64,128]{1,0:T(8,128)(2,1)S(1)}, bf16[64,128]{1,0:T(8,128)(2,1)S(1)}, u32[]{:S(2)}, u32[]{:S(2)}) collective-permute-start(bf16[64,128]{1,0:T(8,128)(2,1)S(1)} %get-tuple-element.68), channel_id=1, source_target_pairs={{0,12},{4,8},{8,4},{12,0},{1,13},{5,9},{9,5},{13,1},{2,14},{6,10},... | collective-permute-start | bytes 49160 | tf_op jit(solution)/shard_map/ppermute | solution.py:620
  25.5 0.0 copy-done.1
  25.5 0.0 copy-done.2
  25.5 1.7 %attend_own.1 = (bf16[8,64,256]{2,1,0:T(8,128)(2,1)S(1)}, bf16[8,32,256]{2,1,0:T(8,128)(2,1)S(1)}, f32[512,128]{1,0:T(8,128)S(1)}, f32[512,128]{1,0:T(8,128)S(1)}) custom-call(bf16[512,1024]{1,0:T(8,128)(2,1)S(1)} %copy-done, bf16[512,1024]{1,0:T(8,128)(2,1)S(1)} %get-tuple-element.39.refs_2_.refs_1_.out_ref, ...), custom_call_target="tpu_custom_call" | custom-call | flops 107374184 | bytes 65536 | tf_op jit(solution)/shard_map/attend_own/pallas_call | solution.py:456
  27.2 0.0 collective-permute-done.4.refs_10_
  27.2 1.7 %query_grads.1 = (bf16[512,1024]{1,0:T(8,128)(2,1)}, f32[512,128]{1,0:T(8,128)S(1)}) custom-call(bf16[512,128]{1,0:T(8,128)(2,1)S(1)} %copy-done.1, bf16[8,64,256]{2,1,0:T(8,128)(2,1)S(1)} %get-tuple-element.52.refs_1_, bf16[8,32,256]{2,1,0:T(8,128)(2,1)S(1)} %get-tuple-element.53.refs_2_, bf16[128,128]{1,0:T(8,128)(2,1)S(1)} %get-tuple-element.54.refs_3_, ...), custom_call_target="tpu_custom_call" | custom-call | flops 322122560 | bytes 65536 | tf_op jit(solution)/shard_map/query_grads/pallas_call | solution.py:521
  28.9 1.0 %collective-permute-done.7.refs_4_ = bf16[64,128]{1,0:T(8,128)(2,1)S(1)} collective-permute-done((bf16[64,128]{1,0:T(8,128)(2,1)S(1)}, bf16[64,128]{1,0:T(8,128)(2,1)S(1)}, u32[]{:S(2)}, u32[]{:S(2)}) %collective-permute-start.7) | collective-permute-done | bytes 16416 | tf_op jit(solution)/shard_map/ppermute | solution.py:620
  29.9 0.0 collective-permute-done.5.refs_2_
  29.9 0.0 collective-permute-done.6.refs_3_
  29.9 0.8 %finish.1 = (bf16[512,128]{1,0:T(8,128)(2,1)}, bf16[512,128]{1,0:T(8,128)(2,1)}, bf16[32,128]{1,0:T(8,128)(2,1)}, bf16[32,128]{1,0:T(8,128)(2,1)}) custom-call(f32[512,128]{1,0:T(8,128)S(1)} %get-tuple-element.63.key_ref, f32[512,128]{1,0:T(8,128)S(1)} %get-tuple-element.64.value_ref, f32[512,128]{1,0:T(8,128)S(1)} %get-tuple-element.65.refs_0_, ...), custom_call_target="tpu_custom_call" | custom-call | flops 10737418 | bytes 65536 | tf_op jit(solution)/shard_map/finish/pallas_call | solution.py:557
  (1 shorter events, 0.0 us)
Async XLA Ops:
  1.6 5.9 %copy-start.3 = (bf16[2048,1024]{1,0:T(8,128)(2,1)S(1)}, bf16[2048,1024]{1,0:T(8,128)(2,1)}, u32[]{:S(2)}) copy-start(bf16[2048,1024]{1,0:T(8,128)(2,1)} %weight_ref.1) | copy-start | bytes 12582916
  1.6 5.9 %copy-start.4 = (bf16[512,2048]{1,0:T(8,128)(2,1)S(1)}, bf16[512,2048]{1,0:T(8,128)(2,1)}, u32[]{:S(2)}) copy-start(bf16[512,2048]{1,0:T(8,128)(2,1)} %grad_ref.1) | copy-start | bytes 6291460
  1.6 5.8 %copy-start.5 = (bf16[512,1024]{1,0:T(8,128)(2,1)S(1)}, bf16[512,1024]{1,0:T(8,128)(2,1)}, u32[]{:S(2)}) copy-start(bf16[512,1024]{1,0:T(8,128)(2,1)} %attn_ref.1) | copy-start | bytes 3145732
  1.6 5.8 %copy-start.6 = (f32[8,512]{1,0:T(8,128)S(1)}, f32[8,512]{1,0:T(8,128)}, u32[]{:S(2)}) copy-start(f32[8,512]{1,0:T(8,128)} %lse_ref.1) | copy-start | bytes 49156
  1.6 5.8 %copy-start.7 = (s32[64,1]{0,1:T(1,128)S(1)}, s32[64,1]{0,1:T(1,128)}, u32[]{:S(2)}) copy-start(s32[64,1]{0,1:T(1,128)} %param.21) | copy-start | bytes 772
  1.6 5.8 %copy-start.8 = (s32[64]{0:T(128)S(1)}, s32[64]{0:T(128)}, u32[]{:S(2)}) copy-start(s32[64]{0:T(128)} %root_ref.1) | copy-start | bytes 772
  1.6 5.8 %copy-start.9 = (s32[64]{0:T(128)S(1)}, s32[64]{0:T(128)}, u32[]{:S(2)}) copy-start(s32[64]{0:T(128)} %offset_ref.1) | copy-start | bytes 772
  1.6 9.4 %collective-permute-start = (bf16[576,128]{1,0:T(8,128)(2,1)S(1)}, bf16[576,128]{1,0:T(8,128)(2,1)S(1)}, u32[]{:S(2)}, u32[]{:S(2)}) collective-permute-start(bf16[576,128]{1,0:T(8,128)(2,1)S(1)} %pack.1.refs_5_.part_ref.refs_4_), channel_id=1, source_target_pairs={{0,12},{4,8},{8,4},{12,0},{1,13},{5,9},{9,5},{13,1},{2,14},{6,10},... | collective-permute-start | bytes 442376 | tf_op jit(solution)/shard_map/ppermute | solution.py:587
  6.8 11.2 %collective-permute-start.3 = (bf16[64,128]{1,0:T(8,128)(2,1)S(1)}, bf16[64,128]{1,0:T(8,128)(2,1)S(1)}, u32[]{:S(2)}, u32[]{:S(2)}) collective-permute-start(bf16[64,128]{1,0:T(8,128)(2,1)S(1)} %get-tuple-element.48), channel_id=1, source_target_pairs={{0,8},{4,12},{8,0},{12,4},{1,9},{5,13},{9,1},{13,5},{2,10},{6,14},... | collective-permute-start | bytes 49160 | tf_op jit(solution)/shard_map/ppermute | solution.py:589
  6.8 11.1 %collective-permute-start.2 = (bf16[576,128]{1,0:T(8,128)(2,1)S(1)}, bf16[576,128]{1,0:T(8,128)(2,1)S(1)}, u32[]{:S(2)}, u32[]{:S(2)}) collective-permute-start(bf16[576,128]{1,0:T(8,128)(2,1)S(1)} %get-tuple-element.47), channel_id=1, source_target_pairs={{0,4},{4,0},{8,12},{12,8},{1,5},{5,1},{9,13},{13,9},{2,6},{6,2},{1... | collective-permute-start | bytes 442376 | tf_op jit(solution)/shard_map/ppermute | solution.py:590
  7.5 6.5 %copy-start = (bf16[512,1024]{1,0:T(8,128)(2,1)S(1)}, bf16[512,1024]{1,0:T(8,128)(2,1)}, u32[]{:S(2)}) copy-start(bf16[512,1024]{1,0:T(8,128)(2,1)} %q_ref.1) | copy-start | bytes 3145732
  11.0 8.7 %collective-permute-start.1 = (bf16[576,128]{1,0:T(8,128)(2,1)S(1)}, bf16[576,128]{1,0:T(8,128)(2,1)S(1)}, u32[]{:S(2)}, u32[]{:S(2)}) collective-permute-start(bf16[576,128]{1,0:T(8,128)(2,1)S(1)} %collective-permute-done.refs_6_.refs_7_), channel_id=1, source_target_pairs={{0,4},{4,0},{8,12},{12,8},{1,5},{5,1},{9,13},{13,9},{2,6},{6,2},{1... | collective-permute-start | bytes 442376 | tf_op jit(solution)/shard_map/ppermute | solution.py:593
  15.3 10.2 %copy-start.1 = (bf16[512,128]{1,0:T(8,128)(2,1)S(1)}, bf16[512,128]{1,0:T(8,128)(2,1)}, u32[]{:S(2)}) copy-start(bf16[512,128]{1,0:T(8,128)(2,1)} %refs_0_.3) | copy-start | bytes 393220
  15.4 10.2 %copy-start.2 = (bf16[512,128]{1,0:T(8,128)(2,1)S(1)}, bf16[512,128]{1,0:T(8,128)(2,1)}, u32[]{:S(2)}) copy-start(bf16[512,128]{1,0:T(8,128)(2,1)} %value_ref.3) | copy-start | bytes 393220
  15.4 11.9 %collective-permute-start.4 = (bf16[512,128]{1,0:T(8,128)(2,1)S(1)}, bf16[512,128]{1,0:T(8,128)(2,1)S(1)}, u32[]{:S(2)}, u32[]{:S(2)}) collective-permute-start(bf16[512,128]{1,0:T(8,128)(2,1)S(1)} %get-tuple-element.61), channel_id=1, source_target_pairs={{0,12},{4,8},{8,4},{12,0},{1,13},{5,9},{9,5},{13,1},{2,14},{6,10},... | collective-permute-start | bytes 393224 | tf_op jit(solution)/shard_map/ppermute | solution.py:604
  21.1 8.8 %collective-permute-start.5 = (bf16[576,128]{1,0:T(8,128)(2,1)S(1)}, bf16[576,128]{1,0:T(8,128)(2,1)S(1)}, u32[]{:S(2)}, u32[]{:S(2)}) collective-permute-start(bf16[576,128]{1,0:T(8,128)(2,1)S(1)} %get-tuple-element.66), channel_id=1, source_target_pairs={{0,8},{4,12},{8,0},{12,4},{1,9},{5,13},{9,1},{13,5},{2,10},{6,14},... | collective-permute-start | bytes 442376 | tf_op jit(solution)/shard_map/ppermute | solution.py:618
  22.8 7.1 %collective-permute-start.6 = (bf16[576,128]{1,0:T(8,128)(2,1)S(1)}, bf16[576,128]{1,0:T(8,128)(2,1)S(1)}, u32[]{:S(2)}, u32[]{:S(2)}) collective-permute-start(bf16[576,128]{1,0:T(8,128)(2,1)S(1)} %get-tuple-element.67), channel_id=1, source_target_pairs={{0,4},{4,0},{8,12},{12,8},{1,5},{5,1},{9,13},{13,9},{2,6},{6,2},{1... | collective-permute-start | bytes 442376 | tf_op jit(solution)/shard_map/ppermute | solution.py:619
  24.2 5.6 %collective-permute-start.7 = (bf16[64,128]{1,0:T(8,128)(2,1)S(1)}, bf16[64,128]{1,0:T(8,128)(2,1)S(1)}, u32[]{:S(2)}, u32[]{:S(2)}) collective-permute-start(bf16[64,128]{1,0:T(8,128)(2,1)S(1)} %get-tuple-element.68), channel_id=1, source_target_pairs={{0,12},{4,8},{8,4},{12,0},{1,13},{5,9},{9,5},{13,1},{2,14},{6,10},... | collective-permute-start | bytes 49160 | tf_op jit(solution)/shard_map/ppermute | solution.py:620

commit v5 on v4

--- a/solution.py
+++ b/solution.py
@@ -12,6 +12,7 @@
 ROOTS_DEV = 4
 RLEN = 64
 CLEN = 16
+MOST = 8
 ROOT_ROWS = ROOTS_DEV * RLEN
 BLOCK = 64
 UNIT = 256
@@ -139,10 +140,17 @@
     width = 2 * HD
     lane = lax.broadcasted_iota(jnp.int32, (rows, HD), 1)
     columns = jnp.zeros((rows, HD), F32)
-    start = lax.axis_index("servers") * CH_DEV
+    my_index = lax.axis_index("servers")
+    for child in range(CH_DEV + 1):
+        forks_out[CH_DEV + child] = CH_DEV
+    found = jnp.int32(0)
     for child in range(CH_DEV):
-        at = start + child
-        forks_out[child] = (owner_ref[at] * ROOTS_DEV + root_ref[at]) * (2 * RLEN) + offset_ref[at]
+        at = my_index * CH_DEV + child
+        owner = owner_ref[at]
+        forks_out[child] = (owner * ROOTS_DEV + root_ref[at]) * (2 * RLEN) + offset_ref[at]
+        forks_out[CH_DEV + found] = child
+        found = found + jnp.where((owner ^ my_index) == 3, 1, 0)
+    forks_out[CH_DEV + found] = CH_DEV
     for unit, row in enumerate(unit_rows(lse_ref[...] * LOG2E)):
         lse_out[unit : unit + 1] = row
     for step in range(cols // width):
@@ -169,7 +177,7 @@
             kept((rows, cols), BF16),
             kept((units, UNIT), F32),
             kept((units, UNIT), F32),
-            pltpu.SMEM((CH_DEV,), jnp.int32),
+            pltpu.SMEM((2 * CH_DEV + 1,), jnp.int32),
         ],
         compiler_params=params(12),
         cost_estimate=cost("out_grad"),
@@ -327,12 +335,16 @@
         owner = fork >> 9
         if is_part:
             slot = owner ^ my_index
-            is_last = slot == held[1]
-            bases[child] = pl.multiple_of(jnp.where(is_last, part, 0) + row, RLEN)
-            limits[child] = jnp.where(is_last | (slot == held[0]), limit, 0)
             at = row + ROOT_ROWS
-            keys = jnp.where(is_last, shards[1][pl.ds(row, RLEN)], shards[0][pl.ds(row, RLEN)])
-            values = jnp.where(is_last, shards[1][pl.ds(at, RLEN)], shards[0][pl.ds(at, RLEN)])
+            keys, values = shards[0][pl.ds(row, RLEN)], shards[0][pl.ds(at, RLEN)]
+            place, inside = 0, slot == held[0]
+            for index in range(1, count):
+                here = slot == held[index]
+                place, inside = jnp.where(here, index, place), inside | here
+                keys = jnp.where(here, shards[index][pl.ds(row, RLEN)], keys)
+                values = jnp.where(here, shards[index][pl.ds(at, RLEN)], values)
+            bases[child] = pl.multiple_of(place * part + row, RLEN)
+            limits[child] = jnp.where(inside, limit, 0)
         else:
             bases[child] = pl.multiple_of(owner * part + row, RLEN)
             limits[child] = limit
@@ -343,19 +355,42 @@
 
     key_index = lax.broadcasted_iota(jnp.int32, (RLEN, heads * CLEN), 0)
 
-    def keep(child, key_grad, value_grad, score_grads):
-        ds_ref[child] = score_grads
-        grads_ref[child, 0:RLEN] = key_grad * SCALE
-        grads_ref[child, RLEN:] = value_grad
-
-    swept(
-        range(CH_DEV),
-        child_loader(q_ref, out_ref, lse_ref, delta_ref),
-        parts,
-        lambda child, weights: jnp.where(key_index < limits[child], weights, 0.0),
-        keep,
-        2,
-    )
+    columns = heads * CLEN
+    load = unit_loader(q_ref, out_ref, lse_ref, delta_ref)
+    roots, _ = unit_counts(q_ref.shape[0], heads)
+    empty = jnp.zeros((RLEN, columns), BF16)
+
+    def diagonal(pieces):
+        rows = [[piece if k == place else empty for place in range(PAIR)] for k, piece in enumerate(pieces)]
+        return jnp.concatenate([jnp.concatenate(row, axis=1) for row in rows], axis=0)
+
+    ready = []
+    for pair in range(CH_DEV // PAIR + 3):
+        if pair < CH_DEV // PAIR:
+            query, out, lse, delta = load(roots + pair)
+            held_parts = [parts(pair * PAIR + k) for k in range(PAIR)]
+            scores = dot(jnp.concatenate([keys for keys, _ in held_parts], axis=0), query, NT)
+            weight_grads = dot(jnp.concatenate([values for _, values in held_parts], axis=0), out, NT)
+            ready.append((pair, query, out, lse, delta, scores, weight_grads))
+            if len(ready) <= 3:
+                continue
+        done, query, out, lse, delta, scores, weight_grads = ready.pop(0)
+        low, score_grads = [], []
+        for k in range(PAIR):
+            child = done * PAIR + k
+            rows, lanes = slice(k * RLEN, (k + 1) * RLEN), slice(k * columns, (k + 1) * columns)
+            weights = jnp.exp2(scores[rows, lanes] * (SCALE * LOG2E) - lse[:, lanes])
+            weights = jnp.where(key_index < limits[child], weights, 0.0)
+            grads = (weights * (weight_grads[rows, lanes] - delta[:, lanes])).astype(BF16)
+            ds_ref[child] = grads
+            low.append(weights.astype(BF16))
+            score_grads.append(grads)
+        key_grads = dot(diagonal(score_grads), query, NN) * SCALE
+        value_grads = dot(diagonal(low), out, NN)
+        for k in range(PAIR):
+            child, rows = done * PAIR + k, slice(k * RLEN, (k + 1) * RLEN)
+            grads_ref[child, 0:RLEN] = key_grads[rows]
+            grads_ref[child, RLEN:] = value_grads[rows]
     sums_ref[...] = jnp.zeros(sums_ref.shape, F32)
     for child in range(CH_DEV):
         base = bases[child]
@@ -401,6 +436,95 @@
         cost_estimate=cost(name),
         name=name,
     )(pinned_scalars(forks), *(pinned(x) for x in operands))
+
+
+def near_body(fork_ref, q_ref, out_ref, lse_ref, delta_ref, shard_ref, ds_ref, key_ref, send_ref, grads_ref, sums_ref):
+    tokens, heads = q_ref.shape[0], q_ref.shape[1] // HD
+    columns = heads * CLEN
+    roots, _ = unit_counts(tokens, heads)
+    ds_ref[...] = jnp.zeros(ds_ref.shape, BF16)
+    key_ref[...] = jnp.zeros(key_ref.shape, BF16)
+    key_index = lax.broadcasted_iota(jnp.int32, (RLEN, columns), 0)
+    empty = jnp.zeros((RLEN, columns), BF16)
+
+    def diagonal(pieces):
+        rows = [[piece if k == place else empty for place in range(PAIR)] for k, piece in enumerate(pieces)]
+        return jnp.concatenate([jnp.concatenate(row, axis=1) for row in rows], axis=0)
+
+    def tiles(ref, starts):
+        return jnp.concatenate(
+            [ref[pl.ds(start, CLEN), head * HD : (head + 1) * HD] for start in starts for head in range(heads)], axis=0
+        )
+
+    def half(ref, child):
+        row = ref[pl.ds(roots + child // PAIR, 1)]
+        return jnp.where(child % PAIR == 0, row[:, :columns], row[:, columns:])
+
+    places, ready = [], []
+    for pair in range(MOST // PAIR + 2):
+        if pair < MOST // PAIR:
+            picked, starts, keys, values, lse, delta = [], [], [], [], [], []
+            for k in range(PAIR):
+                target = fork_ref[CH_DEV + pair * PAIR + k]
+                child = jnp.minimum(target, CH_DEV - 1)
+                fork = fork_ref[child]
+                limit = jnp.where(target < CH_DEV, fork & (2 * RLEN - 1), 0)
+                row = pl.multiple_of(((fork >> 7) & (ROOTS_DEV - 1)) * RLEN, RLEN)
+                starts.append(pl.multiple_of(ROOT_ROWS + child * CLEN, CLEN))
+                keys.append(shard_ref[pl.ds(row, RLEN)])
+                values.append(shard_ref[pl.ds(row + ROOT_ROWS, RLEN)])
+                lse.append(half(lse_ref, child))
+                delta.append(half(delta_ref, child))
+                key_ref[target] = keys[k]
+                picked.append((target, limit, row))
+            places += [row for _, _, row in picked]
+            query, out = tiles(q_ref, starts), tiles(out_ref, starts)
+            scores = dot(jnp.concatenate(keys, axis=0), query, NT)
+            weight_grads = dot(jnp.concatenate(values, axis=0), out, NT)
+            ready.append((pair, picked, query, out, lse, delta, scores, weight_grads))
+            if len(ready) <= 2:
+                continue
+        done, picked, query, out, lse, delta, scores, weight_grads = ready.pop(0)
+        low, score_grads = [], []
+        for k, (target, limit, _) in enumerate(picked):
+            rows, lanes = slice(k * RLEN, (k + 1) * RLEN), slice(k * columns, (k + 1) * columns)
+            weights = jnp.exp2(scores[rows, lanes] * (SCALE * LOG2E) - lse[k])
+            weights = jnp.where(key_index < limit, weights, 0.0)
+            grads = (weights * (weight_grads[rows, lanes] - delta[k])).astype(BF16)
+            ds_ref[target] = grads
+            low.append(weights.astype(BF16))
+            score_grads.append(grads)
+        key_grads = dot(diagonal(score_grads), query, NN) * SCALE
+        value_grads = dot(diagonal(low), out, NN)
+        for k in range(PAIR):
+            rows = slice(k * RLEN, (k + 1) * RLEN)
+            grads_ref[done * PAIR + k, 0:RLEN] = key_grads[rows]
+            grads_ref[done * PAIR + k, RLEN:] = value_grads[rows]
+    sums_ref[...] = jnp.zeros(sums_ref.shape, F32)
+    for index, row in enumerate(places):
+        sums_ref[pl.ds(row, RLEN)] = sums_ref[pl.ds(row, RLEN)] + grads_ref[index, 0:RLEN]
+        at = row + ROOT_ROWS
+        sums_ref[pl.ds(at, RLEN)] = sums_ref[pl.ds(at, RLEN)] + grads_ref[index, RLEN:]
+    send_ref[...] = sums_ref[...].astype(BF16)
+
+
+def near_call(forks, shared, shard):
+    columns = shared[0].shape[1] // HD * CLEN
+    part = 2 * ROOT_ROWS
+    return pl.pallas_call(
+        near_body,
+        in_specs=[SMEM] + [VMEM] * 5,
+        out_specs=[VMEM] * 3,
+        out_shape=[
+            kept((CH_DEV + 1, RLEN, columns), BF16),
+            kept((CH_DEV + 1, RLEN, HD), BF16),
+            kept((part, HD), BF16),
+        ],
+        scratch_shapes=[pltpu.VMEM((MOST, 2 * RLEN, HD), F32), pltpu.VMEM((part, HD), F32)],
+        compiler_params=params(8),
+        cost_estimate=cost("attend_near"),
+        name="attend_near",
+    )(pinned_scalars(forks), *(pinned(x) for x in (*shared, shard)))
 
 
 def own_rows(tokens, heads, unit):
@@ -590,28 +714,20 @@
         part_one = lax.ppermute(later_part, "servers", pairs[1])
         out_grad, lse_rows, delta, forks = out_grad_call(grad_out, out_weight, attn_out, lse, *forks)
         part_two, delta = lax.optimization_barrier((part_two, delta))
-        part_far = lax.ppermute(part_two, "servers", pairs[1])
+        part_far = lax.ppermute(part_two[: 2 * ROOT_ROWS], "servers", pairs[1])
         part, whole = (2 * ROOT_ROWS, HD), (2 * ROOT_ROWS + 2 * own, HD)
-        near_ds, near_keys, own_sums, send_two = parent_call(
-            forks,
-            (queries, out_grad, lse_rows, delta),
-            [own_part, part_two],
-            (0, 3),
-            [kept(part, F32), kept(part, BF16)],
-            None,
-            "attend_near",
-        )
+        near_ds, near_keys, send_two = near_call(forks, (queries, out_grad, lse_rows, delta), part_two)
         back_two = lax.ppermute(send_two, "servers", pairs[3])
-        delta, own_sums = lax.optimization_barrier((delta, own_sums))
+        delta, near_ds = lax.optimization_barrier((delta, near_ds))
         prompt_ds, prompt_keys, prompt_sums, send_two_prompt = prompt_call(
             (queries, out_grad, lse_rows, delta), [own_part, part_one, prompt_far, part_two], 2 * own, True
         )
-        far_ds, far_keys, send_far, send_one = parent_call(
+        far_ds, far_keys, own_sums, send_far, send_one = parent_call(
             forks,
             (queries, out_grad, lse_rows, delta),
-            [part_far, part_one],
-            (2, 1),
-            [kept(whole, BF16), kept(whole, BF16)],
+            [own_part, part_far, part_one],
+            (0, 2, 1),
+            [kept(part, F32), kept(whole, BF16), kept(whole, BF16)],
             prompt_sums,
             "attend_far",
         )

time: 30.8 us -> 30 us (0.974)
  Pallas kernels: 12.8 us -> 11.6 us
  waiting for transfers between devices: 1.14 us -> 1.5 us
    pallas_call x2 -> x1, Pallas kernels: 2.69 us -> 0.91 us  [parent_call(): pl.pallas_call(body, in_specs=[SMEM] + [VMEM] * len(operands), out_specs=...]
    pallas_call x0 -> x1, Pallas kernels: none -> 0.58 us  [near_call(): pl.pallas_call(near_body, in_specs=[SMEM] + [VMEM] * 5, out_specs=[VMEM]...]
    ppermute x1, starting transfers between devices: 1.72 us -> 2.26 us  [local(): back_far = lax.ppermute(send_far, 'servers', pairs[2])]
    ppermute x1, starting transfers between devices: 1.3 us -> 0.88 us  [local(): back_two_prompt = lax.ppermute(send_two_prompt, 'servers', pairs[3])]
    ppermute x1, waiting for transfers between devices: 0.97 us -> 1.34 us  [local(): back_two_prompt = lax.ppermute(send_two_prompt, 'servers', pairs[3])]
  transfers between devices with their start and end apart: 8 -> 8, of which waited for: 2 -> 2; matrix products, arithmetic and copies ran while one was open for 0% -> 0% of each run, Pallas kernels for 36% -> 33%
where the time goes in v5:
time: 30 us; the launch traced here: 29.9 us
  starting transfers between devices  15.8 us (53%)
  Pallas kernels  11.6 us (39%)
  waiting for transfers between devices  1.5 us (5%)
  between operations  0.83 us (3%)
    ppermute x1, starting transfers between devices, local(): part_two = lax.ppermute(own_part, 'servers', pairs[3])  5.11 us
    pallas_call x1, Pallas kernels, out_grad_call(): pl.pallas_call(out_grad_body, in_specs=[VMEM] * 4 + [SMEM] * 3, out_specs...  3.38 us
    ppermute x1, starting transfers between devices, local(): part_far = lax.ppermute(part_two[:2 * ROOT_ROWS], 'servers', pairs[1])  3.06 us
    ppermute x1, starting transfers between devices, local(): back_two = lax.ppermute(send_two, 'servers', pairs[3])  2.57 us
    ppermute x1, starting transfers between devices, local(): back_far = lax.ppermute(send_far, 'servers', pairs[2])  2.26 us
    pallas_call x1, Pallas kernels, prompt_call(): pl.pallas_call(body, in_specs=[VMEM] * len(operands), out_specs=[VMEM] *...  1.73 us
    pallas_call x1, Pallas kernels, own_call(): pl.pallas_call(own_body, in_specs=[VMEM] * 6, out_specs=[VMEM] * 4, out_s...  1.68 us
    pallas_call x1, Pallas kernels, query_call(): pl.pallas_call(body, in_specs=[VMEM] * len(operands), out_specs=[ANY, *[V...  1.65 us
  transfers between devices with their start and end apart: 8, of which 2 were waited for; matrix products, arithmetic and copies ran while one was open for 0% of the time, Pallas kernels for 33%

profile of v5, /device:TPU:0, one launch (start us, length us, event | category | flops | bytes accessed | tf_op | source)
XLA Modules:
  0.0 29.9 jit_solution(2575533280914240006)
XLA Ops:
  0.6 0.9 %pack.1.part_ref.refs_4_.refs_5_ = bf16[576,128]{1,0:T(8,128)(2,1)S(1)} custom-call(bf16[512,128]{1,0:T(8,128)(2,1)} %refs_0_.3, bf16[512,128]{1,0:T(8,128)(2,1)} %value_ref.3, bf16[32,128]{1,0:T(8,128)(2,1)} %prefix_key_ref.1, bf16[32,128]{1,0:T(8,128)(2,1)} %prefix_value_ref.1), custom_call_target="tpu_custom_call" | custom-call | flops 8589934592 | bytes 65536 | tf_op jit(solution)/shard_map/pack/pallas_call | solution.py:94
  1.6 0.0 copy-start.3
  1.6 0.0 copy-start.4
  1.6 0.0 copy-start.5
  1.6 0.0 copy-start.6
  1.6 0.0 copy-start.7
  1.6 0.0 copy-start.8
  1.6 0.0 copy-start.9
  1.6 5.1 %collective-permute-start = (bf16[576,128]{1,0:T(8,128)(2,1)S(1)}, bf16[576,128]{1,0:T(8,128)(2,1)S(1)}, u32[]{:S(2)}, u32[]{:S(2)}) collective-permute-start(bf16[576,128]{1,0:T(8,128)(2,1)S(1)} %pack.1.part_ref.refs_4_.refs_5_), channel_id=1, source_target_pairs={{0,12},{4,8},{8,4},{12,0},{1,13},{5,9},{9,5},{13,1},{2,14},{6,10},... | collective-permute-start | bytes 442376 | tf_op jit(solution)/shard_map/ppermute | solution.py:711
  6.8 0.1 collective-permute-start.3
  6.8 0.6 %collective-permute-start.2 = (bf16[576,128]{1,0:T(8,128)(2,1)S(1)}, bf16[576,128]{1,0:T(8,128)(2,1)S(1)}, u32[]{:S(2)}, u32[]{:S(2)}) collective-permute-start(bf16[576,128]{1,0:T(8,128)(2,1)S(1)} %get-tuple-element.47), channel_id=1, source_target_pairs={{0,4},{4,0},{8,12},{12,8},{1,5},{5,1},{9,13},{13,9},{2,6},{6,2},{1... | collective-permute-start | bytes 442376 | tf_op jit(solution)/shard_map/ppermute | solution.py:714
  7.4 0.0 copy-done.3
  7.4 0.0 copy-done.4
  7.4 0.0 copy-done.5
  7.4 0.0 copy-done.6
  7.4 0.0 copy-done.7
  7.4 0.0 copy-done.8
  7.5 0.0 copy-done.9
  7.5 0.0 copy-start
  7.5 3.4 %out_grad.1 = (bf16[512,1024]{1,0:T(8,128)(2,1)S(1)}, f32[16,256]{1,0:T(8,128)S(1)}, f32[16,256]{1,0:T(8,128)S(1)}, s32[33]{0:T(128)S(4)}) custom-call(bf16[512,2048]{1,0:T(8,128)(2,1)S(1)} %copy-done.4, bf16[2048,1024]{1,0:T(8,128)(2,1)S(1)} %copy-done.3, bf16[512,1024]{1,0:T(8,128)(2,1)S(1)} %copy-done.5, f32[8,512]{1,0:T(8,128)S(1)} %copy-done.6, ...), custom_call_target="tpu_custom_call" | custom-call | flops 6442450944 | bytes 65536 | tf_op jit(solution)/shard_map/out_grad/pallas_call | solution.py:172
  10.9 0.2 collective-permute-done.shard_ref.refs_7_
  11.0 3.1 %collective-permute-start.1 = (bf16[512,128]{1,0:T(8,128)(2,1)S(1)}, bf16[512,128]{1,0:T(8,128)(2,1)S(1)}, u32[]{:S(2)}, u32[]{:S(2)}) collective-permute-start(bf16[512,128]{1,0:T(8,128)(2,1)S(1)} %slice.3), channel_id=1, source_target_pairs={{0,4},{4,0},{8,12},{12,8},{1,5},{5,1},{9,13},{13,9},{2,6},{6,2},{1... | collective-permute-start | bytes 393224 | tf_op jit(solution)/shard_map/ppermute | solution.py:717
  14.1 0.0 copy-done
  14.1 0.6 %attend_near.1 = (bf16[17,64,128]{2,1,0:T(8,128)(2,1)S(1)}, bf16[17,64,128]{2,1,0:T(8,128)(2,1)S(1)}, bf16[512,128]{1,0:T(8,128)(2,1)S(1)}) custom-call(s32[33]{0:T(128)S(4)} %get-tuple-element.43.fork_ref.refs_0_, bf16[512,1024]{1,0:T(8,128)(2,1)S(1)} %copy-done, bf16[512,1024]{1,0:T(8,128)(2,1)S(1)} %get-tuple-element.39.out_ref.refs_1_.refs_2_, ...), custom_call_target="tpu_custom_call" | custom-call | flops 3221225472 | bytes 65536 | tf_op jit(solution)/shard_map/attend_near/pallas_call | solution.py:514
  14.7 0.0 copy-start.1
  14.7 0.0 copy-start.2
  14.7 2.6 %collective-permute-start.4 = (bf16[512,128]{1,0:T(8,128)(2,1)S(1)}, bf16[512,128]{1,0:T(8,128)(2,1)S(1)}, u32[]{:S(2)}, u32[]{:S(2)}) collective-permute-start(bf16[512,128]{1,0:T(8,128)(2,1)S(1)} %get-tuple-element.61), channel_id=1, source_target_pairs={{0,12},{4,8},{8,4},{12,0},{1,13},{5,9},{9,5},{13,1},{2,14},{6,10},... | collective-permute-start | bytes 393224 | tf_op jit(solution)/shard_map/ppermute | solution.py:720
  17.3 0.0 collective-permute-done.3.refs_6_
  17.3 0.0 collective-permute-done.2.refs_5_.refs_7_
  17.3 1.7 %attend_prompt.1 = (bf16[16,128,256]{2,1,0:T(8,128)(2,1)S(1)}, bf16[128,128]{1,0:T(8,128)(2,1)S(1)}, f32[256,128]{1,0:T(8,128)S(1)}, bf16[64,128]{1,0:T(8,128)(2,1)S(1)}) custom-call(bf16[512,1024]{1,0:T(8,128)(2,1)S(1)} %copy-done, bf16[512,1024]{1,0:T(8,128)(2,1)S(1)} %get-tuple-element.39.out_ref.refs_1_.refs_2_, ...), custom_call_target="tpu_custom_call" | custom-call | flops 107374184 | bytes 65536 | tf_op jit(solution)/shard_map/attend_prompt/pallas_call | solution.py:306
  19.0 0.0 collective-permute-done.1.refs_6_
  19.0 0.9 %attend_far.1 = (bf16[16,64,128]{2,1,0:T(8,128)(2,1)S(1)}, bf16[16,64,128]{2,1,0:T(8,128)(2,1)S(1)}, f32[512,128]{1,0:T(8,128)S(1)}, bf16[576,128]{1,0:T(8,128)(2,1)S(1)}, bf16[576,128]{1,0:T(8,128)(2,1)S(1)}) custom-call(s32[33]{0:T(128)S(4)} %get-tuple-element.43.fork_ref.refs_0_, bf16[512,1024]{1,0:T(8,128)(2,1)S(1)} %copy-done, ...), custom_call_target="tpu_custom_call" | custom-call | flops 107374184 | bytes 65536 | tf_op jit(solution)/shard_map/attend_far/pallas_call | solution.py:426
  19.9 2.3 %collective-permute-start.5 = (bf16[576,128]{1,0:T(8,128)(2,1)S(1)}, bf16[576,128]{1,0:T(8,128)(2,1)S(1)}, u32[]{:S(2)}, u32[]{:S(2)}) collective-permute-start(bf16[576,128]{1,0:T(8,128)(2,1)S(1)} %get-tuple-element.66), channel_id=1, source_target_pairs={{0,8},{4,12},{8,0},{12,4},{1,9},{5,13},{9,1},{13,5},{2,10},{6,14},... | collective-permute-start | bytes 442376 | tf_op jit(solution)/shard_map/ppermute | solution.py:734
  22.2 1.3 %collective-permute-start.6 = (bf16[576,128]{1,0:T(8,128)(2,1)S(1)}, bf16[576,128]{1,0:T(8,128)(2,1)S(1)}, u32[]{:S(2)}, u32[]{:S(2)}) collective-permute-start(bf16[576,128]{1,0:T(8,128)(2,1)S(1)} %get-tuple-element.67), channel_id=1, source_target_pairs={{0,4},{4,0},{8,12},{12,8},{1,5},{5,1},{9,13},{13,9},{2,6},{6,2},{1... | collective-permute-start | bytes 442376 | tf_op jit(solution)/shard_map/ppermute | solution.py:735
  23.5 0.9 %collective-permute-start.7 = (bf16[64,128]{1,0:T(8,128)(2,1)S(1)}, bf16[64,128]{1,0:T(8,128)(2,1)S(1)}, u32[]{:S(2)}, u32[]{:S(2)}) collective-permute-start(bf16[64,128]{1,0:T(8,128)(2,1)S(1)} %get-tuple-element.68), channel_id=1, source_target_pairs={{0,12},{4,8},{8,4},{12,0},{1,13},{5,9},{9,5},{13,1},{2,14},{6,10},... | collective-permute-start | bytes 49160 | tf_op jit(solution)/shard_map/ppermute | solution.py:736
  24.4 0.0 copy-done.1
  24.4 0.0 copy-done.2
  24.4 1.7 %attend_own.1 = (bf16[8,64,256]{2,1,0:T(8,128)(2,1)S(1)}, bf16[8,32,256]{2,1,0:T(8,128)(2,1)S(1)}, f32[512,128]{1,0:T(8,128)S(1)}, f32[512,128]{1,0:T(8,128)S(1)}) custom-call(bf16[512,1024]{1,0:T(8,128)(2,1)S(1)} %copy-done, bf16[512,1024]{1,0:T(8,128)(2,1)S(1)} %get-tuple-element.39.out_ref.refs_1_.refs_2_, ...), custom_call_target="tpu_custom_call" | custom-call | flops 107374184 | bytes 65536 | tf_op jit(solution)/shard_map/attend_own/pallas_call | solution.py:580
  26.1 0.0 collective-permute-done.4.refs_10_
  26.1 1.7 %query_grads.1 = (bf16[512,1024]{1,0:T(8,128)(2,1)}, f32[512,128]{1,0:T(8,128)S(1)}) custom-call(bf16[512,128]{1,0:T(8,128)(2,1)S(1)} %copy-done.1, bf16[8,64,256]{2,1,0:T(8,128)(2,1)S(1)} %get-tuple-element.52.refs_1_, bf16[8,32,256]{2,1,0:T(8,128)(2,1)S(1)} %get-tuple-element.53.refs_2_, bf16[128,128]{1,0:T(8,128)(2,1)S(1)} %get-tuple-element.54.refs_3_, ...), custom_call_target="tpu_custom_call" | custom-call | flops 322122560 | bytes 65536 | tf_op jit(solution)/shard_map/query_grads/pallas_call | solution.py:645
  27.8 1.3 %collective-permute-done.7.refs_4_ = bf16[64,128]{1,0:T(8,128)(2,1)S(1)} collective-permute-done((bf16[64,128]{1,0:T(8,128)(2,1)S(1)}, bf16[64,128]{1,0:T(8,128)(2,1)S(1)}, u32[]{:S(2)}, u32[]{:S(2)}) %collective-permute-start.7) | collective-permute-done | bytes 16416 | tf_op jit(solution)/shard_map/ppermute | solution.py:736
  29.1 0.0 collective-permute-done.5.refs_2_
  29.1 0.0 collective-permute-done.6.refs_3_
  29.1 0.8 %finish.1 = (bf16[512,128]{1,0:T(8,128)(2,1)}, bf16[512,128]{1,0:T(8,128)(2,1)}, bf16[32,128]{1,0:T(8,128)(2,1)}, bf16[32,128]{1,0:T(8,128)(2,1)}) custom-call(f32[512,128]{1,0:T(8,128)S(1)} %get-tuple-element.63.key_ref, f32[512,128]{1,0:T(8,128)S(1)} %get-tuple-element.64.value_ref, f32[512,128]{1,0:T(8,128)S(1)} %get-tuple-element.65.refs_0_, ...), custom_call_target="tpu_custom_call" | custom-call | flops 10737418 | bytes 65536 | tf_op jit(solution)/shard_map/finish/pallas_call | solution.py:681
  (2 shorter events, 0.0 us)
Async XLA Ops:
  1.6 5.9 %copy-start.3 = (bf16[2048,1024]{1,0:T(8,128)(2,1)S(1)}, bf16[2048,1024]{1,0:T(8,128)(2,1)}, u32[]{:S(2)}) copy-start(bf16[2048,1024]{1,0:T(8,128)(2,1)} %weight_ref.1) | copy-start | bytes 12582916
  1.6 5.9 %copy-start.4 = (bf16[512,2048]{1,0:T(8,128)(2,1)S(1)}, bf16[512,2048]{1,0:T(8,128)(2,1)}, u32[]{:S(2)}) copy-start(bf16[512,2048]{1,0:T(8,128)(2,1)} %grad_ref.1) | copy-start | bytes 6291460
  1.6 5.8 %copy-start.5 = (bf16[512,1024]{1,0:T(8,128)(2,1)S(1)}, bf16[512,1024]{1,0:T(8,128)(2,1)}, u32[]{:S(2)}) copy-start(bf16[512,1024]{1,0:T(8,128)(2,1)} %attn_ref.1) | copy-start | bytes 3145732
  1.6 5.8 %copy-start.6 = (f32[8,512]{1,0:T(8,128)S(1)}, f32[8,512]{1,0:T(8,128)}, u32[]{:S(2)}) copy-start(f32[8,512]{1,0:T(8,128)} %lse_ref.1) | copy-start | bytes 49156
  1.6 5.8 %copy-start.7 = (s32[64,1]{0,1:T(1,128)S(1)}, s32[64,1]{0,1:T(1,128)}, u32[]{:S(2)}) copy-start(s32[64,1]{0,1:T(1,128)} %param.21) | copy-start | bytes 772
  1.6 5.8 %copy-start.8 = (s32[64]{0:T(128)S(1)}, s32[64]{0:T(128)}, u32[]{:S(2)}) copy-start(s32[64]{0:T(128)} %root_ref.1) | copy-start | bytes 772
  1.6 5.8 %copy-start.9 = (s32[64]{0:T(128)S(1)}, s32[64]{0:T(128)}, u32[]{:S(2)}) copy-start(s32[64]{0:T(128)} %offset_ref.1) | copy-start | bytes 772
  1.6 9.4 %collective-permute-start = (bf16[576,128]{1,0:T(8,128)(2,1)S(1)}, bf16[576,128]{1,0:T(8,128)(2,1)S(1)}, u32[]{:S(2)}, u32[]{:S(2)}) collective-permute-start(bf16[576,128]{1,0:T(8,128)(2,1)S(1)} %pack.1.part_ref.refs_4_.refs_5_), channel_id=1, source_target_pairs={{0,12},{4,8},{8,4},{12,0},{1,13},{5,9},{9,5},{13,1},{2,14},{6,10},... | collective-permute-start | bytes 442376 | tf_op jit(solution)/shard_map/ppermute | solution.py:711
  6.8 10.5 %collective-permute-start.3 = (bf16[64,128]{1,0:T(8,128)(2,1)S(1)}, bf16[64,128]{1,0:T(8,128)(2,1)S(1)}, u32[]{:S(2)}, u32[]{:S(2)}) collective-permute-start(bf16[64,128]{1,0:T(8,128)(2,1)S(1)} %get-tuple-element.48), channel_id=1, source_target_pairs={{0,8},{4,12},{8,0},{12,4},{1,9},{5,13},{9,1},{13,5},{2,10},{6,14},... | collective-permute-start | bytes 49160 | tf_op jit(solution)/shard_map/ppermute | solution.py:713
  6.8 10.4 %collective-permute-start.2 = (bf16[576,128]{1,0:T(8,128)(2,1)S(1)}, bf16[576,128]{1,0:T(8,128)(2,1)S(1)}, u32[]{:S(2)}, u32[]{:S(2)}) collective-permute-start(bf16[576,128]{1,0:T(8,128)(2,1)S(1)} %get-tuple-element.47), channel_id=1, source_target_pairs={{0,4},{4,0},{8,12},{12,8},{1,5},{5,1},{9,13},{13,9},{2,6},{6,2},{1... | collective-permute-start | bytes 442376 | tf_op jit(solution)/shard_map/ppermute | solution.py:714
  7.5 6.6 %copy-start = (bf16[512,1024]{1,0:T(8,128)(2,1)S(1)}, bf16[512,1024]{1,0:T(8,128)(2,1)}, u32[]{:S(2)}) copy-start(bf16[512,1024]{1,0:T(8,128)(2,1)} %q_ref.3) | copy-start | bytes 3145732
  11.0 8.0 %collective-permute-start.1 = (bf16[512,128]{1,0:T(8,128)(2,1)S(1)}, bf16[512,128]{1,0:T(8,128)(2,1)S(1)}, u32[]{:S(2)}, u32[]{:S(2)}) collective-permute-start(bf16[512,128]{1,0:T(8,128)(2,1)S(1)} %slice.3), channel_id=1, source_target_pairs={{0,4},{4,0},{8,12},{12,8},{1,5},{5,1},{9,13},{13,9},{2,6},{6,2},{1... | collective-permute-start | bytes 393224 | tf_op jit(solution)/shard_map/ppermute | solution.py:717
  14.7 9.7 %copy-start.1 = (bf16[512,128]{1,0:T(8,128)(2,1)S(1)}, bf16[512,128]{1,0:T(8,128)(2,1)}, u32[]{:S(2)}) copy-start(bf16[512,128]{1,0:T(8,128)(2,1)} %refs_0_.3) | copy-start | bytes 393220
  14.7 9.7 %copy-start.2 = (bf16[512,128]{1,0:T(8,128)(2,1)S(1)}, bf16[512,128]{1,0:T(8,128)(2,1)}, u32[]{:S(2)}) copy-start(bf16[512,128]{1,0:T(8,128)(2,1)} %value_ref.3) | copy-start | bytes 393220
  14.7 11.4 %collective-permute-start.4 = (bf16[512,128]{1,0:T(8,128)(2,1)S(1)}, bf16[512,128]{1,0:T(8,128)(2,1)S(1)}, u32[]{:S(2)}, u32[]{:S(2)}) collective-permute-start(bf16[512,128]{1,0:T(8,128)(2,1)S(1)} %get-tuple-element.61), channel_id=1, source_target_pairs={{0,12},{4,8},{8,4},{12,0},{1,13},{5,9},{9,5},{13,1},{2,14},{6,10},... | collective-permute-start | bytes 393224 | tf_op jit(solution)/shard_map/ppermute | solution.py:720
  19.9 9.2 %collective-permute-start.5 = (bf16[576,128]{1,0:T(8,128)(2,1)S(1)}, bf16[576,128]{1,0:T(8,128)(2,1)S(1)}, u32[]{:S(2)}, u32[]{:S(2)}) collective-permute-start(bf16[576,128]{1,0:T(8,128)(2,1)S(1)} %get-tuple-element.66), channel_id=1, source_target_pairs={{0,8},{4,12},{8,0},{12,4},{1,9},{5,13},{9,1},{13,5},{2,10},{6,14},... | collective-permute-start | bytes 442376 | tf_op jit(solution)/shard_map/ppermute | solution.py:734
  22.2 6.9 %collective-permute-start.6 = (bf16[576,128]{1,0:T(8,128)(2,1)S(1)}, bf16[576,128]{1,0:T(8,128)(2,1)S(1)}, u32[]{:S(2)}, u32[]{:S(2)}) collective-permute-start(bf16[576,128]{1,0:T(8,128)(2,1)S(1)} %get-tuple-element.67), channel_id=1, source_target_pairs={{0,4},{4,0},{8,12},{12,8},{1,5},{5,1},{9,13},{13,9},{2,6},{6,2},{1... | collective-permute-start | bytes 442376 | tf_op jit(solution)/shard_map/ppermute | solution.py:735
  23.5 5.6 %collective-permute-start.7 = (bf16[64,128]{1,0:T(8,128)(2,1)S(1)}, bf16[64,128]{1,0:T(8,128)(2,1)S(1)}, u32[]{:S(2)}, u32[]{:S(2)}) collective-permute-start(bf16[64,128]{1,0:T(8,128)(2,1)S(1)} %get-tuple-element.68), channel_id=1, source_target_pairs={{0,12},{4,8},{8,4},{12,0},{1,13},{5,9},{9,5},{13,1},{2,14},{6,10},... | collective-permute-start | bytes 49160 | tf_op jit(solution)/shard_map/ppermute | solution.py:736

commit v6 on v5

--- a/solution.py
+++ b/solution.py
@@ -275,6 +275,7 @@
         lambda unit: (key_ref[...], value_ref[...]),
         lambda unit, weights: weights,
         keep,
+        2,
     )
 
     def store(ref, at, index):
@@ -571,6 +572,7 @@
         parts,
         lambda unit, weights: jnp.where(root_allowed if unit < roots else child_allowed, weights, 0.0),
         keep,
+        2,
     )
 
 
@@ -710,8 +712,8 @@
         pairs = [[(i, i ^ d) for i in range(4)] for d in range(4)]
         part_two = lax.ppermute(own_part, "servers", pairs[3])
         later_part, later_prompt = repeat_call(own_part)
+        part_one = lax.ppermute(later_part, "servers", pairs[1])
         prompt_far = lax.ppermute(later_prompt, "servers", pairs[2])
-        part_one = lax.ppermute(later_part, "servers", pairs[1])
         out_grad, lse_rows, delta, forks = out_grad_call(grad_out, out_weight, attn_out, lse, *forks)
         part_two, delta = lax.optimization_barrier((part_two, delta))
         part_far = lax.ppermute(part_two[: 2 * ROOT_ROWS], "servers", pairs[1])

time: 30 us -> 30 us (level)
  waiting for transfers between devices: 1.5 us -> 2.15 us
  Pallas kernels: 11.6 us -> 11 us
    ppermute x1, waiting for transfers between devices: 1.34 us -> 1.99 us  [local(): back_two_prompt = lax.ppermute(send_two_prompt, 'servers', pairs[3])]
    pallas_call x1, Pallas kernels: 1.68 us -> 1.33 us  [own_call(): pl.pallas_call(own_body, in_specs=[VMEM] * 6, out_specs=[VMEM] * 4, out_s...]
  transfers between devices with their start and end apart: 8 -> 8, of which waited for: 2 -> 2; matrix products, arithmetic and copies ran while one was open for 0% -> 0% of each run, Pallas kernels for 33% -> 31%
where the time goes in v6:
time: 30 us; the launch traced here: 29.9 us
  starting transfers between devices  15.8 us (53%)
  Pallas kernels  11 us (37%)
  waiting for transfers between devices  2.15 us (7%)
  between operations  0.82 us (3%)
    ppermute x1, starting transfers between devices, local(): part_two = lax.ppermute(own_part, 'servers', pairs[3])  5.11 us
    pallas_call x1, Pallas kernels, out_grad_call(): pl.pallas_call(out_grad_body, in_specs=[VMEM] * 4 + [SMEM] * 3, out_specs...  3.38 us
    ppermute x1, starting transfers between devices, local(): part_far = lax.ppermute(part_two[:2 * ROOT_ROWS], 'servers', pairs[1])  3.06 us
    ppermute x1, starting transfers between devices, local(): back_two = lax.ppermute(send_two, 'servers', pairs[3])  2.57 us
    ppermute x1, starting transfers between devices, local(): back_far = lax.ppermute(send_far, 'servers', pairs[2])  2.56 us
    ppermute x1, waiting for transfers between devices, local(): back_two_prompt = lax.ppermute(send_two_prompt, 'servers', pairs[3])  1.99 us
    pallas_call x1, Pallas kernels, query_call(): pl.pallas_call(body, in_specs=[VMEM] * len(operands), out_specs=[ANY, *[V...  1.65 us
    pallas_call x1, Pallas kernels, prompt_call(): pl.pallas_call(body, in_specs=[VMEM] * len(operands), out_specs=[VMEM] *...  1.43 us
  transfers between devices with their start and end apart: 8, of which 2 were waited for; matrix products, arithmetic and copies ran while one was open for 0% of the time, Pallas kernels for 31%

profile of v6, /device:TPU:0, one launch (start us, length us, event | category | flops | bytes accessed | tf_op | source)
XLA Modules:
  0.0 29.9 jit_solution(5403975807961224056)
XLA Ops:
  0.6 0.9 %pack.1.part_ref.refs_4_.refs_5_ = bf16[576,128]{1,0:T(8,128)(2,1)S(1)} custom-call(bf16[512,128]{1,0:T(8,128)(2,1)} %refs_0_.3, bf16[512,128]{1,0:T(8,128)(2,1)} %value_ref.3, bf16[32,128]{1,0:T(8,128)(2,1)} %prefix_key_ref.1, bf16[32,128]{1,0:T(8,128)(2,1)} %prefix_value_ref.1), custom_call_target="tpu_custom_call" | custom-call | flops 8589934592 | bytes 65536 | tf_op jit(solution)/shard_map/pack/pallas_call | solution.py:94
  1.6 0.0 copy-start.3
  1.6 0.0 copy-start.4
  1.6 0.0 copy-start.5
  1.6 0.0 copy-start.6
  1.6 0.0 copy-start.7
  1.6 0.0 copy-start.8
  1.6 0.0 copy-start.9
  1.6 5.1 %collective-permute-start = (bf16[576,128]{1,0:T(8,128)(2,1)S(1)}, bf16[576,128]{1,0:T(8,128)(2,1)S(1)}, u32[]{:S(2)}, u32[]{:S(2)}) collective-permute-start(bf16[576,128]{1,0:T(8,128)(2,1)S(1)} %pack.1.part_ref.refs_4_.refs_5_), channel_id=1, source_target_pairs={{0,12},{4,8},{8,4},{12,0},{1,13},{5,9},{9,5},{13,1},{2,14},{6,10},... | collective-permute-start | bytes 442376 | tf_op jit(solution)/shard_map/ppermute | solution.py:713
  6.8 0.1 collective-permute-start.3
  6.8 0.6 %collective-permute-start.2 = (bf16[576,128]{1,0:T(8,128)(2,1)S(1)}, bf16[576,128]{1,0:T(8,128)(2,1)S(1)}, u32[]{:S(2)}, u32[]{:S(2)}) collective-permute-start(bf16[576,128]{1,0:T(8,128)(2,1)S(1)} %get-tuple-element.47), channel_id=1, source_target_pairs={{0,4},{4,0},{8,12},{12,8},{1,5},{5,1},{9,13},{13,9},{2,6},{6,2},{1... | collective-permute-start | bytes 442376 | tf_op jit(solution)/shard_map/ppermute | solution.py:715
  7.4 0.0 copy-done.3
  7.4 0.0 copy-done.4
  7.4 0.0 copy-done.5
  7.4 0.0 copy-done.6
  7.4 0.0 copy-done.7
  7.4 0.0 copy-done.8
  7.5 0.0 copy-done.9
  7.5 0.0 copy-start
  7.5 3.4 %out_grad.1 = (bf16[512,1024]{1,0:T(8,128)(2,1)S(1)}, f32[16,256]{1,0:T(8,128)S(1)}, f32[16,256]{1,0:T(8,128)S(1)}, s32[33]{0:T(128)S(4)}) custom-call(bf16[512,2048]{1,0:T(8,128)(2,1)S(1)} %copy-done.4, bf16[2048,1024]{1,0:T(8,128)(2,1)S(1)} %copy-done.3, bf16[512,1024]{1,0:T(8,128)(2,1)S(1)} %copy-done.5, f32[8,512]{1,0:T(8,128)S(1)} %copy-done.6, ...), custom_call_target="tpu_custom_call" | custom-call | flops 6442450944 | bytes 65536 | tf_op jit(solution)/shard_map/out_grad/pallas_call | solution.py:172
  10.9 0.2 collective-permute-done.shard_ref.refs_7_
  11.0 3.1 %collective-permute-start.1 = (bf16[512,128]{1,0:T(8,128)(2,1)S(1)}, bf16[512,128]{1,0:T(8,128)(2,1)S(1)}, u32[]{:S(2)}, u32[]{:S(2)}) collective-permute-start(bf16[512,128]{1,0:T(8,128)(2,1)S(1)} %slice.3), channel_id=1, source_target_pairs={{0,4},{4,0},{8,12},{12,8},{1,5},{5,1},{9,13},{13,9},{2,6},{6,2},{1... | collective-permute-start | bytes 393224 | tf_op jit(solution)/shard_map/ppermute | solution.py:719
  14.1 0.0 copy-done
  14.1 0.6 %attend_near.1 = (bf16[17,64,128]{2,1,0:T(8,128)(2,1)S(1)}, bf16[17,64,128]{2,1,0:T(8,128)(2,1)S(1)}, bf16[512,128]{1,0:T(8,128)(2,1)S(1)}) custom-call(s32[33]{0:T(128)S(4)} %get-tuple-element.43.fork_ref.refs_0_, bf16[512,1024]{1,0:T(8,128)(2,1)S(1)} %copy-done, bf16[512,1024]{1,0:T(8,128)(2,1)S(1)} %get-tuple-element.39.out_ref.refs_1_.refs_2_, ...), custom_call_target="tpu_custom_call" | custom-call | flops 3221225472 | bytes 65536 | tf_op jit(solution)/shard_map/attend_near/pallas_call | solution.py:515
  14.7 0.0 copy-start.1
  14.7 0.0 copy-start.2
  14.7 2.6 %collective-permute-start.4 = (bf16[512,128]{1,0:T(8,128)(2,1)S(1)}, bf16[512,128]{1,0:T(8,128)(2,1)S(1)}, u32[]{:S(2)}, u32[]{:S(2)}) collective-permute-start(bf16[512,128]{1,0:T(8,128)(2,1)S(1)} %get-tuple-element.61), channel_id=1, source_target_pairs={{0,12},{4,8},{8,4},{12,0},{1,13},{5,9},{9,5},{13,1},{2,14},{6,10},... | collective-permute-start | bytes 393224 | tf_op jit(solution)/shard_map/ppermute | solution.py:722
  17.3 0.0 collective-permute-done.3.refs_6_
  17.3 0.0 collective-permute-done.2.refs_5_.refs_7_
  17.3 1.4 %attend_prompt.1 = (bf16[16,128,256]{2,1,0:T(8,128)(2,1)S(1)}, bf16[128,128]{1,0:T(8,128)(2,1)S(1)}, f32[256,128]{1,0:T(8,128)S(1)}, bf16[64,128]{1,0:T(8,128)(2,1)S(1)}) custom-call(bf16[512,1024]{1,0:T(8,128)(2,1)S(1)} %copy-done, bf16[512,1024]{1,0:T(8,128)(2,1)S(1)} %get-tuple-element.39.out_ref.refs_1_.refs_2_, ...), custom_call_target="tpu_custom_call" | custom-call | flops 107374184 | bytes 65536 | tf_op jit(solution)/shard_map/attend_prompt/pallas_call | solution.py:307
  18.7 0.0 collective-permute-done.1.refs_6_
  18.7 0.9 %attend_far.1 = (bf16[16,64,128]{2,1,0:T(8,128)(2,1)S(1)}, bf16[16,64,128]{2,1,0:T(8,128)(2,1)S(1)}, f32[512,128]{1,0:T(8,128)S(1)}, bf16[576,128]{1,0:T(8,128)(2,1)S(1)}, bf16[576,128]{1,0:T(8,128)(2,1)S(1)}) custom-call(s32[33]{0:T(128)S(4)} %get-tuple-element.43.fork_ref.refs_0_, bf16[512,1024]{1,0:T(8,128)(2,1)S(1)} %copy-done, ...), custom_call_target="tpu_custom_call" | custom-call | flops 107374184 | bytes 65536 | tf_op jit(solution)/shard_map/attend_far/pallas_call | solution.py:427
  19.6 2.6 %collective-permute-start.5 = (bf16[576,128]{1,0:T(8,128)(2,1)S(1)}, bf16[576,128]{1,0:T(8,128)(2,1)S(1)}, u32[]{:S(2)}, u32[]{:S(2)}) collective-permute-start(bf16[576,128]{1,0:T(8,128)(2,1)S(1)} %get-tuple-element.66), channel_id=1, source_target_pairs={{0,8},{4,12},{8,0},{12,4},{1,9},{5,13},{9,1},{13,5},{2,10},{6,14},... | collective-permute-start | bytes 442376 | tf_op jit(solution)/shard_map/ppermute | solution.py:736
  22.2 1.3 %collective-permute-start.6 = (bf16[576,128]{1,0:T(8,128)(2,1)S(1)}, bf16[576,128]{1,0:T(8,128)(2,1)S(1)}, u32[]{:S(2)}, u32[]{:S(2)}) collective-permute-start(bf16[576,128]{1,0:T(8,128)(2,1)S(1)} %get-tuple-element.67), channel_id=1, source_target_pairs={{0,4},{4,0},{8,12},{12,8},{1,5},{5,1},{9,13},{13,9},{2,6},{6,2},{1... | collective-permute-start | bytes 442376 | tf_op jit(solution)/shard_map/ppermute | solution.py:737
  23.5 0.6 %collective-permute-start.7 = (bf16[64,128]{1,0:T(8,128)(2,1)S(1)}, bf16[64,128]{1,0:T(8,128)(2,1)S(1)}, u32[]{:S(2)}, u32[]{:S(2)}) collective-permute-start(bf16[64,128]{1,0:T(8,128)(2,1)S(1)} %get-tuple-element.68), channel_id=1, source_target_pairs={{0,12},{4,8},{8,4},{12,0},{1,13},{5,9},{9,5},{13,1},{2,14},{6,10},... | collective-permute-start | bytes 49160 | tf_op jit(solution)/shard_map/ppermute | solution.py:738
  24.1 0.0 copy-done.1
  24.1 0.0 copy-done.2
  24.1 1.3 %attend_own.1 = (bf16[8,64,256]{2,1,0:T(8,128)(2,1)S(1)}, bf16[8,32,256]{2,1,0:T(8,128)(2,1)S(1)}, f32[512,128]{1,0:T(8,128)S(1)}, f32[512,128]{1,0:T(8,128)S(1)}) custom-call(bf16[512,1024]{1,0:T(8,128)(2,1)S(1)} %copy-done, bf16[512,1024]{1,0:T(8,128)(2,1)S(1)} %get-tuple-element.39.out_ref.refs_1_.refs_2_, ...), custom_call_target="tpu_custom_call" | custom-call | flops 107374184 | bytes 65536 | tf_op jit(solution)/shard_map/attend_own/pallas_call | solution.py:582
  25.4 0.0 collective-permute-done.4.refs_10_
  25.5 1.7 %query_grads.1 = (bf16[512,1024]{1,0:T(8,128)(2,1)}, f32[512,128]{1,0:T(8,128)S(1)}) custom-call(bf16[512,128]{1,0:T(8,128)(2,1)S(1)} %copy-done.1, bf16[8,64,256]{2,1,0:T(8,128)(2,1)S(1)} %get-tuple-element.52.refs_1_, bf16[8,32,256]{2,1,0:T(8,128)(2,1)S(1)} %get-tuple-element.53.refs_2_, bf16[128,128]{1,0:T(8,128)(2,1)S(1)} %get-tuple-element.54.refs_3_, ...), custom_call_target="tpu_custom_call" | custom-call | flops 322122560 | bytes 65536 | tf_op jit(solution)/shard_map/query_grads/pallas_call | solution.py:647
  27.1 2.0 %collective-permute-done.7.refs_4_ = bf16[64,128]{1,0:T(8,128)(2,1)S(1)} collective-permute-done((bf16[64,128]{1,0:T(8,128)(2,1)S(1)}, bf16[64,128]{1,0:T(8,128)(2,1)S(1)}, u32[]{:S(2)}, u32[]{:S(2)}) %collective-permute-start.7) | collective-permute-done | bytes 16416 | tf_op jit(solution)/shard_map/ppermute | solution.py:738
  29.1 0.0 collective-permute-done.5.refs_2_
  29.1 0.0 collective-permute-done.6.refs_3_
  29.1 0.8 %finish.1 = (bf16[512,128]{1,0:T(8,128)(2,1)}, bf16[512,128]{1,0:T(8,128)(2,1)}, bf16[32,128]{1,0:T(8,128)(2,1)}, bf16[32,128]{1,0:T(8,128)(2,1)}) custom-call(f32[512,128]{1,0:T(8,128)S(1)} %get-tuple-element.63.key_ref, f32[512,128]{1,0:T(8,128)S(1)} %get-tuple-element.64.value_ref, f32[512,128]{1,0:T(8,128)S(1)} %get-tuple-element.65.refs_0_, ...), custom_call_target="tpu_custom_call" | custom-call | flops 10737418 | bytes 65536 | tf_op jit(solution)/shard_map/finish/pallas_call | solution.py:683
  (2 shorter events, 0.0 us)
Async XLA Ops:
  1.6 5.9 %copy-start.3 = (bf16[2048,1024]{1,0:T(8,128)(2,1)S(1)}, bf16[2048,1024]{1,0:T(8,128)(2,1)}, u32[]{:S(2)}) copy-start(bf16[2048,1024]{1,0:T(8,128)(2,1)} %weight_ref.1) | copy-start | bytes 12582916
  1.6 5.9 %copy-start.4 = (bf16[512,2048]{1,0:T(8,128)(2,1)S(1)}, bf16[512,2048]{1,0:T(8,128)(2,1)}, u32[]{:S(2)}) copy-start(bf16[512,2048]{1,0:T(8,128)(2,1)} %grad_ref.1) | copy-start | bytes 6291460
  1.6 5.8 %copy-start.5 = (bf16[512,1024]{1,0:T(8,128)(2,1)S(1)}, bf16[512,1024]{1,0:T(8,128)(2,1)}, u32[]{:S(2)}) copy-start(bf16[512,1024]{1,0:T(8,128)(2,1)} %attn_ref.1) | copy-start | bytes 3145732
  1.6 5.8 %copy-start.6 = (f32[8,512]{1,0:T(8,128)S(1)}, f32[8,512]{1,0:T(8,128)}, u32[]{:S(2)}) copy-start(f32[8,512]{1,0:T(8,128)} %lse_ref.1) | copy-start | bytes 49156
  1.6 5.8 %copy-start.7 = (s32[64,1]{0,1:T(1,128)S(1)}, s32[64,1]{0,1:T(1,128)}, u32[]{:S(2)}) copy-start(s32[64,1]{0,1:T(1,128)} %param.21) | copy-start | bytes 772
  1.6 5.8 %copy-start.8 = (s32[64]{0:T(128)S(1)}, s32[64]{0:T(128)}, u32[]{:S(2)}) copy-start(s32[64]{0:T(128)} %root_ref.1) | copy-start | bytes 772
  1.6 5.8 %copy-start.9 = (s32[64]{0:T(128)S(1)}, s32[64]{0:T(128)}, u32[]{:S(2)}) copy-start(s32[64]{0:T(128)} %offset_ref.1) | copy-start | bytes 772
  1.6 9.4 %collective-permute-start = (bf16[576,128]{1,0:T(8,128)(2,1)S(1)}, bf16[576,128]{1,0:T(8,128)(2,1)S(1)}, u32[]{:S(2)}, u32[]{:S(2)}) collective-permute-start(bf16[576,128]{1,0:T(8,128)(2,1)S(1)} %pack.1.part_ref.refs_4_.refs_5_), channel_id=1, source_target_pairs={{0,12},{4,8},{8,4},{12,0},{1,13},{5,9},{9,5},{13,1},{2,14},{6,10},... | collective-permute-start | bytes 442376 | tf_op jit(solution)/shard_map/ppermute | solution.py:713
  6.8 10.5 %collective-permute-start.3 = (bf16[64,128]{1,0:T(8,128)(2,1)S(1)}, bf16[64,128]{1,0:T(8,128)(2,1)S(1)}, u32[]{:S(2)}, u32[]{:S(2)}) collective-permute-start(bf16[64,128]{1,0:T(8,128)(2,1)S(1)} %get-tuple-element.48), channel_id=1, source_target_pairs={{0,8},{4,12},{8,0},{12,4},{1,9},{5,13},{9,1},{13,5},{2,10},{6,14},... | collective-permute-start | bytes 49160 | tf_op jit(solution)/shard_map/ppermute | solution.py:716
  6.8 10.4 %collective-permute-start.2 = (bf16[576,128]{1,0:T(8,128)(2,1)S(1)}, bf16[576,128]{1,0:T(8,128)(2,1)S(1)}, u32[]{:S(2)}, u32[]{:S(2)}) collective-permute-start(bf16[576,128]{1,0:T(8,128)(2,1)S(1)} %get-tuple-element.47), channel_id=1, source_target_pairs={{0,4},{4,0},{8,12},{12,8},{1,5},{5,1},{9,13},{13,9},{2,6},{6,2},{1... | collective-permute-start | bytes 442376 | tf_op jit(solution)/shard_map/ppermute | solution.py:715
  7.5 6.6 %copy-start = (bf16[512,1024]{1,0:T(8,128)(2,1)S(1)}, bf16[512,1024]{1,0:T(8,128)(2,1)}, u32[]{:S(2)}) copy-start(bf16[512,1024]{1,0:T(8,128)(2,1)} %q_ref.3) | copy-start | bytes 3145732
  11.0 7.7 %collective-permute-start.1 = (bf16[512,128]{1,0:T(8,128)(2,1)S(1)}, bf16[512,128]{1,0:T(8,128)(2,1)S(1)}, u32[]{:S(2)}, u32[]{:S(2)}) collective-permute-start(bf16[512,128]{1,0:T(8,128)(2,1)S(1)} %slice.3), channel_id=1, source_target_pairs={{0,4},{4,0},{8,12},{12,8},{1,5},{5,1},{9,13},{13,9},{2,6},{6,2},{1... | collective-permute-start | bytes 393224 | tf_op jit(solution)/shard_map/ppermute | solution.py:719
  14.7 9.4 %copy-start.1 = (bf16[512,128]{1,0:T(8,128)(2,1)S(1)}, bf16[512,128]{1,0:T(8,128)(2,1)}, u32[]{:S(2)}) copy-start(bf16[512,128]{1,0:T(8,128)(2,1)} %refs_0_.3) | copy-start | bytes 393220
  14.7 9.4 %copy-start.2 = (bf16[512,128]{1,0:T(8,128)(2,1)S(1)}, bf16[512,128]{1,0:T(8,128)(2,1)}, u32[]{:S(2)}) copy-start(bf16[512,128]{1,0:T(8,128)(2,1)} %value_ref.3) | copy-start | bytes 393220
  14.7 10.7 %collective-permute-start.4 = (bf16[512,128]{1,0:T(8,128)(2,1)S(1)}, bf16[512,128]{1,0:T(8,128)(2,1)S(1)}, u32[]{:S(2)}, u32[]{:S(2)}) collective-permute-start(bf16[512,128]{1,0:T(8,128)(2,1)S(1)} %get-tuple-element.61), channel_id=1, source_target_pairs={{0,12},{4,8},{8,4},{12,0},{1,13},{5,9},{9,5},{13,1},{2,14},{6,10},... | collective-permute-start | bytes 393224 | tf_op jit(solution)/shard_map/ppermute | solution.py:722
  19.6 9.5 %collective-permute-start.5 = (bf16[576,128]{1,0:T(8,128)(2,1)S(1)}, bf16[576,128]{1,0:T(8,128)(2,1)S(1)}, u32[]{:S(2)}, u32[]{:S(2)}) collective-permute-start(bf16[576,128]{1,0:T(8,128)(2,1)S(1)} %get-tuple-element.66), channel_id=1, source_target_pairs={{0,8},{4,12},{8,0},{12,4},{1,9},{5,13},{9,1},{13,5},{2,10},{6,14},... | collective-permute-start | bytes 442376 | tf_op jit(solution)/shard_map/ppermute | solution.py:736
  22.2 6.9 %collective-permute-start.6 = (bf16[576,128]{1,0:T(8,128)(2,1)S(1)}, bf16[576,128]{1,0:T(8,128)(2,1)S(1)}, u32[]{:S(2)}, u32[]{:S(2)}) collective-permute-start(bf16[576,128]{1,0:T(8,128)(2,1)S(1)} %get-tuple-element.67), channel_id=1, source_target_pairs={{0,4},{4,0},{8,12},{12,8},{1,5},{5,1},{9,13},{13,9},{2,6},{6,2},{1... | collective-permute-start | bytes 442376 | tf_op jit(solution)/shard_map/ppermute | solution.py:737
  23.5 5.6 %collective-permute-start.7 = (bf16[64,128]{1,0:T(8,128)(2,1)S(1)}, bf16[64,128]{1,0:T(8,128)(2,1)S(1)}, u32[]{:S(2)}, u32[]{:S(2)}) collective-permute-start(bf16[64,128]{1,0:T(8,128)(2,1)S(1)} %get-tuple-element.68), channel_id=1, source_target_pairs={{0,12},{4,8},{8,4},{12,0},{1,13},{5,9},{9,5},{13,1},{2,14},{6,10},... | collective-permute-start | bytes 49160 | tf_op jit(solution)/shard_map/ppermute | solution.py:738

commit v7 on v5

--- a/solution.py
+++ b/solution.py
@@ -275,6 +275,7 @@
         lambda unit: (key_ref[...], value_ref[...]),
         lambda unit, weights: weights,
         keep,
+        2,
     )
 
     def store(ref, at, index):

time: 30 us -> 30 us (level)
  waiting for transfers between devices: 1.5 us -> 1.8 us
  transfers between devices with their start and end apart: 8 -> 8, of which waited for: 2 -> 2; matrix products, arithmetic and copies ran while one was open for 0% -> 0% of each run, Pallas kernels for 33% -> 32%
where the time goes in v7:
time: 30 us; the launch traced here: 29.9 us
  starting transfers between devices  15.8 us (53%)
  Pallas kernels  11.3 us (38%)
  waiting for transfers between devices  1.8 us (6%)
  between operations  0.83 us (3%)
    ppermute x1, starting transfers between devices, local(): part_two = lax.ppermute(own_part, 'servers', pairs[3])  5.11 us
    pallas_call x1, Pallas kernels, out_grad_call(): pl.pallas_call(out_grad_body, in_specs=[VMEM] * 4 + [SMEM] * 3, out_specs...  3.38 us
    ppermute x1, starting transfers between devices, local(): part_far = lax.ppermute(part_two[:2 * ROOT_ROWS], 'servers', pairs[1])  3.06 us
    ppermute x1, starting transfers between devices, local(): back_two = lax.ppermute(send_two, 'servers', pairs[3])  2.57 us
    ppermute x1, starting transfers between devices, local(): back_far = lax.ppermute(send_far, 'servers', pairs[2])  2.56 us
    pallas_call x1, Pallas kernels, own_call(): pl.pallas_call(own_body, in_specs=[VMEM] * 6, out_specs=[VMEM] * 4, out_s...  1.68 us
    pallas_call x1, Pallas kernels, query_call(): pl.pallas_call(body, in_specs=[VMEM] * len(operands), out_specs=[ANY, *[V...  1.65 us
    ppermute x1, waiting for transfers between devices, local(): back_two_prompt = lax.ppermute(send_two_prompt, 'servers', pairs[3])  1.63 us
  transfers between devices with their start and end apart: 8, of which 2 were waited for; matrix products, arithmetic and copies ran while one was open for 0% of the time, Pallas kernels for 32%

profile of v7, /device:TPU:0, one launch (start us, length us, event | category | flops | bytes accessed | tf_op | source)
XLA Modules:
  0.0 29.9 jit_solution(17164532607478598099)
XLA Ops:
  0.6 0.9 %pack.1.part_ref.refs_4_.refs_5_ = bf16[576,128]{1,0:T(8,128)(2,1)S(1)} custom-call(bf16[512,128]{1,0:T(8,128)(2,1)} %refs_0_.3, bf16[512,128]{1,0:T(8,128)(2,1)} %value_ref.3, bf16[32,128]{1,0:T(8,128)(2,1)} %prefix_key_ref.1, bf16[32,128]{1,0:T(8,128)(2,1)} %prefix_value_ref.1), custom_call_target="tpu_custom_call" | custom-call | flops 8589934592 | bytes 65536 | tf_op jit(solution)/shard_map/pack/pallas_call | solution.py:94
  1.6 0.0 copy-start.3
  1.6 0.0 copy-start.4
  1.6 0.0 copy-start.5
  1.6 0.0 copy-start.6
  1.6 0.0 copy-start.7
  1.6 0.0 copy-start.8
  1.6 0.0 copy-start.9
  1.6 5.1 %collective-permute-start = (bf16[576,128]{1,0:T(8,128)(2,1)S(1)}, bf16[576,128]{1,0:T(8,128)(2,1)S(1)}, u32[]{:S(2)}, u32[]{:S(2)}) collective-permute-start(bf16[576,128]{1,0:T(8,128)(2,1)S(1)} %pack.1.part_ref.refs_4_.refs_5_), channel_id=1, source_target_pairs={{0,12},{4,8},{8,4},{12,0},{1,13},{5,9},{9,5},{13,1},{2,14},{6,10},... | collective-permute-start | bytes 442376 | tf_op jit(solution)/shard_map/ppermute | solution.py:712
  6.8 0.1 collective-permute-start.3
  6.8 0.6 %collective-permute-start.2 = (bf16[576,128]{1,0:T(8,128)(2,1)S(1)}, bf16[576,128]{1,0:T(8,128)(2,1)S(1)}, u32[]{:S(2)}, u32[]{:S(2)}) collective-permute-start(bf16[576,128]{1,0:T(8,128)(2,1)S(1)} %get-tuple-element.47), channel_id=1, source_target_pairs={{0,4},{4,0},{8,12},{12,8},{1,5},{5,1},{9,13},{13,9},{2,6},{6,2},{1... | collective-permute-start | bytes 442376 | tf_op jit(solution)/shard_map/ppermute | solution.py:715
  7.4 0.0 copy-done.3
  7.4 0.0 copy-done.4
  7.4 0.0 copy-done.5
  7.4 0.0 copy-done.6
  7.4 0.0 copy-done.7
  7.4 0.0 copy-done.8
  7.5 0.0 copy-done.9
  7.5 0.0 copy-start
  7.5 3.4 %out_grad.1 = (bf16[512,1024]{1,0:T(8,128)(2,1)S(1)}, f32[16,256]{1,0:T(8,128)S(1)}, f32[16,256]{1,0:T(8,128)S(1)}, s32[33]{0:T(128)S(4)}) custom-call(bf16[512,2048]{1,0:T(8,128)(2,1)S(1)} %copy-done.4, bf16[2048,1024]{1,0:T(8,128)(2,1)S(1)} %copy-done.3, bf16[512,1024]{1,0:T(8,128)(2,1)S(1)} %copy-done.5, f32[8,512]{1,0:T(8,128)S(1)} %copy-done.6, ...), custom_call_target="tpu_custom_call" | custom-call | flops 6442450944 | bytes 65536 | tf_op jit(solution)/shard_map/out_grad/pallas_call | solution.py:172
  10.9 0.2 collective-permute-done.shard_ref.refs_7_
  11.0 3.1 %collective-permute-start.1 = (bf16[512,128]{1,0:T(8,128)(2,1)S(1)}, bf16[512,128]{1,0:T(8,128)(2,1)S(1)}, u32[]{:S(2)}, u32[]{:S(2)}) collective-permute-start(bf16[512,128]{1,0:T(8,128)(2,1)S(1)} %slice.3), channel_id=1, source_target_pairs={{0,4},{4,0},{8,12},{12,8},{1,5},{5,1},{9,13},{13,9},{2,6},{6,2},{1... | collective-permute-start | bytes 393224 | tf_op jit(solution)/shard_map/ppermute | solution.py:718
  14.1 0.0 copy-done
  14.1 0.6 %attend_near.1 = (bf16[17,64,128]{2,1,0:T(8,128)(2,1)S(1)}, bf16[17,64,128]{2,1,0:T(8,128)(2,1)S(1)}, bf16[512,128]{1,0:T(8,128)(2,1)S(1)}) custom-call(s32[33]{0:T(128)S(4)} %get-tuple-element.43.fork_ref.refs_0_, bf16[512,1024]{1,0:T(8,128)(2,1)S(1)} %copy-done, bf16[512,1024]{1,0:T(8,128)(2,1)S(1)} %get-tuple-element.39.out_ref.refs_1_.refs_2_, ...), custom_call_target="tpu_custom_call" | custom-call | flops 3221225472 | bytes 65536 | tf_op jit(solution)/shard_map/attend_near/pallas_call | solution.py:515
  14.7 0.0 copy-start.1
  14.7 0.0 copy-start.2
  14.7 2.6 %collective-permute-start.4 = (bf16[512,128]{1,0:T(8,128)(2,1)S(1)}, bf16[512,128]{1,0:T(8,128)(2,1)S(1)}, u32[]{:S(2)}, u32[]{:S(2)}) collective-permute-start(bf16[512,128]{1,0:T(8,128)(2,1)S(1)} %get-tuple-element.61), channel_id=1, source_target_pairs={{0,12},{4,8},{8,4},{12,0},{1,13},{5,9},{9,5},{13,1},{2,14},{6,10},... | collective-permute-start | bytes 393224 | tf_op jit(solution)/shard_map/ppermute | solution.py:721
  17.3 0.0 collective-permute-done.3.refs_6_
  17.3 0.0 collective-permute-done.2.refs_5_.refs_7_
  17.3 1.4 %attend_prompt.1 = (bf16[16,128,256]{2,1,0:T(8,128)(2,1)S(1)}, bf16[128,128]{1,0:T(8,128)(2,1)S(1)}, f32[256,128]{1,0:T(8,128)S(1)}, bf16[64,128]{1,0:T(8,128)(2,1)S(1)}) custom-call(bf16[512,1024]{1,0:T(8,128)(2,1)S(1)} %copy-done, bf16[512,1024]{1,0:T(8,128)(2,1)S(1)} %get-tuple-element.39.out_ref.refs_1_.refs_2_, ...), custom_call_target="tpu_custom_call" | custom-call | flops 107374184 | bytes 65536 | tf_op jit(solution)/shard_map/attend_prompt/pallas_call | solution.py:307
  18.7 0.0 collective-permute-done.1.refs_6_
  18.7 0.9 %attend_far.1 = (bf16[16,64,128]{2,1,0:T(8,128)(2,1)S(1)}, bf16[16,64,128]{2,1,0:T(8,128)(2,1)S(1)}, f32[512,128]{1,0:T(8,128)S(1)}, bf16[576,128]{1,0:T(8,128)(2,1)S(1)}, bf16[576,128]{1,0:T(8,128)(2,1)S(1)}) custom-call(s32[33]{0:T(128)S(4)} %get-tuple-element.43.fork_ref.refs_0_, bf16[512,1024]{1,0:T(8,128)(2,1)S(1)} %copy-done, ...), custom_call_target="tpu_custom_call" | custom-call | flops 107374184 | bytes 65536 | tf_op jit(solution)/shard_map/attend_far/pallas_call | solution.py:427
  19.6 2.6 %collective-permute-start.5 = (bf16[576,128]{1,0:T(8,128)(2,1)S(1)}, bf16[576,128]{1,0:T(8,128)(2,1)S(1)}, u32[]{:S(2)}, u32[]{:S(2)}) collective-permute-start(bf16[576,128]{1,0:T(8,128)(2,1)S(1)} %get-tuple-element.66), channel_id=1, source_target_pairs={{0,8},{4,12},{8,0},{12,4},{1,9},{5,13},{9,1},{13,5},{2,10},{6,14},... | collective-permute-start | bytes 442376 | tf_op jit(solution)/shard_map/ppermute | solution.py:735
  22.2 1.3 %collective-permute-start.6 = (bf16[576,128]{1,0:T(8,128)(2,1)S(1)}, bf16[576,128]{1,0:T(8,128)(2,1)S(1)}, u32[]{:S(2)}, u32[]{:S(2)}) collective-permute-start(bf16[576,128]{1,0:T(8,128)(2,1)S(1)} %get-tuple-element.67), channel_id=1, source_target_pairs={{0,4},{4,0},{8,12},{12,8},{1,5},{5,1},{9,13},{13,9},{2,6},{6,2},{1... | collective-permute-start | bytes 442376 | tf_op jit(solution)/shard_map/ppermute | solution.py:736
  23.5 0.6 %collective-permute-start.7 = (bf16[64,128]{1,0:T(8,128)(2,1)S(1)}, bf16[64,128]{1,0:T(8,128)(2,1)S(1)}, u32[]{:S(2)}, u32[]{:S(2)}) collective-permute-start(bf16[64,128]{1,0:T(8,128)(2,1)S(1)} %get-tuple-element.68), channel_id=1, source_target_pairs={{0,12},{4,8},{8,4},{12,0},{1,13},{5,9},{9,5},{13,1},{2,14},{6,10},... | collective-permute-start | bytes 49160 | tf_op jit(solution)/shard_map/ppermute | solution.py:737
  24.1 0.0 copy-done.1
  24.1 0.0 copy-done.2
  24.1 1.7 %attend_own.1 = (bf16[8,64,256]{2,1,0:T(8,128)(2,1)S(1)}, bf16[8,32,256]{2,1,0:T(8,128)(2,1)S(1)}, f32[512,128]{1,0:T(8,128)S(1)}, f32[512,128]{1,0:T(8,128)S(1)}) custom-call(bf16[512,1024]{1,0:T(8,128)(2,1)S(1)} %copy-done, bf16[512,1024]{1,0:T(8,128)(2,1)S(1)} %get-tuple-element.39.out_ref.refs_1_.refs_2_, ...), custom_call_target="tpu_custom_call" | custom-call | flops 107374184 | bytes 65536 | tf_op jit(solution)/shard_map/attend_own/pallas_call | solution.py:581
  25.8 0.0 collective-permute-done.4.refs_10_
  25.8 1.7 %query_grads.1 = (bf16[512,1024]{1,0:T(8,128)(2,1)}, f32[512,128]{1,0:T(8,128)S(1)}) custom-call(bf16[512,128]{1,0:T(8,128)(2,1)S(1)} %copy-done.1, bf16[8,64,256]{2,1,0:T(8,128)(2,1)S(1)} %get-tuple-element.52.refs_1_, bf16[8,32,256]{2,1,0:T(8,128)(2,1)S(1)} %get-tuple-element.53.refs_2_, bf16[128,128]{1,0:T(8,128)(2,1)S(1)} %get-tuple-element.54.refs_3_, ...), custom_call_target="tpu_custom_call" | custom-call | flops 322122560 | bytes 65536 | tf_op jit(solution)/shard_map/query_grads/pallas_call | solution.py:646
  27.5 1.6 %collective-permute-done.7.refs_4_ = bf16[64,128]{1,0:T(8,128)(2,1)S(1)} collective-permute-done((bf16[64,128]{1,0:T(8,128)(2,1)S(1)}, bf16[64,128]{1,0:T(8,128)(2,1)S(1)}, u32[]{:S(2)}, u32[]{:S(2)}) %collective-permute-start.7) | collective-permute-done | bytes 16416 | tf_op jit(solution)/shard_map/ppermute | solution.py:737
  29.1 0.0 collective-permute-done.5.refs_2_
  29.1 0.0 collective-permute-done.6.refs_3_
  29.1 0.8 %finish.1 = (bf16[512,128]{1,0:T(8,128)(2,1)}, bf16[512,128]{1,0:T(8,128)(2,1)}, bf16[32,128]{1,0:T(8,128)(2,1)}, bf16[32,128]{1,0:T(8,128)(2,1)}) custom-call(f32[512,128]{1,0:T(8,128)S(1)} %get-tuple-element.63.key_ref, f32[512,128]{1,0:T(8,128)S(1)} %get-tuple-element.64.value_ref, f32[512,128]{1,0:T(8,128)S(1)} %get-tuple-element.65.refs_0_, ...), custom_call_target="tpu_custom_call" | custom-call | flops 10737418 | bytes 65536 | tf_op jit(solution)/shard_map/finish/pallas_call | solution.py:682
  (2 shorter events, 0.0 us)
Async XLA Ops:
  1.6 5.9 %copy-start.3 = (bf16[2048,1024]{1,0:T(8,128)(2,1)S(1)}, bf16[2048,1024]{1,0:T(8,128)(2,1)}, u32[]{:S(2)}) copy-start(bf16[2048,1024]{1,0:T(8,128)(2,1)} %weight_ref.1) | copy-start | bytes 12582916
  1.6 5.9 %copy-start.4 = (bf16[512,2048]{1,0:T(8,128)(2,1)S(1)}, bf16[512,2048]{1,0:T(8,128)(2,1)}, u32[]{:S(2)}) copy-start(bf16[512,2048]{1,0:T(8,128)(2,1)} %grad_ref.1) | copy-start | bytes 6291460
  1.6 5.8 %copy-start.5 = (bf16[512,1024]{1,0:T(8,128)(2,1)S(1)}, bf16[512,1024]{1,0:T(8,128)(2,1)}, u32[]{:S(2)}) copy-start(bf16[512,1024]{1,0:T(8,128)(2,1)} %attn_ref.1) | copy-start | bytes 3145732
  1.6 5.8 %copy-start.6 = (f32[8,512]{1,0:T(8,128)S(1)}, f32[8,512]{1,0:T(8,128)}, u32[]{:S(2)}) copy-start(f32[8,512]{1,0:T(8,128)} %lse_ref.1) | copy-start | bytes 49156
  1.6 5.8 %copy-start.7 = (s32[64,1]{0,1:T(1,128)S(1)}, s32[64,1]{0,1:T(1,128)}, u32[]{:S(2)}) copy-start(s32[64,1]{0,1:T(1,128)} %param.21) | copy-start | bytes 772
  1.6 5.8 %copy-start.8 = (s32[64]{0:T(128)S(1)}, s32[64]{0:T(128)}, u32[]{:S(2)}) copy-start(s32[64]{0:T(128)} %root_ref.1) | copy-start | bytes 772
  1.6 5.8 %copy-start.9 = (s32[64]{0:T(128)S(1)}, s32[64]{0:T(128)}, u32[]{:S(2)}) copy-start(s32[64]{0:T(128)} %offset_ref.1) | copy-start | bytes 772
  1.6 9.4 %collective-permute-start = (bf16[576,128]{1,0:T(8,128)(2,1)S(1)}, bf16[576,128]{1,0:T(8,128)(2,1)S(1)}, u32[]{:S(2)}, u32[]{:S(2)}) collective-permute-start(bf16[576,128]{1,0:T(8,128)(2,1)S(1)} %pack.1.part_ref.refs_4_.refs_5_), channel_id=1, source_target_pairs={{0,12},{4,8},{8,4},{12,0},{1,13},{5,9},{9,5},{13,1},{2,14},{6,10},... | collective-permute-start | bytes 442376 | tf_op jit(solution)/shard_map/ppermute | solution.py:712
  6.8 10.5 %collective-permute-start.3 = (bf16[64,128]{1,0:T(8,128)(2,1)S(1)}, bf16[64,128]{1,0:T(8,128)(2,1)S(1)}, u32[]{:S(2)}, u32[]{:S(2)}) collective-permute-start(bf16[64,128]{1,0:T(8,128)(2,1)S(1)} %get-tuple-element.48), channel_id=1, source_target_pairs={{0,8},{4,12},{8,0},{12,4},{1,9},{5,13},{9,1},{13,5},{2,10},{6,14},... | collective-permute-start | bytes 49160 | tf_op jit(solution)/shard_map/ppermute | solution.py:714
  6.8 10.4 %collective-permute-start.2 = (bf16[576,128]{1,0:T(8,128)(2,1)S(1)}, bf16[576,128]{1,0:T(8,128)(2,1)S(1)}, u32[]{:S(2)}, u32[]{:S(2)}) collective-permute-start(bf16[576,128]{1,0:T(8,128)(2,1)S(1)} %get-tuple-element.47), channel_id=1, source_target_pairs={{0,4},{4,0},{8,12},{12,8},{1,5},{5,1},{9,13},{13,9},{2,6},{6,2},{1... | collective-permute-start | bytes 442376 | tf_op jit(solution)/shard_map/ppermute | solution.py:715
  7.5 6.6 %copy-start = (bf16[512,1024]{1,0:T(8,128)(2,1)S(1)}, bf16[512,1024]{1,0:T(8,128)(2,1)}, u32[]{:S(2)}) copy-start(bf16[512,1024]{1,0:T(8,128)(2,1)} %q_ref.3) | copy-start | bytes 3145732
  11.0 7.7 %collective-permute-start.1 = (bf16[512,128]{1,0:T(8,128)(2,1)S(1)}, bf16[512,128]{1,0:T(8,128)(2,1)S(1)}, u32[]{:S(2)}, u32[]{:S(2)}) collective-permute-start(bf16[512,128]{1,0:T(8,128)(2,1)S(1)} %slice.3), channel_id=1, source_target_pairs={{0,4},{4,0},{8,12},{12,8},{1,5},{5,1},{9,13},{13,9},{2,6},{6,2},{1... | collective-permute-start | bytes 393224 | tf_op jit(solution)/shard_map/ppermute | solution.py:718
  14.7 9.4 %copy-start.1 = (bf16[512,128]{1,0:T(8,128)(2,1)S(1)}, bf16[512,128]{1,0:T(8,128)(2,1)}, u32[]{:S(2)}) copy-start(bf16[512,128]{1,0:T(8,128)(2,1)} %refs_0_.3) | copy-start | bytes 393220
  14.7 9.4 %copy-start.2 = (bf16[512,128]{1,0:T(8,128)(2,1)S(1)}, bf16[512,128]{1,0:T(8,128)(2,1)}, u32[]{:S(2)}) copy-start(bf16[512,128]{1,0:T(8,128)(2,1)} %value_ref.3) | copy-start | bytes 393220
  14.7 11.1 %collective-permute-start.4 = (bf16[512,128]{1,0:T(8,128)(2,1)S(1)}, bf16[512,128]{1,0:T(8,128)(2,1)S(1)}, u32[]{:S(2)}, u32[]{:S(2)}) collective-permute-start(bf16[512,128]{1,0:T(8,128)(2,1)S(1)} %get-tuple-element.61), channel_id=1, source_target_pairs={{0,12},{4,8},{8,4},{12,0},{1,13},{5,9},{9,5},{13,1},{2,14},{6,10},... | collective-permute-start | bytes 393224 | tf_op jit(solution)/shard_map/ppermute | solution.py:721
  19.6 9.5 %collective-permute-start.5 = (bf16[576,128]{1,0:T(8,128)(2,1)S(1)}, bf16[576,128]{1,0:T(8,128)(2,1)S(1)}, u32[]{:S(2)}, u32[]{:S(2)}) collective-permute-start(bf16[576,128]{1,0:T(8,128)(2,1)S(1)} %get-tuple-element.66), channel_id=1, source_target_pairs={{0,8},{4,12},{8,0},{12,4},{1,9},{5,13},{9,1},{13,5},{2,10},{6,14},... | collective-permute-start | bytes 442376 | tf_op jit(solution)/shard_map/ppermute | solution.py:735
  22.2 6.9 %collective-permute-start.6 = (bf16[576,128]{1,0:T(8,128)(2,1)S(1)}, bf16[576,128]{1,0:T(8,128)(2,1)S(1)}, u32[]{:S(2)}, u32[]{:S(2)}) collective-permute-start(bf16[576,128]{1,0:T(8,128)(2,1)S(1)} %get-tuple-element.67), channel_id=1, source_target_pairs={{0,4},{4,0},{8,12},{12,8},{1,5},{5,1},{9,13},{13,9},{2,6},{6,2},{1... | collective-permute-start | bytes 442376 | tf_op jit(solution)/shard_map/ppermute | solution.py:736
  23.5 5.6 %collective-permute-start.7 = (bf16[64,128]{1,0:T(8,128)(2,1)S(1)}, bf16[64,128]{1,0:T(8,128)(2,1)S(1)}, u32[]{:S(2)}, u32[]{:S(2)}) collective-permute-start(bf16[64,128]{1,0:T(8,128)(2,1)S(1)} %get-tuple-element.68), channel_id=1, source_target_pairs={{0,12},{4,8},{8,4},{12,0},{1,13},{5,9},{9,5},{13,1},{2,14},{6,10},... | collective-permute-start | bytes 49160 | tf_op jit(solution)/shard_map/ppermute | solution.py:737
